TPU v7x, 128 devices: a whole 4x4x4 slice. The times are simulated.
128 devices in a mesh: expert: 4 (over y), blk: 32 (over z, x, core).
Axes of the slice: x: 4, y: 4, z: 4, core: 2. Of those that a mesh axis runs over, the one named last changes fastest.
Arguments:
- tokens: bfloat16 [2, 512, 6144], P(None, 'expert', 'blk'), may hold values from -6 to 6
- expert_ids: int32 [2, 512, 2], P(None, 'expert'), may hold values from 0 to 3, all different within a row; in each aligned block of 128 rows (0 to 127, 128 to 255, ..., all dimensions but the last counted through in order) at most 128 rows name the same one
- route_share: float32 [2, 512], P(None, 'expert'), may hold values from 0.1 to 0.9
- gate_weight: bfloat16 [4, 6144, 16384], P('expert', None, 'blk'), may hold values from -0.078125 to 0.078125
- up_weight: bfloat16 [4, 6144, 16384], P('expert', None, 'blk'), may hold values from -0.078125 to 0.078125
- down_weight: bfloat16 [4, 16384, 6144], P('expert', 'blk'), may hold values from -0.09375 to 0.09375
Outputs:
- combined: bfloat16 [2, 512, 6144], P(None, 'expert', 'blk')
Inputs may be any that keep to these rules, and one draw needn't show every extreme that they name: `expert_ids`: each row names two different experts.
All inputs are finite; a program needn't handle non-finite values.
Results may differ from a plain program's by a relative error of at most 0.023.
Values may be sent and summed in bfloat16 or wider, within the bound.
No kernel may reach another device: no remote copies, remote signals or barrier semaphores. Data moves between devices by JAX's collectives and lax.ppermute only.
A program may use at most 128 MiB of HBM per device.

v0:
```python
import jax
import jax.numpy as jnp
from jax import lax
from jax.sharding import PartitionSpec as P


def routing(expert_ids, route_share, experts):
    row_count = expert_ids.shape[1]
    labels = jnp.arange(experts, dtype=jnp.int32)
    first_hit = (expert_ids[:, :, 0:1] == labels).astype(jnp.float32)
    second = (expert_ids[:, :, 1:2] == labels).astype(jnp.float32)
    chosen = first_hit + second
    weight = route_share[:, :, None] * first_hit + (1.0 - route_share[:, :, None]) * second
    slot_pos = jnp.cumsum(chosen.astype(jnp.int32), axis=1) - 1
    slot_ids = jnp.arange(row_count, dtype=jnp.int32)
    placed = ((slot_pos[:, :, :, None] == slot_ids) & (chosen[:, :, :, None] > 0)).astype(
        jnp.bfloat16
    )
    return (placed, weight)


def expert_layer(tokens, expert_ids, route_share, gate_mat, up_mat, down_mat, experts):
    step_count, row_count, feature_cols = tokens.shape
    placed, weight = routing(expert_ids, route_share, experts)
    outgoing = jnp.einsum(
        "gres,grd->gesd", placed, tokens, preferred_element_type=jnp.float32
    ).astype(jnp.bfloat16)
    arrived = lax.all_to_all(outgoing, "expert", split_axis=1, concat_axis=1, tiled=True)
    slot_rows = arrived.reshape(-1, feature_cols)
    fragment = lax.all_gather(slot_rows, "blk", axis=1, tiled=True)
    gate_pre = jnp.dot(fragment, gate_mat, preferred_element_type=jnp.float32)
    up_pre = jnp.dot(fragment, up_mat, preferred_element_type=jnp.float32)
    hidden = (jax.nn.silu(gate_pre) * up_pre).astype(jnp.bfloat16)
    summed = lax.psum_scatter(
        lax.dot_general(
            down_mat, hidden, (((0,), (1,)), ((), ())), preferred_element_type=jnp.float32
        ).astype(jnp.bfloat16),
        "blk",
        scatter_dimension=0,
        tiled=True,
    )
    returned = lax.all_to_all(
        summed.reshape(feature_cols, step_count, experts, row_count),
        "expert",
        split_axis=2,
        concat_axis=2,
        tiled=True,
    )
    picked = jnp.einsum("gres,dges->gerd", placed, returned, preferred_element_type=jnp.float32)
    combined = jnp.sum(jnp.transpose(weight, (0, 2, 1))[:, :, :, None] * picked, axis=1)
    return combined.astype(jnp.bfloat16)


def body(tokens, expert_ids, route_share, gate_weight, up_weight, down_weight):
    experts = lax.axis_size("expert")
    gate_mat = gate_weight[0]
    up_mat = up_weight[0]
    down_mat = down_weight[0]
    results = []
    for step_idx in range(tokens.shape[0]):
        results.append(
            expert_layer(
                tokens[step_idx : step_idx + 1],
                expert_ids[step_idx : step_idx + 1],
                route_share[step_idx : step_idx + 1],
                gate_mat,
                up_mat,
                down_mat,
                experts,
            )
        )
    return jnp.concatenate(results, axis=0)


def solution(mesh):
    return jax.shard_map(
        body,
        mesh=mesh,
        in_specs=(
            P(None, "expert", "blk"),
            P(None, "expert", None),
            P(None, "expert"),
            P("expert", None, "blk"),
            P("expert", None, "blk"),
            P("expert", "blk", None),
        ),
        out_specs=P(None, "expert", "blk"),
        check_vma=False,
    )
```

profile of v0, /device:TPU:1, one launch (start us, length us, event | category | flops | bytes accessed | tf_op | source)
XLA Modules:
  0.0 317.3 jit_solution(13525887074447122003)
XLA Ops:
  6.5 0.0 all-gather.3.cloned.1.call-start
  6.5 0.8 slice_bitcast_fusion.5
  7.3 0.1 fusion.45
  7.4 0.1 fusion.44
  7.6 0.2 reduce_window_sum.17
  7.8 0.1 copy.21
  7.8 0.1 copy.22
  7.9 1.2 fusion.26
  9.1 10.0 %all_to_all.20 = bf16[1,4,128,192]{2,3,0,1:T(8,128)(2,1)S(1)} all-to-all(bf16[1,4,128,192]{2,3,0,1:T(8,128)(2,1)S(1)} %fusion.26), channel_id=1, replica_groups=mesh['expert'=4,'blk'=32] {'expert'}, dimensions={1} | all-to-all | bytes 393216 | tf_op jit(solution)/shard_map/all_to_all | solution.py:28
  19.1 0.2 copy.24
  19.3 0.7 copy.40
  20.0 0.0 all-gather.3.cloned.1.call-update
  20.0 0.0 all-gather.5.cloned.1.call-start
  20.1 0.2 reduce_window_sum.18
  20.2 0.1 copy.26
  20.3 0.1 copy.27
  20.4 1.2 fusion.27
  21.6 7.5 %all_to_all.21 = bf16[1,4,128,192]{2,3,0,1:T(8,128)(2,1)S(1)} all-to-all(bf16[1,4,128,192]{2,3,0,1:T(8,128)(2,1)S(1)} %fusion.27), channel_id=1, replica_groups=mesh['expert'=4,'blk'=32] {'expert'}, dimensions={1} | all-to-all | bytes 393216 | tf_op jit(solution)/shard_map/all_to_all | solution.py:28
  29.2 0.2 copy.29
  29.3 0.7 copy.39
  30.0 0.0 all-gather.5.cloned.1.call-update
  30.1 0.0 reduce-scatter.7.cloned.1.call-start
  30.1 41.5 %all-gather.3.cloned.1.call-done = bf16[512,6144]{0,1:T(8,128)(2,1)} async-done(((bf16[512,192]{0,1:T(8,128)(2,1)}), bf16[512,6144]{0,1:T(8,128)(2,1)}) %all-gather.3.cloned.1.call-update) | async-done | bytes 6291472 | tf_op jit(solution)/shard_map/all_gather | solution.py:30
  71.6 0.0 copy-start.1
  71.6 0.0 slice-start
  71.6 8.2 %fusion.10 = f32[512,512]{1,0:T(8,128)S(1)} fusion(bf16[512,6144]{0,1:T(8,128)(2,1)} %all-gather.3.cloned.1.call-done, bf16[1,6144,512]{2,1,0:T(8,128)(2,1)} %param.9), kind=kOutput, calls=%fused_computation.12 | convolution fusion | flops 3221225472 | bytes 13631488 | tf_op jit(solution)/shard_map/dot_general | solution.py:31
  79.8 0.0 copy-done.1
  79.8 0.0 slice-start.1
  79.8 6.5 %fusion.21 = bf16[512,512]{1,0:T(8,128)(2,1)S(1)} fusion(bf16[512,6144]{0,1:T(8,128)(2,1)S(1)} %copy-done.1, bf16[1,6144,512]{2,1,0:T(8,128)(2,1)} %param.10, f32[512,512]{1,0:T(8,128)S(1)} %fusion.10), kind=kOutput, calls=%fused_computation.17 | convolution fusion | flops 3222798336 | bytes 14155776 | tf_op jit(solution)/shard_map/dot_general | solution.py:32
  86.4 0.0 slice-done
  86.4 0.0 slice-done.1
  86.4 5.3 %fusion = bf16[6144,512]{0,1:T(8,128)(2,1)} fusion(bf16[512,512]{1,0:T(8,128)(2,1)S(1)} %fusion.21, bf16[1,512,6144]{2,1,0:T(8,128)(2,1)S(1)} %bitcast.112), kind=kOutput, calls=%fused_computation.2 | convolution fusion | flops 3224371200 | bytes 13107200 | tf_op jit(solution)/shard_map/dot_general | solution.py:35
  91.7 8.7 %copy.31 = bf16[6144,512]{1,0:T(8,128)(2,1)} copy(bf16[6144,512]{0,1:T(8,128)(2,1)} %fusion) | data formatting | bytes 12582912
  100.3 0.0 reduce-scatter.7.cloned.1.call-update
  100.4 0.2 reduce-scatter.9.cloned.1.call-start
  100.6 21.4 %all-gather.5.cloned.1.call-done = bf16[512,6144]{0,1:T(8,128)(2,1)} async-done(((bf16[512,192]{0,1:T(8,128)(2,1)}), bf16[512,6144]{0,1:T(8,128)(2,1)}) %all-gather.5.cloned.1.call-update) | async-done | bytes 6291472 | tf_op jit(solution)/shard_map/all_gather | solution.py:30
  122.0 0.0 copy-start.2
  122.0 0.0 slice-start.2
  122.0 8.2 %fusion.8 = f32[512,512]{1,0:T(8,128)S(1)} fusion(bf16[512,6144]{0,1:T(8,128)(2,1)} %all-gather.5.cloned.1.call-done, bf16[1,6144,512]{2,1,0:T(8,128)(2,1)} %param.9), kind=kOutput, calls=%fused_computation.10 | convolution fusion | flops 3221225472 | bytes 13631488 | tf_op jit(solution)/shard_map/dot_general | solution.py:31
  130.3 0.0 copy-done.2
  130.3 0.0 slice-start.3
  130.3 6.6 %fusion.18 = bf16[512,512]{1,0:T(8,128)(2,1)S(1)} fusion(bf16[512,6144]{0,1:T(8,128)(2,1)S(1)} %copy-done.2, bf16[1,6144,512]{2,1,0:T(8,128)(2,1)} %param.10, f32[512,512]{1,0:T(8,128)S(1)} %fusion.8), kind=kOutput, calls=%fused_computation.16 | convolution fusion | flops 3222798336 | bytes 14155776 | tf_op jit(solution)/shard_map/dot_general | solution.py:32
  136.9 0.0 slice-done.2
  136.9 0.0 slice-done.3
  136.9 5.3 %fusion.1 = bf16[6144,512]{0,1:T(8,128)(2,1)} fusion(bf16[512,512]{1,0:T(8,128)(2,1)S(1)} %fusion.18, bf16[1,512,6144]{2,1,0:T(8,128)(2,1)S(1)} %bitcast.114), kind=kOutput, calls=%fused_computation.3 | convolution fusion | flops 3224371200 | bytes 13107200 | tf_op jit(solution)/shard_map/dot_general | solution.py:35
  142.2 8.8 %copy.33 = bf16[6144,512]{1,0:T(8,128)(2,1)} copy(bf16[6144,512]{0,1:T(8,128)(2,1)} %fusion.1) | data formatting | bytes 12582912
  151.0 0.0 copy-start
  151.0 0.0 reduce-scatter.9.cloned.1.call-update
  151.0 0.7 copy-done
  151.7 57.3 %reduce-scatter.7.cloned.1.call-done = bf16[192,512]{1,0:T(8,128)(2,1)} async-done(((bf16[6144,512]{1,0:T(8,128)(2,1)}), bf16[192,512]{1,0:T(8,128)(2,1)}) %reduce-scatter.7.cloned.1.call-update) | async-done | bytes 196624
  209.0 1.1 copy.32
  210.0 0.8 copy.25
  210.8 4.0 %all-to-all-start.1 = ((bf16[192,1,4,128]{3,0,1,2:T(8,128)(2,1)}), bf16[192,1,4,128]{3,0,1,2:T(8,128)(2,1)S(1)}, u32[]{:S(2)}, u32[]{:S(2)}) async-start(bf16[192,1,4,128]{3,0,1,2:T(8,128)(2,1)} %copy.25), calls=%async_computation.1 | async-start | bytes 393216 | tf_op jit(solution)/shard_map/all_to_all | solution.py:42
  214.9 83.8 %reduce-scatter.9.cloned.1.call-done = bf16[192,512]{1,0:T(8,128)(2,1)} async-done(((bf16[6144,512]{1,0:T(8,128)(2,1)}), bf16[192,512]{1,0:T(8,128)(2,1)}) %reduce-scatter.9.cloned.1.call-update) | async-done | bytes 196624
  298.7 1.1 copy.34
  299.7 0.8 copy.30
  300.6 0.0 all-to-all-done.1
  300.6 4.0 %all-to-all-start.3 = ((bf16[192,1,4,128]{3,0,1,2:T(8,128)(2,1)}), bf16[192,1,4,128]{3,0,1,2:T(8,128)(2,1)S(1)}, u32[]{:S(2)}, u32[]{:S(2)}) async-start(bf16[192,1,4,128]{3,0,1,2:T(8,128)(2,1)} %copy.30), calls=%async_computation.3 | async-start | bytes 393216 | tf_op jit(solution)/shard_map/all_to_all | solution.py:42
  304.6 0.4 fusion.24
  304.9 4.8 %all-to-all-done.3 = bf16[192,1,4,128]{3,0,1,2:T(8,128)(2,1)S(1)} async-done(((bf16[192,1,4,128]{3,0,1,2:T(8,128)(2,1)}), bf16[192,1,4,128]{3,0,1,2:T(8,128)(2,1)S(1)}, u32[]{:S(2)}, u32[]{:S(2)}) %all-to-all-start.3) | async-done | bytes 196640 | tf_op jit(solution)/shard_map/all_to_all | solution.py:42
  309.7 0.4 fusion.25
  310.1 0.7 pad_maximum_fusion
  (8 shorter events, 0.0 us)
Async XLA Ops:
  6.5 65.1 %all-gather.3.cloned.1.call-start = ((), (), s32[]{:S(2)}) async-start(), calls=%async_computation.6 | async-start | bytes 6488064 | tf_op jit(solution)/shard_map/all_gather | solution.py:30
  20.0 102.0 %all-gather.5.cloned.1.call-start = ((), (), s32[]{:S(2)}) async-start(), calls=%async_computation.7 | async-start | bytes 6488064 | tf_op jit(solution)/shard_map/all_gather | solution.py:30
  30.1 178.9 %reduce-scatter.7.cloned.1.call-start = ((), (), s32[]{:S(2)}) async-start(), calls=%async_computation.8 | async-start | bytes 6488064
  71.6 8.2 %copy-start.1 = (bf16[512,6144]{0,1:T(8,128)(2,1)S(1)}, bf16[512,6144]{0,1:T(8,128)(2,1)}, u32[]{:S(2)}) copy-start(bf16[512,6144]{0,1:T(8,128)(2,1)} %all-gather.3.cloned.1.call-done) | copy-start | bytes 18874372
  71.6 14.8 %slice-start = ((s8[6291456]{0:T(1024)(128)(4,1)}), s8[4194304]{0:T(1024)(128)(4,1)S(1)}, s32[]{:S(2)}) async-start(s8[6291456]{0:T(1024)(128)(4,1)} %bitcast.111), calls=%async_computation.10 | async-start | bytes 8388608
  79.8 6.6 %slice-start.1 = ((s8[6291456]{0:T(1024)(128)(4,1)}), s8[2097152]{0:T(1024)(128)(4,1)S(1)}, s32[]{:S(2)}) async-start(s8[6291456]{0:T(1024)(128)(4,1)} %bitcast.111), calls=%async_computation.11 | async-start | bytes 4194304
  100.4 198.3 %reduce-scatter.9.cloned.1.call-start = ((), (), s32[]{:S(2)}) async-start(), calls=%async_computation.9 | async-start | bytes 6488064
  122.0 8.2 %copy-start.2 = (bf16[512,6144]{0,1:T(8,128)(2,1)S(1)}, bf16[512,6144]{0,1:T(8,128)(2,1)}, u32[]{:S(2)}) copy-start(bf16[512,6144]{0,1:T(8,128)(2,1)} %all-gather.5.cloned.1.call-done) | copy-start | bytes 18874372
  122.0 14.8 %slice-start.2 = ((s8[6291456]{0:T(1024)(128)(4,1)}), s8[4194304]{0:T(1024)(128)(4,1)S(1)}, s32[]{:S(2)}) async-start(s8[6291456]{0:T(1024)(128)(4,1)} %bitcast.113), calls=%async_computation.12 | async-start | bytes 8388608
  130.3 6.6 %slice-start.3 = ((s8[6291456]{0:T(1024)(128)(4,1)}), s8[2097152]{0:T(1024)(128)(4,1)S(1)}, s32[]{:S(2)}) async-start(s8[6291456]{0:T(1024)(128)(4,1)} %bitcast.113), calls=%async_computation.13 | async-start | bytes 4194304
  151.0 0.7 copy-start
  210.8 89.7 %all-to-all-start.1 = ((bf16[192,1,4,128]{3,0,1,2:T(8,128)(2,1)}), bf16[192,1,4,128]{3,0,1,2:T(8,128)(2,1)S(1)}, u32[]{:S(2)}, u32[]{:S(2)}) async-start(bf16[192,1,4,128]{3,0,1,2:T(8,128)(2,1)} %copy.25), calls=%async_computation.1 | async-start | bytes 393216 | tf_op jit(solution)/shard_map/all_to_all | solution.py:42
  300.6 9.2 %all-to-all-start.3 = ((bf16[192,1,4,128]{3,0,1,2:T(8,128)(2,1)}), bf16[192,1,4,128]{3,0,1,2:T(8,128)(2,1)S(1)}, u32[]{:S(2)}, u32[]{:S(2)}) async-start(bf16[192,1,4,128]{3,0,1,2:T(8,128)(2,1)} %copy.30), calls=%async_computation.3 | async-start | bytes 393216 | tf_op jit(solution)/shard_map/all_to_all | solution.py:42
Sparse Core Ops, SparseCore 0:
  20.1 51.4 all-gather.2
  73.9 48.1 all-gather.4
  125.8 83.1 reduce-scatter.6
  213.0 85.6 reduce-scatter.8
where the time goes:
time: 321 us; the launch traced here: 317 us
  waiting for transfers between devices  209 us (65%)
  matrix products  43.2 us (13%)
  local copies, waits for them, and re-layouts  24.7 us (8%)
  blocking collectives  17.5 us (5%)
  between operations  13.3 us (4%)
  starting transfers between devices  8.31 us (3%)
    unnamed x6, waiting for transfers between devices  141 us
    all_gather x2, waiting for transfers between devices, expert_layer(): fragment = lax.all_gather(slot_rows, 'blk', axis=1, tiled=True)  63 us
    unnamed x20, local copies, waits for them, and re-layouts  21.7 us
    all_to_all x2, blocking collectives, expert_layer(): lax.all_to_all(outgoing, 'expert', split_axis=1, concat_axis=1, tiled=True)  17.5 us
    dot_general x2, matrix products, expert_layer(): gate_pre = jnp.dot(fragment, gate_mat, preferred_element_type=jnp.float32)  16.4 us
    dot_general x2, matrix products, expert_layer(): up_pre = jnp.dot(fragment, up_mat, preferred_element_type=jnp.float32)  13.1 us
    dot_general x2, matrix products, expert_layer(): lax.dot_general(down_mat, hidden, (((0,), (1,)), ((), ())), preferred_ele...  10.6 us
    all_to_all x2, starting transfers between devices, expert_layer(): lax.all_to_all(summed.reshape(feature_cols, step_count, experts, row_coun...  8 us
  transfers between devices with their start and end apart: 6, of which 5 were waited for; matrix products, arithmetic and copies ran while one was open for 20% of the time, Pallas kernels for 0%

commit v1 on v0

v1 whole, which is shorter than its diff:
```python
import jax
import jax.numpy as jnp
from jax import lax
from jax.experimental import pallas as pl
from jax.experimental.pallas import tpu as pltpu
from jax.sharding import PartitionSpec as P

SIDE = 4
BF = jnp.bfloat16
F32 = jnp.float32


def blk_perm(bulk, shift):
    pairs = []
    for z in range(SIDE):
        for x in range(SIDE):
            for c in range(2):
                along_z = (c == 0) == bulk
                z2 = (z + shift) % SIDE if along_z else z
                x2 = x if along_z else (x + shift) % SIDE
                pairs.append(((z * SIDE + x) * 2 + c, (z2 * SIDE + x2) * 2 + c))
    return pairs


def move_bulk(v, shift):
    return lax.ppermute(v, "blk", blk_perm(True, shift))


def move_small(v, shift):
    return lax.ppermute(v, "blk", blk_perm(False, shift))


def move_core(v):
    return lax.ppermute(v, "blk", [(i, i ^ 1) for i in range(2 * SIDE * SIDE)])


def move_expert(v, shift):
    return lax.ppermute(v, "expert", [(i, (i + shift) % SIDE) for i in range(SIDE)])


def feature_block(z, x, core, bulk_shift, small_shift):
    along_z = jnp.where(core == 0, bulk_shift, small_shift)
    along_x = jnp.where(core == 0, small_shift, bulk_shift)
    return ((z + along_z) % SIDE) * SIDE + (x + along_x) % SIDE


def up_call(pieces, idx, gate_w, up_w, carry, final):
    n = len(pieces)
    rows, width = pieces[0].shape[1:]
    cols = gate_w.shape[1]
    tile = 256

    def kernel(idx_ref, *refs):
        xs = refs[:n]
        ws = refs[n : n + 8 * n]
        rest = refs[n + 8 * n :]
        x = jnp.concatenate([r[k] for r in xs for k in range(SIDE)], axis=1)
        g = jnp.dot(x, jnp.concatenate([w[...] for w in ws[: 4 * n]], axis=0), preferred_element_type=F32)
        u = jnp.dot(x, jnp.concatenate([w[...] for w in ws[4 * n :]], axis=0), preferred_element_type=F32)
        if carry is not None:
            g = g + rest[0][...]
            u = u + rest[1][...]
            rest = rest[2:]
        if final:
            rest[0][...] = (g / (1.0 + jnp.exp(-g)) * u).astype(BF)
        else:
            rest[0][...] = g
            rest[1][...] = u

    def wspec(k):
        return pl.BlockSpec((width, tile), lambda j, idx_ref: (idx_ref[k], j))

    out_spec = pl.BlockSpec((rows, tile), lambda j, idx_ref: (0, j))
    in_specs = [pl.BlockSpec((SIDE, rows, width), lambda j, idx_ref: (0, 0, 0))] * n
    in_specs += [wspec(k) for k in range(4 * n)] * 2
    args = [*pieces, *([gate_w] * (4 * n)), *([up_w] * (4 * n))]
    if carry is not None:
        in_specs += [out_spec] * 2
        args += list(carry)
    if final:
        out_shape = jax.ShapeDtypeStruct((rows, cols), BF)
        out_specs = out_spec
    else:
        out_shape = [jax.ShapeDtypeStruct((rows, cols), F32)] * 2
        out_specs = [out_spec] * 2
    return pl.pallas_call(
        kernel,
        grid_spec=pltpu.PrefetchScalarGridSpec(
            num_scalar_prefetch=1, grid=(cols // tile,), in_specs=in_specs, out_specs=out_specs
        ),
        out_shape=out_shape,
        compiler_params=pltpu.CompilerParams(vmem_limit_bytes=24 << 20),
        cost_estimate=pl.CostEstimate(
            flops=2 * rows * 4 * n * width * cols * 2,
            bytes_accessed=4 * n * width * cols * 4 + n * 4 * rows * width * 2 + rows * cols * 8,
            transcendentals=0,
        ),
        name="up",
    )(idx, *args)


def down_call(hidden, idx, down_w, add):
    rows, depth = hidden.shape
    width = down_w.shape[1] // (SIDE * SIDE)

    def kernel(idx_ref, h_ref, w0, w1, *rest):
        y = jnp.dot(h_ref[...], jnp.concatenate([w0[...], w1[...]], axis=1), preferred_element_type=F32)
        for k in range(2):
            part = y[:, k * width : (k + 1) * width]
            if add is not None:
                part = part + rest[0][k].astype(F32)
            rest[-1][k] = part.astype(BF)

    block = pl.BlockSpec((2, rows, width), lambda j, idx_ref: (j, 0, 0))
    in_specs = [
        pl.BlockSpec((rows, depth), lambda j, idx_ref: (0, 0)),
        pl.BlockSpec((depth, width), lambda j, idx_ref: (0, idx_ref[2 * j])),
        pl.BlockSpec((depth, width), lambda j, idx_ref: (0, idx_ref[2 * j + 1])),
    ]
    args = [hidden, down_w, down_w]
    if add is not None:
        in_specs.append(block)
        args.append(add)
    return pl.pallas_call(
        kernel,
        grid_spec=pltpu.PrefetchScalarGridSpec(
            num_scalar_prefetch=1, grid=(SIDE // 2,), in_specs=in_specs, out_specs=block
        ),
        out_shape=jax.ShapeDtypeStruct((SIDE, rows, width), BF),
        compiler_params=pltpu.CompilerParams(vmem_limit_bytes=16 << 20),
        cost_estimate=pl.CostEstimate(
            flops=2 * rows * depth * width * SIDE,
            bytes_accessed=SIDE * width * (depth + rows * 2) * 2 + rows * depth * 2,
            transcendentals=0,
        ),
        name="down",
    )(idx, *args)


def fsum(parts):
    total = parts[0].astype(F32)
    for p in parts[1:]:
        total = total + p.astype(F32)
    return total


def body(tokens, expert_ids, route_share, gate_weight, up_weight, down_weight):
    expert = lax.axis_index("expert")
    place = lax.axis_index("blk")
    z, x, c = place // (2 * SIDE), (place // 2) % SIDE, place % 2
    gate_w, up_w, down_w = gate_weight[0], up_weight[0], down_weight[0]
    half = tokens.shape[2]
    rows = tokens.shape[1]

    mine = jnp.where(c == 0, tokens[0], tokens[1])
    theirs = jnp.where(c == 0, tokens[1], tokens[0])
    got = move_core(theirs)
    pair = jnp.where(
        c == 0, jnp.concatenate([mine, got], axis=1), jnp.concatenate([got, mine], axis=1)
    )
    owners = jnp.concatenate([pair] + [move_expert(pair, d) for d in range(1, SIDE)], axis=0)
    line = jnp.stack([owners] + [move_small(owners, d) for d in range(1, SIDE)])
    own = {0: line}
    for d in (1, 3, 2):
        own[d] = move_bulk(line, d)
    other = {d: move_core(own[d]) for d in (0, 1, 3, 2)}

    def idx_in(core, d):
        return jnp.stack([feature_block(z, x, core, -d, -k) for k in range(SIDE)]).astype(jnp.int32)

    def idx_out(core, d):
        return jnp.stack([feature_block(z, x, core, d, k) for k in range(SIDE)]).astype(jnp.int32)

    hidden = []
    carry_own = carry_other = None
    for d in (0, 1, 3, 2):
        carry_own = up_call([own[d]], idx_in(c, d), gate_w, up_w, carry_own, d == 2)
        carry_other = up_call([other[d]], idx_in(1 - c, d), gate_w, up_w, carry_other, d == 2)
    h_own, h_other = carry_own, carry_other

    merged = {}
    for d in (2, 1, 3, 0):
        sent = move_core(down_call(h_own, idx_out(1 - c, d), down_w, None))
        merged[d] = down_call(h_other, idx_out(c, d), down_w, sent)
    line_sum = fsum([merged[0]] + [move_bulk(merged[d], d) for d in (1, 3, 2)]).astype(BF)
    plane = fsum([line_sum[0]] + [move_small(line_sum[k], k) for k in (1, 3, 2)]).astype(BF)
    plane = plane.reshape(SIDE, rows, 2 * half)

    ids = jnp.where(c == 0, expert_ids[1], expert_ids[0])
    share = jnp.where(c == 0, route_share[1], route_share[0])
    total = 0.0
    for d in range(SIDE):
        back = plane[d] if d == 0 else move_expert(plane[d], -d)
        named = (expert + d) % SIDE
        factor = jnp.where(ids[:, 0] == named, share, 0.0) + jnp.where(ids[:, 1] == named, 1.0 - share, 0.0)
        total = total + factor[:, None] * back.astype(F32)
    total = total.astype(BF)
    low, high = total[:, :half], total[:, half:]
    keep = jnp.where(c == 0, low, high)
    came = move_core(jnp.where(c == 0, high, low))
    return jnp.stack([jnp.where(c == 0, came, keep), jnp.where(c == 0, keep, came)])


def solution(mesh):
    return jax.shard_map(
        body,
        mesh=mesh,
        in_specs=(
            P(None, "expert", "blk"),
            P(None, "expert", None),
            P(None, "expert"),
            P("expert", None, "blk"),
            P("expert", None, "blk"),
            P("expert", "blk", None),
        ),
        out_specs=P(None, "expert", "blk"),
        check_vma=False,
    )
```

time: 321 us -> 188 us (0.59)
  waiting for transfers between devices: 209 us -> 68 us
  Pallas kernels: 0 us -> 51.7 us
  matrix products: 43.2 us -> 0 us
  starting transfers between devices: 8.31 us -> 50.5 us
  blocking collectives: 17.5 us -> 0 us
  local copies, waits for them, and re-layouts: 24.7 us -> 10.3 us
  between operations: 13.3 us -> 0.3 us
  other arithmetic: 1.3 us -> 5.37 us
    unnamed x6 -> x0, waiting for transfers between devices: 141 us -> none
    ppermute x0 -> x28, waiting for transfers between devices: none -> 68 us  [the longest x6 39.5 us: move_bulk(): return lax.ppermute(v, 'blk', blk_perm(True, shift))]
    all_gather x2 -> x0, waiting for transfers between devices: 63 us -> none  [expert_layer(): fragment = lax.all_gather(slot_rows, 'blk', axis=1, tiled=True)]
    pallas_call x0 -> x16, Pallas kernels: none -> 51.7 us  [the longest x8 29.8 us: up_call(): pl.pallas_call(kernel, grid_spec=pltpu.PrefetchScalarGridSpec(num_scalar_...]
    ppermute x0 -> x28, starting transfers between devices: none -> 50.5 us  [the longest x6 18.5 us: move_small(): return lax.ppermute(v, 'blk', blk_perm(False, shift))]
    dot_general x10 -> x0, matrix products: 43.2 us -> none  [the longest x2 16.4 us: expert_layer(): gate_pre = jnp.dot(fragment, gate_mat, preferred_element_type=jnp.float32)]
    all_to_all x2 -> x0, blocking collectives: 17.5 us -> none  [expert_layer(): lax.all_to_all(outgoing, 'expert', split_axis=1, concat_axis=1, tiled=True)]
    unnamed x20, local copies, waits for them, and re-layouts: 21.7 us -> 8.61 us
  transfers between devices with their start and end apart: 6 -> 28, of which waited for: 5 -> 15; matrix products, arithmetic and copies ran while one was open for 20% -> 1% of each run, Pallas kernels for 0% -> 28%
where the time goes in v1:
time: 188 us; the launch traced here: 186 us
  waiting for transfers between devices  68 us (36%)
  Pallas kernels  51.7 us (28%)
  starting transfers between devices  50.5 us (27%)
  local copies, waits for them, and re-layouts  10.3 us (5%)
  other arithmetic  5.37 us (3%)
    ppermute x6, waiting for transfers between devices, move_bulk(): return lax.ppermute(v, 'blk', blk_perm(True, shift))  39.5 us
    pallas_call x8, Pallas kernels, up_call(): pl.pallas_call(kernel, grid_spec=pltpu.PrefetchScalarGridSpec(num_scalar_...  29.8 us
    pallas_call x8, Pallas kernels, down_call(): pl.pallas_call(kernel, grid_spec=pltpu.PrefetchScalarGridSpec(num_scalar_...  22 us
    ppermute x6, starting transfers between devices, move_small(): return lax.ppermute(v, 'blk', blk_perm(False, shift))  18.5 us
    ppermute x10, starting transfers between devices, move_core(): return lax.ppermute(v, 'blk', [(i, i ^ 1) for i in range(2 * SIDE * SIDE)])  18.2 us
    ppermute x6, waiting for transfers between devices, move_small(): return lax.ppermute(v, 'blk', blk_perm(False, shift))  14.8 us
    ppermute x6, waiting for transfers between devices, move_expert(): lax.ppermute(v, 'expert', [(i, (i + shift) % SIDE) for i in range(SIDE)])  11.8 us
    unnamed x20, local copies, waits for them, and re-layouts  8.61 us
  transfers between devices with their start and end apart: 28, of which 15 were waited for; matrix products, arithmetic and copies ran while one was open for 1% of the time, Pallas kernels for 28%

profile of v1, /device:TPU:1, one launch (start us, length us, event | category | flops | bytes accessed | tf_op | source)
XLA Modules:
  0.0 186.2 jit_solution(1474297554622939146)
XLA Ops:
  0.0 0.8 fusion.15
  1.1 1.5 collective-permute-start
  2.6 0.9 collective-permute-done
  3.6 2.9 %collective-permute-start.3 = (bf16[128,384]{1,0:T(8,128)(2,1)S(1)}, bf16[128,384]{1,0:T(8,128)(2,1)S(1)}, u32[]{:S(2)}, u32[]{:S(2)}) collective-permute-start(bf16[128,384]{1,0:T(8,128)(2,1)S(1)} %maximum_select_fusion), channel_id=1, source_target_pairs={{0,96},{32,0},{64,32},{96,64},{1,97},{33,1},{65,33},{97,65},{2,98}... | collective-permute-start | bytes 294920 | tf_op jit(solution)/shard_map/ppermute | solution.py:38
  6.5 0.3 collective-permute-start.2
  6.8 0.7 collective-permute-start.1
  7.5 2.8 %collective-permute-done.3 = bf16[128,384]{1,0:T(8,128)(2,1)S(1)} collective-permute-done((bf16[128,384]{1,0:T(8,128)(2,1)S(1)}, bf16[128,384]{1,0:T(8,128)(2,1)S(1)}, u32[]{:S(2)}, u32[]{:S(2)}) %collective-permute-start.3) | collective-permute-done | bytes 98336 | tf_op jit(solution)/shard_map/ppermute | solution.py:38
  10.3 1.3 collective-permute-done.2
  11.6 3.1 %collective-permute-done.1 = bf16[128,384]{1,0:T(8,128)(2,1)S(1)} collective-permute-done((bf16[128,384]{1,0:T(8,128)(2,1)S(1)}, bf16[128,384]{1,0:T(8,128)(2,1)S(1)}, u32[]{:S(2)}, u32[]{:S(2)}) %collective-permute-start.1) | collective-permute-done | bytes 98336 | tf_op jit(solution)/shard_map/ppermute | solution.py:38
  14.8 3.7 %collective-permute-start.5 = (bf16[512,384]{1,0:T(8,128)(2,1)S(1)}, bf16[512,384]{1,0:T(8,128)(2,1)S(1)}, u32[]{:S(2)}, u32[]{:S(2)}) collective-permute-start(bf16[512,384]{1,0:T(8,128)(2,1)S(1)} %get-tuple-element.38), channel_id=1, source_target_pairs={{0,4},{1,17},{2,6},{3,19},{4,0},{5,21},{6,2},{7,23},{8,12},{9,25},... | collective-permute-start | bytes 1179656 | tf_op jit(solution)/shard_map/ppermute | solution.py:30
  18.4 0.7 collective-permute-start.4
  19.2 1.9 %collective-permute-start.6 = (bf16[512,384]{1,0:T(8,128)(2,1)S(1)}, bf16[512,384]{1,0:T(8,128)(2,1)S(1)}, u32[]{:S(2)}, u32[]{:S(2)}) collective-permute-start(bf16[512,384]{1,0:T(8,128)(2,1)S(1)} %get-tuple-element.38), channel_id=1, source_target_pairs={{0,6},{1,25},{2,0},{3,27},{4,2},{5,29},{6,4},{7,31},{8,14},{9,1},{... | collective-permute-start | bytes 1179656 | tf_op jit(solution)/shard_map/ppermute | solution.py:30
  21.1 2.8 %collective-permute-done.5 = bf16[512,384]{1,0:T(8,128)(2,1)S(1)} collective-permute-done((bf16[512,384]{1,0:T(8,128)(2,1)S(1)}, bf16[512,384]{1,0:T(8,128)(2,1)S(1)}, u32[]{:S(2)}, u32[]{:S(2)}) %collective-permute-start.5) | collective-permute-done | bytes 393248 | tf_op jit(solution)/shard_map/ppermute | solution.py:30
  23.9 4.2 %collective-permute-done.4 = bf16[512,384]{1,0:T(8,128)(2,1)S(1)} collective-permute-done((bf16[512,384]{1,0:T(8,128)(2,1)S(1)}, bf16[512,384]{1,0:T(8,128)(2,1)S(1)}, u32[]{:S(2)}, u32[]{:S(2)}) %collective-permute-start.4) | collective-permute-done | bytes 393248 | tf_op jit(solution)/shard_map/ppermute | solution.py:30
  28.1 0.5 collective-permute-done.6
  28.6 0.2 pad_maximum_fusion.refs_0_
  28.9 1.3 collective-permute-start.11
  30.2 1.5 collective-permute-start.9
  31.6 1.5 collective-permute-start.7
  33.2 2.1 %collective-permute-start.13 = (bf16[4,512,384]{2,1,0:T(8,128)(2,1)S(1)}, bf16[4,512,384]{2,1,0:T(8,128)(2,1)}, u32[]{:S(2)}, u32[]{:S(2)}) collective-permute-start(bf16[4,512,384]{2,1,0:T(8,128)(2,1)S(1)} %pad_maximum_fusion.refs_0_), channel_id=1, source_target_pairs={{0,1},{1,0},{2,3},{3,2},{4,5},{5,4},{6,7},{7,6},{8,9},{9,8},{10,11... | collective-permute-start | bytes 4718600 | tf_op jit(solution)/shard_map/ppermute | solution.py:34
  35.4 14.5 %collective-permute-done.11.refs_0_ = bf16[4,512,384]{2,1,0:T(8,128)(2,1)} collective-permute-done((bf16[4,512,384]{2,1,0:T(8,128)(2,1)S(1)}, bf16[4,512,384]{2,1,0:T(8,128)(2,1)}, u32[]{:S(2)}, u32[]{:S(2)}) %collective-permute-start.11) | collective-permute-done | bytes 1572896 | tf_op jit(solution)/shard_map/ppermute | solution.py:26
  49.8 2.1 %collective-permute-start.12 = (bf16[4,512,384]{2,1,0:T(8,128)(2,1)}, bf16[4,512,384]{2,1,0:T(8,128)(2,1)S(1)}, u32[]{:S(2)}, u32[]{:S(2)}) collective-permute-start(bf16[4,512,384]{2,1,0:T(8,128)(2,1)} %collective-permute-done.11.refs_0_), channel_id=1, source_target_pairs={{0,1},{1,0},{2,3},{3,2},{4,5},{5,4},{6,7},{7,6},{8,9},{9,8},{10,11... | collective-permute-start | bytes 4718600 | tf_op jit(solution)/shard_map/ppermute | solution.py:34
  52.4 2.8 %copy-done = bf16[1,6144,512]{2,1,0:T(8,128)(2,1)S(1)} copy-done((bf16[1,6144,512]{2,1,0:T(8,128)(2,1)S(1)}, bf16[1,6144,512]{2,1,0:T(8,128)(2,1)}, u32[]{:S(2)}) %copy-start) | copy-done | bytes 6291480
  55.2 2.8 %copy-done.1 = bf16[1,6144,512]{2,1,0:T(8,128)(2,1)S(1)} copy-done((bf16[1,6144,512]{2,1,0:T(8,128)(2,1)S(1)}, bf16[1,6144,512]{2,1,0:T(8,128)(2,1)}, u32[]{:S(2)}) %copy-start.1) | copy-done | bytes 6291480
  58.0 3.1 %up.12 = (f32[512,512]{1,0:T(8,128)S(1)}, f32[512,512]{1,0:T(8,128)S(1)}) custom-call(s32[4]{0:T(128)S(1)} %pad_add_fusion.7.idx_ref, bf16[4,512,384]{2,1,0:T(8,128)(2,1)S(1)} %pad_maximum_fusion.refs_0_, bf16[6144,512]{1,0:T(8,128)(2,1)S(1)} %bitcast.95, bf16[6144,512]{1,0:T(8,128)(2,1)S(1)} %bitcast.96, bf16[6144,512]{1,0:T(8,128)(2,1)S(1)} %bitcast.97, ...), custom_call_target="tpu_custom_call" | custom-call | flops 1610612736 | bytes 6815744 | tf_op jit(solution)/shard_map/up/pallas_call | solution.py:86
  61.1 7.2 %collective-permute-start.10 = (bf16[4,512,384]{2,1,0:T(8,128)(2,1)}, bf16[4,512,384]{2,1,0:T(8,128)(2,1)S(1)}, u32[]{:S(2)}, u32[]{:S(2)}) collective-permute-start(bf16[4,512,384]{2,1,0:T(8,128)(2,1)} %collective-permute-done.9.refs_0_), channel_id=1, source_target_pairs={{0,1},{1,0},{2,3},{3,2},{4,5},{5,4},{6,7},{7,6},{8,9},{9,8},{10,11... | collective-permute-start | bytes 4718600 | tf_op jit(solution)/shard_map/ppermute | solution.py:34
  68.3 1.8 collective-permute-start.8
  70.1 4.5 %up.13 = (f32[512,512]{1,0:T(8,128)S(1)}, f32[512,512]{1,0:T(8,128)S(1)}) custom-call(s32[4]{0:T(128)S(1)} %pad_add_fusion.6.idx_ref, bf16[4,512,384]{2,1,0:T(8,128)(2,1)} %collective-permute-done.11.refs_0_, bf16[6144,512]{1,0:T(8,128)(2,1)S(1)} %bitcast.99, bf16[6144,512]{1,0:T(8,128)(2,1)S(1)} %bitcast.100, bf16[6144,512]{1,0:T(8,128)(2,1)S(1)} %bitcast.101, ...), custom_call_target="tpu_custom_call" | custom-call | flops 1610612736 | bytes 6815744 | tf_op jit(solution)/shard_map/up/pallas_call | solution.py:86
  74.6 4.9 %up.14 = (f32[512,512]{1,0:T(8,128)S(1)}, f32[512,512]{1,0:T(8,128)S(1)}) custom-call(s32[4]{0:T(128)S(1)} %add_add_fusion.1.idx_ref, bf16[4,512,384]{2,1,0:T(8,128)(2,1)} %collective-permute-done.9.refs_0_, bf16[6144,512]{1,0:T(8,128)(2,1)S(1)} %bitcast.103, bf16[6144,512]{1,0:T(8,128)(2,1)S(1)} %bitcast.104, bf16[6144,512]{1,0:T(8,128)(2,1)S(1)} %bitcast.105, ...), custom_call_target="tpu_custom_call" | custom-call | flops 1610612736 | bytes 6815744 | tf_op jit(solution)/shard_map/up/pallas_call | solution.py:86
  79.5 3.2 %up.15.h_ref = bf16[512,512]{1,0:T(8,128)(2,1)S(1)} custom-call(s32[4]{0:T(128)S(1)} %pad_add_fusion.5.idx_ref, bf16[4,512,384]{2,1,0:T(8,128)(2,1)S(1)} %collective-permute-done.7.refs_0_, bf16[6144,512]{1,0:T(8,128)(2,1)S(1)} %bitcast.110, bf16[6144,512]{1,0:T(8,128)(2,1)S(1)} %bitcast.108, bf16[6144,512]{1,0:T(8,128)(2,1)S(1)} %bitcast.109, ...), custom_call_target="tpu_custom_call" | custom-call | flops 1610612736 | bytes 6815744 | tf_op jit(solution)/shard_map/up/pallas_call | solution.py:86
  82.7 2.8 %down.10 = bf16[4,512,384]{2,1,0:T(8,128)(2,1)} custom-call(s32[4]{0:T(128)S(1)} %pad_add_fusion.9.idx_ref, bf16[512,512]{1,0:T(8,128)(2,1)S(1)} %up.15.h_ref, bf16[512,6144]{1,0:T(8,128)(2,1)S(1)} %bitcast.163, bf16[512,6144]{1,0:T(8,128)(2,1)S(1)} %bitcast.164), custom_call_target="tpu_custom_call" | custom-call | flops 805306368 | bytes 5242880 | tf_op jit(solution)/shard_map/down/pallas_call | solution.py:124
  85.6 2.9 %down.12 = bf16[4,512,384]{2,1,0:T(8,128)(2,1)} custom-call(s32[4]{0:T(128)S(1)} %add_add_fusion.3.idx_ref, bf16[512,512]{1,0:T(8,128)(2,1)S(1)} %up.15.h_ref, bf16[512,6144]{1,0:T(8,128)(2,1)S(1)} %bitcast.165, bf16[512,6144]{1,0:T(8,128)(2,1)S(1)} %bitcast.166), custom_call_target="tpu_custom_call" | custom-call | flops 805306368 | bytes 5242880 | tf_op jit(solution)/shard_map/down/pallas_call | solution.py:124
  88.5 0.5 collective-permute-start.17
  89.0 2.8 %down.14 = bf16[4,512,384]{2,1,0:T(8,128)(2,1)} custom-call(s32[4]{0:T(128)S(1)} %pad_add_fusion.11.idx_ref, bf16[512,512]{1,0:T(8,128)(2,1)S(1)} %up.15.h_ref, bf16[512,6144]{1,0:T(8,128)(2,1)S(1)} %bitcast.167, bf16[512,6144]{1,0:T(8,128)(2,1)S(1)} %bitcast.168), custom_call_target="tpu_custom_call" | custom-call | flops 805306368 | bytes 5242880 | tf_op jit(solution)/shard_map/down/pallas_call | solution.py:124
  92.4 2.9 %down.8 = bf16[4,512,384]{2,1,0:T(8,128)(2,1)} custom-call(s32[4]{0:T(128)S(1)} %pad_add_fusion.4.idx_ref, bf16[512,512]{1,0:T(8,128)(2,1)S(1)} %up.15.h_ref, bf16[512,6144]{1,0:T(8,128)(2,1)S(1)} %bitcast.169, bf16[512,6144]{1,0:T(8,128)(2,1)S(1)} %bitcast.170), custom_call_target="tpu_custom_call" | custom-call | flops 805306368 | bytes 5242880 | tf_op jit(solution)/shard_map/down/pallas_call | solution.py:124
  95.2 4.3 %up.8 = (f32[512,512]{1,0:T(8,128)S(1)}, f32[512,512]{1,0:T(8,128)S(1)}) custom-call(s32[4]{0:T(128)S(1)} %pad_add_fusion.3.idx_ref, bf16[4,512,384]{2,1,0:T(8,128)(2,1)} %collective-permute-done.13.refs_0_, bf16[6144,512]{1,0:T(8,128)(2,1)S(1)} %bitcast.113, bf16[6144,512]{1,0:T(8,128)(2,1)S(1)} %bitcast.114, bf16[6144,512]{1,0:T(8,128)(2,1)S(1)} %bitcast.115, ...), custom_call_target="tpu_custom_call" | custom-call | flops 1610612736 | bytes 6815744 | tf_op jit(solution)/shard_map/up/pallas_call | solution.py:86
  99.6 3.3 %up.9 = (f32[512,512]{1,0:T(8,128)S(1)}, f32[512,512]{1,0:T(8,128)S(1)}) custom-call(s32[4]{0:T(128)S(1)} %pad_add_fusion.2.idx_ref, bf16[4,512,384]{2,1,0:T(8,128)(2,1)S(1)} %collective-permute-done.12.refs_0_, bf16[6144,512]{1,0:T(8,128)(2,1)S(1)} %bitcast.117, bf16[6144,512]{1,0:T(8,128)(2,1)S(1)} %bitcast.118, bf16[6144,512]{1,0:T(8,128)(2,1)S(1)} %bitcast.119, ...), custom_call_target="tpu_custom_call" | custom-call | flops 1610612736 | bytes 6815744 | tf_op jit(solution)/shard_map/up/pallas_call | solution.py:86
  102.9 0.6 collective-permute-start.14
  103.5 3.3 %up.10 = (f32[512,512]{1,0:T(8,128)S(1)}, f32[512,512]{1,0:T(8,128)S(1)}) custom-call(s32[4]{0:T(128)S(1)} %add_add_fusion.idx_ref, bf16[4,512,384]{2,1,0:T(8,128)(2,1)S(1)} %collective-permute-done.10.refs_0_, bf16[6144,512]{1,0:T(8,128)(2,1)S(1)} %bitcast.121, bf16[6144,512]{1,0:T(8,128)(2,1)S(1)} %bitcast.122, bf16[6144,512]{1,0:T(8,128)(2,1)S(1)} %bitcast.123, ...), custom_call_target="tpu_custom_call" | custom-call | flops 1610612736 | bytes 6815744 | tf_op jit(solution)/shard_map/up/pallas_call | solution.py:86
  106.8 3.2 %up.11.h_ref = bf16[512,512]{1,0:T(8,128)(2,1)S(1)} custom-call(s32[4]{0:T(128)S(1)} %pad_add_fusion.1.idx_ref, bf16[4,512,384]{2,1,0:T(8,128)(2,1)S(1)} %collective-permute-done.8.refs_0_, bf16[6144,512]{1,0:T(8,128)(2,1)S(1)} %bitcast.125, bf16[6144,512]{1,0:T(8,128)(2,1)S(1)} %bitcast.126, bf16[6144,512]{1,0:T(8,128)(2,1)S(1)} %bitcast.127, ...), custom_call_target="tpu_custom_call" | custom-call | flops 1610612736 | bytes 6815744 | tf_op jit(solution)/shard_map/up/pallas_call | solution.py:86
  110.0 1.9 %down.11 = bf16[4,512,384]{2,1,0:T(8,128)(2,1)S(1)} custom-call(s32[4]{0:T(128)S(1)} %pad_add_fusion.8.idx_ref, bf16[512,512]{1,0:T(8,128)(2,1)S(1)} %up.11.h_ref, bf16[512,6144]{1,0:T(8,128)(2,1)S(1)} %bitcast.171, bf16[512,6144]{1,0:T(8,128)(2,1)S(1)} %bitcast.172, bf16[4,512,384]{2,1,0:T(8,128)(2,1)S(1)} %collective-permute-done.15.rest_0_), custom_call_target="tpu_custom_call" | custom-call | flops 805306368 | bytes 5242880 | tf_op jit(solution)/shard_map/down/pallas_call | solution.py:124
  112.0 1.3 collective-permute-start.16
  113.2 2.8 %down.13 = bf16[4,512,384]{2,1,0:T(8,128)(2,1)} custom-call(s32[4]{0:T(128)S(1)} %add_add_fusion.2.idx_ref, bf16[512,512]{1,0:T(8,128)(2,1)S(1)} %up.11.h_ref, bf16[512,6144]{1,0:T(8,128)(2,1)S(1)} %bitcast.173, bf16[512,6144]{1,0:T(8,128)(2,1)S(1)} %bitcast.174, bf16[4,512,384]{2,1,0:T(8,128)(2,1)S(1)} %collective-permute-done.17.rest_0_), custom_call_target="tpu_custom_call" | custom-call | flops 805306368 | bytes 5242880 | tf_op jit(solution)/shard_map/down/pallas_call | solution.py:124
  116.1 1.5 collective-permute-start.18
  117.5 2.8 %down.15 = bf16[4,512,384]{2,1,0:T(8,128)(2,1)} custom-call(s32[4]{0:T(128)S(1)} %pad_add_fusion.10.idx_ref, bf16[512,512]{1,0:T(8,128)(2,1)S(1)} %up.11.h_ref, bf16[512,6144]{1,0:T(8,128)(2,1)S(1)} %bitcast.175, bf16[512,6144]{1,0:T(8,128)(2,1)S(1)} %bitcast.176, bf16[4,512,384]{2,1,0:T(8,128)(2,1)S(1)} %collective-permute-done.19.rest_0_), custom_call_target="tpu_custom_call" | custom-call | flops 805306368 | bytes 5242880 | tf_op jit(solution)/shard_map/down/pallas_call | solution.py:124
  120.4 0.9 collective-permute-start.20
  121.3 2.8 %copy-done.2 = bf16[1,512,6144]{2,1,0:T(8,128)(2,1)S(1)} copy-done((bf16[1,512,6144]{2,1,0:T(8,128)(2,1)S(1)}, bf16[1,512,6144]{2,1,0:T(8,128)(2,1)}, u32[]{:S(2)}) %copy-start.2) | copy-done | bytes 6291480
  124.1 3.0 %down.9 = bf16[4,512,384]{2,1,0:T(8,128)(2,1)S(1)} custom-call(s32[4]{0:T(128)S(1)} %pad_add_fusion.idx_ref, bf16[512,512]{1,0:T(8,128)(2,1)S(1)} %up.11.h_ref, bf16[512,6144]{1,0:T(8,128)(2,1)S(1)} %bitcast.177, bf16[512,6144]{1,0:T(8,128)(2,1)S(1)} %bitcast.178, bf16[4,512,384]{2,1,0:T(8,128)(2,1)} %collective-permute-done.14.rest_0_), custom_call_target="tpu_custom_call" | custom-call | flops 805306368 | bytes 5242880 | tf_op jit(solution)/shard_map/down/pallas_call | solution.py:124
  127.1 5.8 %collective-permute-done.16 = bf16[4,512,384]{2,1,0:T(8,128)(2,1)} collective-permute-done((bf16[4,512,384]{2,1,0:T(8,128)(2,1)S(1)}, bf16[4,512,384]{2,1,0:T(8,128)(2,1)}, u32[]{:S(2)}, u32[]{:S(2)}) %collective-permute-start.16) | collective-permute-done | bytes 1572896 | tf_op jit(solution)/shard_map/ppermute | solution.py:26
  132.9 19.2 %collective-permute-done.18 = bf16[4,512,384]{2,1,0:T(8,128)(2,1)} collective-permute-done((bf16[4,512,384]{2,1,0:T(8,128)(2,1)}, bf16[4,512,384]{2,1,0:T(8,128)(2,1)}, u32[]{:S(2)}, u32[]{:S(2)}) %collective-permute-start.18) | collective-permute-done | bytes 1572896 | tf_op jit(solution)/shard_map/ppermute | solution.py:26
  152.1 3.1 %add_convert_fusion = bf16[4,512,384]{2,1,0:T(8,128)(2,1)S(1)} fusion(bf16[4,512,384]{2,1,0:T(8,128)(2,1)} %collective-permute-done.20, bf16[4,512,384]{2,1,0:T(8,128)(2,1)} %collective-permute-done.18, bf16[4,512,384]{2,1,0:T(8,128)(2,1)} %collective-permute-done.16, bf16[4,512,384]{2,1,0:T(8,128)(2,1)S(1)} %down.9), kind=kLoop, calls=%fused_computation | loop fusion | flops 6291456 | bytes 7864320 | tf_op jit(solution)/shard_map/convert_element_type | solution.py:185
  155.4 7.5 %collective-permute-start.21 = (bf16[512,384]{1,0:T(8,128)(2,1)S(1)}, bf16[512,384]{1,0:T(8,128)(2,1)S(1)}, u32[]{:S(2)}, u32[]{:S(2)}) collective-permute-start(bf16[512,384]{1,0:T(8,128)(2,1)S(1)} %get-tuple-element.31), channel_id=1, source_target_pairs={{0,2},{1,9},{2,4},{3,11},{4,6},{5,13},{6,0},{7,15},{8,10},{9,17},{... | collective-permute-start | bytes 1179656 | tf_op jit(solution)/shard_map/ppermute | solution.py:30
  162.9 2.7 %collective-permute-start.23 = (bf16[512,384]{1,0:T(8,128)(2,1)S(1)}, bf16[512,384]{1,0:T(8,128)(2,1)S(1)}, u32[]{:S(2)}, u32[]{:S(2)}) collective-permute-start(bf16[512,384]{1,0:T(8,128)(2,1)S(1)} %get-tuple-element.32), channel_id=1, source_target_pairs={{0,4},{1,17},{2,6},{3,19},{4,0},{5,21},{6,2},{7,23},{8,12},{9,25},... | collective-permute-start | bytes 1179656 | tf_op jit(solution)/shard_map/ppermute | solution.py:30
  165.6 2.0 %collective-permute-start.22 = (bf16[512,384]{1,0:T(8,128)(2,1)S(1)}, bf16[512,384]{1,0:T(8,128)(2,1)S(1)}, u32[]{:S(2)}, u32[]{:S(2)}) collective-permute-start(bf16[512,384]{1,0:T(8,128)(2,1)S(1)} %get-tuple-element.33), channel_id=1, source_target_pairs={{0,6},{1,25},{2,0},{3,27},{4,2},{5,29},{6,4},{7,31},{8,14},{9,1},{... | collective-permute-start | bytes 1179656 | tf_op jit(solution)/shard_map/ppermute | solution.py:30
  167.6 7.3 %collective-permute-done.23 = bf16[512,384]{1,0:T(8,128)(2,1)S(1)} collective-permute-done((bf16[512,384]{1,0:T(8,128)(2,1)S(1)}, bf16[512,384]{1,0:T(8,128)(2,1)S(1)}, u32[]{:S(2)}, u32[]{:S(2)}) %collective-permute-start.23) | collective-permute-done | bytes 393248 | tf_op jit(solution)/shard_map/ppermute | solution.py:30
  175.1 0.3 collective-permute-start.24
  175.5 1.2 collective-permute-start.26
  176.7 0.4 collective-permute-start.25
  177.1 2.1 %collective-permute-done.24 = bf16[128,384]{1,0:T(8,128)(2,1)S(1)} collective-permute-done((bf16[128,384]{1,0:T(8,128)(2,1)S(1)}, bf16[128,384]{1,0:T(8,128)(2,1)S(1)}, u32[]{:S(2)}, u32[]{:S(2)}) %collective-permute-start.24) | collective-permute-done | bytes 98336 | tf_op jit(solution)/shard_map/ppermute | solution.py:38
  179.2 0.9 collective-permute-done.26
  180.2 1.6 collective-permute-done.25
  182.0 2.4 %collective-permute-start.27 = (bf16[128,192]{1,0:T(8,128)(2,1)S(1)}, bf16[128,192]{1,0:T(8,128)(2,1)S(1)}, u32[]{:S(2)}, u32[]{:S(2)}) collective-permute-start(bf16[128,192]{1,0:T(8,128)(2,1)S(1)} %broadcast_select_fusion.1), channel_id=1, source_target_pairs={{0,1},{1,0},{2,3},{3,2},{4,5},{5,4},{6,7},{7,6},{8,9},{9,8},{10,11... | collective-permute-start | bytes 147464 | tf_op jit(solution)/shard_map/ppermute | solution.py:34
  184.4 0.9 collective-permute-done.27
  185.4 0.7 copy.9
  (63 shorter events, 2.5 us)
Async XLA Ops:
  1.1 2.4 %collective-permute-start = (bf16[128,192]{1,0:T(8,128)(2,1)S(1)}, bf16[128,192]{1,0:T(8,128)(2,1)S(1)}, u32[]{:S(2)}, u32[]{:S(2)}) collective-permute-start(bf16[128,192]{1,0:T(8,128)(2,1)S(1)} %get-tuple-element.42), channel_id=1, source_target_pairs={{0,1},{1,0},{2,3},{3,2},{4,5},{5,4},{6,7},{7,6},{8,9},{9,8},{10,11... | collective-permute-start | bytes 147464 | tf_op jit(solution)/shard_map/ppermute | solution.py:34
  3.6 6.7 %collective-permute-start.3 = (bf16[128,384]{1,0:T(8,128)(2,1)S(1)}, bf16[128,384]{1,0:T(8,128)(2,1)S(1)}, u32[]{:S(2)}, u32[]{:S(2)}) collective-permute-start(bf16[128,384]{1,0:T(8,128)(2,1)S(1)} %maximum_select_fusion), channel_id=1, source_target_pairs={{0,96},{32,0},{64,32},{96,64},{1,97},{33,1},{65,33},{97,65},{2,98}... | collective-permute-start | bytes 294920 | tf_op jit(solution)/shard_map/ppermute | solution.py:38
  6.5 5.1 %collective-permute-start.2 = (bf16[128,384]{1,0:T(8,128)(2,1)S(1)}, bf16[128,384]{1,0:T(8,128)(2,1)S(1)}, u32[]{:S(2)}, u32[]{:S(2)}) collective-permute-start(bf16[128,384]{1,0:T(8,128)(2,1)S(1)} %maximum_select_fusion), channel_id=1, source_target_pairs={{0,64},{32,96},{64,0},{96,32},{1,65},{33,97},{65,1},{97,33},{2,66}... | collective-permute-start | bytes 294920 | tf_op jit(solution)/shard_map/ppermute | solution.py:38
  6.8 7.9 %collective-permute-start.1 = (bf16[128,384]{1,0:T(8,128)(2,1)S(1)}, bf16[128,384]{1,0:T(8,128)(2,1)S(1)}, u32[]{:S(2)}, u32[]{:S(2)}) collective-permute-start(bf16[128,384]{1,0:T(8,128)(2,1)S(1)} %maximum_select_fusion), channel_id=1, source_target_pairs={{0,32},{32,64},{64,96},{96,0},{1,33},{33,65},{65,97},{97,1},{2,34}... | collective-permute-start | bytes 294920 | tf_op jit(solution)/shard_map/ppermute | solution.py:38
  14.8 9.1 %collective-permute-start.5 = (bf16[512,384]{1,0:T(8,128)(2,1)S(1)}, bf16[512,384]{1,0:T(8,128)(2,1)S(1)}, u32[]{:S(2)}, u32[]{:S(2)}) collective-permute-start(bf16[512,384]{1,0:T(8,128)(2,1)S(1)} %get-tuple-element.38), channel_id=1, source_target_pairs={{0,4},{1,17},{2,6},{3,19},{4,0},{5,21},{6,2},{7,23},{8,12},{9,25},... | collective-permute-start | bytes 1179656 | tf_op jit(solution)/shard_map/ppermute | solution.py:30
  18.4 9.7 %collective-permute-start.4 = (bf16[512,384]{1,0:T(8,128)(2,1)S(1)}, bf16[512,384]{1,0:T(8,128)(2,1)S(1)}, u32[]{:S(2)}, u32[]{:S(2)}) collective-permute-start(bf16[512,384]{1,0:T(8,128)(2,1)S(1)} %get-tuple-element.38), channel_id=1, source_target_pairs={{0,2},{1,9},{2,4},{3,11},{4,6},{5,13},{6,0},{7,15},{8,10},{9,17},{... | collective-permute-start | bytes 1179656 | tf_op jit(solution)/shard_map/ppermute | solution.py:30
  19.2 9.5 %collective-permute-start.6 = (bf16[512,384]{1,0:T(8,128)(2,1)S(1)}, bf16[512,384]{1,0:T(8,128)(2,1)S(1)}, u32[]{:S(2)}, u32[]{:S(2)}) collective-permute-start(bf16[512,384]{1,0:T(8,128)(2,1)S(1)} %get-tuple-element.38), channel_id=1, source_target_pairs={{0,6},{1,25},{2,0},{3,27},{4,2},{5,29},{6,4},{7,31},{8,14},{9,1},{... | collective-permute-start | bytes 1179656 | tf_op jit(solution)/shard_map/ppermute | solution.py:30
  28.9 20.9 %collective-permute-start.11 = (bf16[4,512,384]{2,1,0:T(8,128)(2,1)S(1)}, bf16[4,512,384]{2,1,0:T(8,128)(2,1)}, u32[]{:S(2)}, u32[]{:S(2)}) collective-permute-start(bf16[4,512,384]{2,1,0:T(8,128)(2,1)S(1)} %pad_maximum_fusion.refs_0_), channel_id=1, source_target_pairs={{0,8},{1,3},{2,10},{3,5},{4,12},{5,7},{6,14},{7,1},{8,16},{9,11},{... | collective-permute-start | bytes 4718600 | tf_op jit(solution)/shard_map/ppermute | solution.py:26
  30.2 30.9 %collective-permute-start.9 = (bf16[4,512,384]{2,1,0:T(8,128)(2,1)S(1)}, bf16[4,512,384]{2,1,0:T(8,128)(2,1)}, u32[]{:S(2)}, u32[]{:S(2)}) collective-permute-start(bf16[4,512,384]{2,1,0:T(8,128)(2,1)S(1)} %pad_maximum_fusion.refs_0_), channel_id=1, source_target_pairs={{0,24},{1,7},{2,26},{3,1},{4,28},{5,3},{6,30},{7,5},{8,0},{9,15},{... | collective-permute-start | bytes 4718600 | tf_op jit(solution)/shard_map/ppermute | solution.py:26
  31.6 36.7 %collective-permute-start.7 = (bf16[4,512,384]{2,1,0:T(8,128)(2,1)S(1)}, bf16[4,512,384]{2,1,0:T(8,128)(2,1)S(1)}, u32[]{:S(2)}, u32[]{:S(2)}) collective-permute-start(bf16[4,512,384]{2,1,0:T(8,128)(2,1)S(1)} %pad_maximum_fusion.refs_0_), channel_id=1, source_target_pairs={{0,16},{1,5},{2,18},{3,7},{4,20},{5,1},{6,22},{7,3},{8,24},{9,13},... | collective-permute-start | bytes 4718600 | tf_op jit(solution)/shard_map/ppermute | solution.py:26
  33.2 55.2 %collective-permute-start.13 = (bf16[4,512,384]{2,1,0:T(8,128)(2,1)S(1)}, bf16[4,512,384]{2,1,0:T(8,128)(2,1)}, u32[]{:S(2)}, u32[]{:S(2)}) collective-permute-start(bf16[4,512,384]{2,1,0:T(8,128)(2,1)S(1)} %pad_maximum_fusion.refs_0_), channel_id=1, source_target_pairs={{0,1},{1,0},{2,3},{3,2},{4,5},{5,4},{6,7},{7,6},{8,9},{9,8},{10,11... | collective-permute-start | bytes 4718600 | tf_op jit(solution)/shard_map/ppermute | solution.py:34
  49.8 42.0 %collective-permute-start.12 = (bf16[4,512,384]{2,1,0:T(8,128)(2,1)}, bf16[4,512,384]{2,1,0:T(8,128)(2,1)S(1)}, u32[]{:S(2)}, u32[]{:S(2)}) collective-permute-start(bf16[4,512,384]{2,1,0:T(8,128)(2,1)} %collective-permute-done.11.refs_0_), channel_id=1, source_target_pairs={{0,1},{1,0},{2,3},{3,2},{4,5},{5,4},{6,7},{7,6},{8,9},{9,8},{10,11... | collective-permute-start | bytes 4718600 | tf_op jit(solution)/shard_map/ppermute | solution.py:34
  52.4 2.8 %copy-start = (bf16[1,6144,512]{2,1,0:T(8,128)(2,1)S(1)}, bf16[1,6144,512]{2,1,0:T(8,128)(2,1)}, u32[]{:S(2)}) copy-start(bf16[1,6144,512]{2,1,0:T(8,128)(2,1)} %param.9) | copy-start | bytes 18874372
  55.2 2.8 %copy-start.1 = (bf16[1,6144,512]{2,1,0:T(8,128)(2,1)S(1)}, bf16[1,6144,512]{2,1,0:T(8,128)(2,1)}, u32[]{:S(2)}) copy-start(bf16[1,6144,512]{2,1,0:T(8,128)(2,1)} %param.10) | copy-start | bytes 18874372
  61.1 41.8 %collective-permute-start.10 = (bf16[4,512,384]{2,1,0:T(8,128)(2,1)}, bf16[4,512,384]{2,1,0:T(8,128)(2,1)S(1)}, u32[]{:S(2)}, u32[]{:S(2)}) collective-permute-start(bf16[4,512,384]{2,1,0:T(8,128)(2,1)} %collective-permute-done.9.refs_0_), channel_id=1, source_target_pairs={{0,1},{1,0},{2,3},{3,2},{4,5},{5,4},{6,7},{7,6},{8,9},{9,8},{10,11... | collective-permute-start | bytes 4718600 | tf_op jit(solution)/shard_map/ppermute | solution.py:34
  68.3 38.5 %collective-permute-start.8 = (bf16[4,512,384]{2,1,0:T(8,128)(2,1)S(1)}, bf16[4,512,384]{2,1,0:T(8,128)(2,1)S(1)}, u32[]{:S(2)}, u32[]{:S(2)}) collective-permute-start(bf16[4,512,384]{2,1,0:T(8,128)(2,1)S(1)} %collective-permute-done.7.refs_0_), channel_id=1, source_target_pairs={{0,1},{1,0},{2,3},{3,2},{4,5},{5,4},{6,7},{7,6},{8,9},{9,8},{10,11... | collective-permute-start | bytes 4718600 | tf_op jit(solution)/shard_map/ppermute | solution.py:34
  74.6 8.1 %slice-start.2 = ((s8[6291456]{0:T(1024)(128)(4,1)}), s8[4194304]{0:T(1024)(128)(4,1)S(1)}, s32[]{:S(2)}) async-start(s8[6291456]{0:T(1024)(128)(4,1)} %bitcast.161), calls=%async_computation.2 | async-start | bytes 8388608
  79.4 3.3 %slice-start.3 = ((s8[6291456]{0:T(1024)(128)(4,1)}), s8[2097152]{0:T(1024)(128)(4,1)S(1)}, s32[]{:S(2)}) async-start(s8[6291456]{0:T(1024)(128)(4,1)} %bitcast.161), calls=%async_computation.3 | async-start | bytes 4194304
  85.5 24.5 %collective-permute-start.15 = (bf16[4,512,384]{2,1,0:T(8,128)(2,1)}, bf16[4,512,384]{2,1,0:T(8,128)(2,1)S(1)}, u32[]{:S(2)}, u32[]{:S(2)}) collective-permute-start(bf16[4,512,384]{2,1,0:T(8,128)(2,1)} %down.10), channel_id=1, source_target_pairs={{0,1},{1,0},{2,3},{3,2},{4,5},{5,4},{6,7},{7,6},{8,9},{9,8},{10,11... | collective-permute-start | bytes 4718600 | tf_op jit(solution)/shard_map/ppermute | solution.py:34
  88.5 24.8 %collective-permute-start.17 = (bf16[4,512,384]{2,1,0:T(8,128)(2,1)}, bf16[4,512,384]{2,1,0:T(8,128)(2,1)S(1)}, u32[]{:S(2)}, u32[]{:S(2)}) collective-permute-start(bf16[4,512,384]{2,1,0:T(8,128)(2,1)} %down.12), channel_id=1, source_target_pairs={{0,1},{1,0},{2,3},{3,2},{4,5},{5,4},{6,7},{7,6},{8,9},{9,8},{10,11... | collective-permute-start | bytes 4718600 | tf_op jit(solution)/shard_map/ppermute | solution.py:34
  89.0 6.3 %slice-start = ((s8[6291456]{0:T(1024)(128)(4,1)}), s8[4194304]{0:T(1024)(128)(4,1)S(1)}, s32[]{:S(2)}) async-start(s8[6291456]{0:T(1024)(128)(4,1)} %bitcast.111), calls=%async_computation | async-start | bytes 8388608
  91.8 25.7 %collective-permute-start.19 = (bf16[4,512,384]{2,1,0:T(8,128)(2,1)}, bf16[4,512,384]{2,1,0:T(8,128)(2,1)S(1)}, u32[]{:S(2)}, u32[]{:S(2)}) collective-permute-start(bf16[4,512,384]{2,1,0:T(8,128)(2,1)} %down.14), channel_id=1, source_target_pairs={{0,1},{1,0},{2,3},{3,2},{4,5},{5,4},{6,7},{7,6},{8,9},{9,8},{10,11... | collective-permute-start | bytes 4718600 | tf_op jit(solution)/shard_map/ppermute | solution.py:34
  92.0 3.2 %slice-start.1 = ((s8[6291456]{0:T(1024)(128)(4,1)}), s8[2097152]{0:T(1024)(128)(4,1)S(1)}, s32[]{:S(2)}) async-start(s8[6291456]{0:T(1024)(128)(4,1)} %bitcast.111), calls=%async_computation.1 | async-start | bytes 4194304
  102.9 18.4 %collective-permute-start.14 = (bf16[4,512,384]{2,1,0:T(8,128)(2,1)}, bf16[4,512,384]{2,1,0:T(8,128)(2,1)}, u32[]{:S(2)}, u32[]{:S(2)}) collective-permute-start(bf16[4,512,384]{2,1,0:T(8,128)(2,1)} %down.8), channel_id=1, source_target_pairs={{0,1},{1,0},{2,3},{3,2},{4,5},{5,4},{6,7},{7,6},{8,9},{9,8},{10,11... | collective-permute-start | bytes 4718600 | tf_op jit(solution)/shard_map/ppermute | solution.py:34
  112.0 20.9 %collective-permute-start.16 = (bf16[4,512,384]{2,1,0:T(8,128)(2,1)S(1)}, bf16[4,512,384]{2,1,0:T(8,128)(2,1)}, u32[]{:S(2)}, u32[]{:S(2)}) collective-permute-start(bf16[4,512,384]{2,1,0:T(8,128)(2,1)S(1)} %down.11), channel_id=1, source_target_pairs={{0,8},{1,3},{2,10},{3,5},{4,12},{5,7},{6,14},{7,1},{8,16},{9,11},{... | collective-permute-start | bytes 4718600 | tf_op jit(solution)/shard_map/ppermute | solution.py:26
  116.1 36.1 %collective-permute-start.18 = (bf16[4,512,384]{2,1,0:T(8,128)(2,1)}, bf16[4,512,384]{2,1,0:T(8,128)(2,1)}, u32[]{:S(2)}, u32[]{:S(2)}) collective-permute-start(bf16[4,512,384]{2,1,0:T(8,128)(2,1)} %down.13), channel_id=1, source_target_pairs={{0,24},{1,7},{2,26},{3,1},{4,28},{5,3},{6,30},{7,5},{8,0},{9,15},{... | collective-permute-start | bytes 4718600 | tf_op jit(solution)/shard_map/ppermute | solution.py:26
  120.4 31.8 %collective-permute-start.20 = (bf16[4,512,384]{2,1,0:T(8,128)(2,1)}, bf16[4,512,384]{2,1,0:T(8,128)(2,1)}, u32[]{:S(2)}, u32[]{:S(2)}) collective-permute-start(bf16[4,512,384]{2,1,0:T(8,128)(2,1)} %down.15), channel_id=1, source_target_pairs={{0,16},{1,5},{2,18},{3,7},{4,20},{5,1},{6,22},{7,3},{8,24},{9,13},... | collective-permute-start | bytes 4718600 | tf_op jit(solution)/shard_map/ppermute | solution.py:26
  121.3 2.8 %copy-start.2 = (bf16[1,512,6144]{2,1,0:T(8,128)(2,1)S(1)}, bf16[1,512,6144]{2,1,0:T(8,128)(2,1)}, u32[]{:S(2)}) copy-start(bf16[1,512,6144]{2,1,0:T(8,128)(2,1)} %param.11) | copy-start | bytes 18874372
  155.2 12.3 %copy-start.3 = (s32[2,128,2]{1,2,0:T(2,128)S(1)}, s32[2,128,2]{1,2,0:T(2,128)}, u32[]{:S(2)}) copy-start(s32[2,128,2]{1,2,0:T(2,128)} %param.7) | copy-start | bytes 6148
  155.3 12.3 %copy-start.4 = (f32[2,128]{1,0:T(2,128)S(1)}, f32[2,128]{1,0:T(2,128)}, u32[]{:S(2)}) copy-start(f32[2,128]{1,0:T(2,128)} %param.8) | copy-start | bytes 3076
  155.4 12.2 %collective-permute-start.21 = (bf16[512,384]{1,0:T(8,128)(2,1)S(1)}, bf16[512,384]{1,0:T(8,128)(2,1)S(1)}, u32[]{:S(2)}, u32[]{:S(2)}) collective-permute-start(bf16[512,384]{1,0:T(8,128)(2,1)S(1)} %get-tuple-element.31), channel_id=1, source_target_pairs={{0,2},{1,9},{2,4},{3,11},{4,6},{5,13},{6,0},{7,15},{8,10},{9,17},{... | collective-permute-start | bytes 1179656 | tf_op jit(solution)/shard_map/ppermute | solution.py:30
  162.9 12.0 %collective-permute-start.23 = (bf16[512,384]{1,0:T(8,128)(2,1)S(1)}, bf16[512,384]{1,0:T(8,128)(2,1)S(1)}, u32[]{:S(2)}, u32[]{:S(2)}) collective-permute-start(bf16[512,384]{1,0:T(8,128)(2,1)S(1)} %get-tuple-element.32), channel_id=1, source_target_pairs={{0,4},{1,17},{2,6},{3,19},{4,0},{5,21},{6,2},{7,23},{8,12},{9,25},... | collective-permute-start | bytes 1179656 | tf_op jit(solution)/shard_map/ppermute | solution.py:30
  165.6 9.3 %collective-permute-start.22 = (bf16[512,384]{1,0:T(8,128)(2,1)S(1)}, bf16[512,384]{1,0:T(8,128)(2,1)S(1)}, u32[]{:S(2)}, u32[]{:S(2)}) collective-permute-start(bf16[512,384]{1,0:T(8,128)(2,1)S(1)} %get-tuple-element.33), channel_id=1, source_target_pairs={{0,6},{1,25},{2,0},{3,27},{4,2},{5,29},{6,4},{7,31},{8,14},{9,1},{... | collective-permute-start | bytes 1179656 | tf_op jit(solution)/shard_map/ppermute | solution.py:30
  175.1 4.1 %collective-permute-start.24 = (bf16[128,384]{1,0:T(8,128)(2,1)S(1)}, bf16[128,384]{1,0:T(8,128)(2,1)S(1)}, u32[]{:S(2)}, u32[]{:S(2)}) collective-permute-start(bf16[128,384]{1,0:T(8,128)(2,1)S(1)} %get-tuple-element.34), channel_id=1, source_target_pairs={{0,96},{32,0},{64,32},{96,64},{1,97},{33,1},{65,33},{97,65},{2,98}... | collective-permute-start | bytes 294920 | tf_op jit(solution)/shard_map/ppermute | solution.py:38
  175.5 4.7 %collective-permute-start.26 = (bf16[128,384]{1,0:T(8,128)(2,1)S(1)}, bf16[128,384]{1,0:T(8,128)(2,1)S(1)}, u32[]{:S(2)}, u32[]{:S(2)}) collective-permute-start(bf16[128,384]{1,0:T(8,128)(2,1)S(1)} %get-tuple-element.35), channel_id=1, source_target_pairs={{0,32},{32,64},{64,96},{96,0},{1,33},{33,65},{65,97},{97,1},{2,34}... | collective-permute-start | bytes 294920 | tf_op jit(solution)/shard_map/ppermute | solution.py:38
  176.7 5.1 %collective-permute-start.25 = (bf16[128,384]{1,0:T(8,128)(2,1)S(1)}, bf16[128,384]{1,0:T(8,128)(2,1)S(1)}, u32[]{:S(2)}, u32[]{:S(2)}) collective-permute-start(bf16[128,384]{1,0:T(8,128)(2,1)S(1)} %get-tuple-element.36), channel_id=1, source_target_pairs={{0,64},{32,96},{64,0},{96,32},{1,65},{33,97},{65,1},{97,33},{2,66}... | collective-permute-start | bytes 294920 | tf_op jit(solution)/shard_map/ppermute | solution.py:38
  182.0 3.3 %collective-permute-start.27 = (bf16[128,192]{1,0:T(8,128)(2,1)S(1)}, bf16[128,192]{1,0:T(8,128)(2,1)S(1)}, u32[]{:S(2)}, u32[]{:S(2)}) collective-permute-start(bf16[128,192]{1,0:T(8,128)(2,1)S(1)} %broadcast_select_fusion.1), channel_id=1, source_target_pairs={{0,1},{1,0},{2,3},{3,2},{4,5},{5,4},{6,7},{7,6},{8,9},{9,8},{10,11... | collective-permute-start | bytes 147464 | tf_op jit(solution)/shard_map/ppermute | solution.py:34

commit v2 on v1

v2 whole, which is shorter than its diff:
```python
import jax
import jax.numpy as jnp
from jax import lax
from jax.experimental import pallas as pl
from jax.experimental.pallas import tpu as pltpu
from jax.sharding import PartitionSpec as P

SIDE = 4
BF = jnp.bfloat16
F32 = jnp.float32


def blk_perm(bulk, shift):
    pairs = []
    for z in range(SIDE):
        for x in range(SIDE):
            for c in range(2):
                along_z = (c == 0) == bulk
                z2 = (z + shift) % SIDE if along_z else z
                x2 = x if along_z else (x + shift) % SIDE
                pairs.append(((z * SIDE + x) * 2 + c, (z2 * SIDE + x2) * 2 + c))
    return pairs


def move_bulk(v, shift):
    return lax.ppermute(v, "blk", blk_perm(True, shift))


def move_small(v, shift):
    return lax.ppermute(v, "blk", blk_perm(False, shift))


def move_core(v):
    return lax.ppermute(v, "blk", [(i, i ^ 1) for i in range(2 * SIDE * SIDE)])


def move_expert(v, shift):
    return lax.ppermute(v, "expert", [(i, (i + shift) % SIDE) for i in range(SIDE)])


def feature_block(place, sign, other, bulk_shift, small_shift):
    z, x, core = place >> 3, (place >> 1) & (SIDE - 1), (place & 1) ^ other
    along_z = jnp.where(core == 0, sign * bulk_shift, sign * small_shift)
    along_x = jnp.where(core == 0, sign * small_shift, sign * bulk_shift)
    return ((z + along_z) & (SIDE - 1)) * SIDE + ((x + along_x) & (SIDE - 1))


def after(value, *others):
    return lax.optimization_barrier((value, *others))[0]


VMEM = pl.BlockSpec(memory_space=pltpu.VMEM)
SMEM = pl.BlockSpec(memory_space=pltpu.SMEM)
ANY = pl.BlockSpec(memory_space=pl.ANY)


def in_vmem(values):
    return [pltpu.with_memory_space_constraint(v, pltpu.VMEM) for v in values]


def up_call(pieces, place, blocks, gate_w, up_w, carry, final, behind):
    n = len(pieces)
    counts = [p.shape[0] for p in pieces]
    total = sum(counts)
    rows, width = pieces[0].shape[1:]
    cols = gate_w.shape[1]
    tile = 256

    def kernel(place_ref, *refs):
        xs = refs[:n]
        gate_ref, up_ref = refs[n : n + 2]
        rest = refs[n + 2 :]
        carried = rest[:2] if carry is not None else None
        outs = rest[(2 if carry is not None else 0) + len(behind) :]
        outs[-1][...] = jnp.zeros((8, 128), F32)
        x = jnp.concatenate([r[k] for r, m in zip(xs, counts) for k in range(m)], axis=1)
        at = [pl.multiple_of(feature_block(place_ref[0], *b) * width, width) for b in blocks]
        for j in range(cols // tile):
            cs = slice(j * tile, (j + 1) * tile)
            g = jnp.dot(x, jnp.concatenate([gate_ref[pl.ds(s, width), cs] for s in at], axis=0), preferred_element_type=F32)
            u = jnp.dot(x, jnp.concatenate([up_ref[pl.ds(s, width), cs] for s in at], axis=0), preferred_element_type=F32)
            if carried is not None:
                g = g + carried[0][:, cs]
                u = u + carried[1][:, cs]
            if final:
                outs[0][:, cs] = (g / (1.0 + jnp.exp(-g)) * u).astype(BF)
            else:
                outs[0][:, cs] = g
                outs[1][:, cs] = u

    args = in_vmem([*pieces, gate_w, up_w, *(carry or [])])
    if final:
        out_shape = [pltpu.VMEM((rows, cols), BF)]
    else:
        out_shape = [pltpu.VMEM((rows, cols), F32)] * 2
    out_shape.append(pltpu.VMEM((8, 128), F32))
    return pl.pallas_call(
        kernel,
        in_specs=[SMEM] + [VMEM] * len(args) + [ANY] * len(behind),
        out_specs=[VMEM] * len(out_shape),
        out_shape=out_shape,
        compiler_params=pltpu.CompilerParams(vmem_limit_bytes=12 << 20),
        cost_estimate=pl.CostEstimate(
            flops=2 * rows * total * width * cols * 2,
            bytes_accessed=total * width * cols * 4 + total * rows * width * 2 + rows * cols * 8,
            transcendentals=0,
        ),
        name="up",
    )(place, *args, *behind)


def down_call(hidden, place, blocks, down_w, adds, splits, dtype, behind):
    rows, depth = hidden.shape
    width = down_w.shape[1] // (SIDE * SIDE)
    n_add = len(adds)
    total = len(blocks)

    def kernel(place_ref, h_ref, w_ref, *rest):
        outs = [(o, k) for o, n in zip(rest[n_add + len(behind) :], splits) for k in range(n)]
        h = h_ref[...]
        for j in range(0, total, 2):
            at = [pl.multiple_of(feature_block(place_ref[0], *b) * width, width) for b in blocks[j : j + 2]]
            w = jnp.concatenate([w_ref[:, pl.ds(s, width)] for s in at], axis=1)
            y = jnp.dot(h, w, preferred_element_type=F32)
            for k in range(2):
                part = y[:, k * width : (k + 1) * width]
                for ref, (_, first) in zip(rest, adds):
                    part = part + ref[j + k + first].astype(F32)
                out, place = outs[j + k]
                out[place] = part.astype(dtype)

    args = in_vmem([hidden, down_w, *[v for v, _ in adds]])
    out_shape = [pltpu.VMEM((n, rows, width), dtype) for n in splits]
    return pl.pallas_call(
        kernel,
        in_specs=[SMEM] + [VMEM] * len(args) + [ANY] * len(behind),
        out_specs=[VMEM] * len(out_shape),
        out_shape=out_shape,
        compiler_params=pltpu.CompilerParams(vmem_limit_bytes=12 << 20),
        cost_estimate=pl.CostEstimate(
            flops=2 * rows * depth * width * total,
            bytes_accessed=total * width * (depth + rows * 2) * 2 + rows * depth * 2,
            transcendentals=0,
        ),
        name="down",
    )(place, *args, *behind)


def load_call(weights, behind):
    n = len(weights)

    def kernel(*refs):
        sem = refs[-1]
        refs[-2][...] = jnp.zeros((8, 128), F32)
        copies = [pltpu.make_async_copy(refs[k], refs[n + len(behind) + k], sem.at[k]) for k in range(n)]
        for copy in copies:
            copy.start()
        for copy in copies:
            copy.wait()

    return pl.pallas_call(
        kernel,
        in_specs=[pl.BlockSpec(memory_space=pltpu.HBM)] * n + [ANY] * len(behind),
        out_specs=[VMEM] * (n + 1),
        out_shape=[pltpu.VMEM(w.shape, w.dtype) for w in weights] + [pltpu.VMEM((8, 128), F32)],
        scratch_shapes=[pltpu.SemaphoreType.DMA((n,))],
        compiler_params=pltpu.CompilerParams(vmem_limit_bytes=1 << 20),
        cost_estimate=pl.CostEstimate(
            flops=0, bytes_accessed=4 * sum(w.size for w in weights), transcendentals=0
        ),
        name="load",
    )(*[pltpu.with_memory_space_constraint(w, pltpu.HBM) for w in weights], *behind)


def gather_call(pieces, out_shapes, places, behind):
    n = len(pieces)

    def kernel(*refs):
        for ref, (k, index) in zip(refs[:n], places):
            refs[n + 1 + k][index] = ref[...]

    return pl.pallas_call(
        kernel,
        in_specs=[VMEM] * n + [ANY],
        out_specs=[VMEM] * len(out_shapes),
        out_shape=[pltpu.VMEM(shape, BF) for shape in out_shapes],
        compiler_params=pltpu.CompilerParams(vmem_limit_bytes=8 << 20),
        cost_estimate=pl.CostEstimate(
            flops=0, bytes_accessed=4 * sum(p.size for p in pieces), transcendentals=0
        ),
        name="gather",
    )(*in_vmem(pieces), behind)


def add_call(total, arrived):
    n = total.shape[0]

    def kernel(total_ref, arrived_ref, *outs):
        for k in range(n):
            outs[k][...] = (total_ref[k] + arrived_ref[k].astype(F32)).astype(BF)

    return pl.pallas_call(
        kernel,
        in_specs=[VMEM] * 2,
        out_specs=[VMEM] * n,
        out_shape=[pltpu.VMEM(total.shape[1:], BF)] * n,
        compiler_params=pltpu.CompilerParams(vmem_limit_bytes=8 << 20),
        cost_estimate=pl.CostEstimate(flops=total.size, bytes_accessed=8 * total.size, transcendentals=0),
        name="add",
    )(*in_vmem([total, arrived]))


def fsum(parts):
    total = parts[0].astype(F32)
    for p in parts[1:]:
        total = total + p.astype(F32)
    return total


def body(tokens, expert_ids, route_share, gate_weight, up_weight, down_weight):
    expert = lax.axis_index("expert")
    place = lax.axis_index("blk")
    where = jnp.reshape(place, (1,))
    tokens, where = lax.optimization_barrier((tokens, where))
    c = place % 2
    gate_w, up_w, down_w = gate_weight[0], up_weight[0], down_weight[0]
    half = tokens.shape[2]
    rows = tokens.shape[1]

    mine = jnp.where(c == 0, tokens[0], tokens[1])
    theirs = jnp.where(c == 0, tokens[1], tokens[0])
    got = move_core(theirs)
    pair = jnp.where(
        c == 0, jnp.concatenate([mine, got], axis=1), jnp.concatenate([got, mine], axis=1)
    )
    two = SIDE // 2
    ids = jnp.where(c == 0, expert_ids[1], expert_ids[0])
    share = jnp.where(c == 0, route_share[1], route_share[0])
    names = (expert + jnp.arange(SIDE, dtype=jnp.int32)) % SIDE
    factors = jnp.where(ids[:, 0] == names[:, None], share, 0.0) + jnp.where(ids[:, 1] == names[:, None], 1.0 - share, 0.0)
    gate_w, up_w, t0 = load_call([gate_w, up_w], [pair, factors])
    (owners,) = gather_call(
        [pair] + [move_expert(pair, d) for d in range(1, SIDE)],
        [(SIDE * rows, 2 * half)],
        [(0, slice(d * rows, (d + 1) * rows)) for d in range(SIDE)],
        t0,
    )
    down_w, t1 = load_call([down_w], [owners])
    line_a, line_b = gather_call(
        [owners] + [move_small(owners, d) for d in range(1, SIDE)],
        [(two, SIDE * rows, 2 * half)] * 2,
        [(d // two, d % two) for d in range(SIDE)],
        t1,
    )
    def at(sign, other, d, blocks=range(SIDE)):
        return [(sign, other, d, k) for k in blocks]

    first, last = range(two), range(two, SIDE)

    def up(pieces, blocks, carry, final=False, behind=()):
        *sums, token = up_call(pieces, where, blocks, gate_w, up_w, carry, final, behind)
        return sums, token

    def down(h, blocks, adds, splits, dtype=BF, behind=()):
        return down_call(h, where, blocks, down_w, adds, splits, dtype, behind)

    right_a, left_b = move_bulk(line_a, 1), move_bulk(line_b, 3)
    right_b, left_a = move_bulk(line_b, 1), move_bulk(line_a, 3)
    far_a, far_b = move_bulk(right_a, 1), move_bulk(left_b, 3)
    other_line = [move_core(line_a), move_core(line_b)]
    other_early = [move_core(right_a), move_core(left_b)]
    own_sum, t0 = up([line_a, line_b], at(-1, 0, 0), None)
    other_sum, t1 = up(other_line, at(-1, 1, 0), None, False, [t0])
    early = [(1, first), (3, last)]
    late = [(1, last), (3, first)]

    def near(other, parts):
        return [b for d, blocks in parts for b in at(-1, other, d, blocks)]

    other_sum, t1 = up(other_early, near(1, early), other_sum)
    right_b, left_a = after(right_b, t1), after(left_a, t1)
    other_late = [move_core(right_b), move_core(left_a)]
    own_sum, t0 = up([right_a, left_b, right_b, left_a], near(0, early + late), own_sum)
    other_sum, t1 = up(other_late, near(1, late), other_sum, False, [t0])
    far_a, far_b = after(far_a, t1), after(far_b, t1)
    other_a, other_b = move_core(far_a), move_core(far_b)
    (h_own,), t0 = up([far_a, far_b], at(-1, 0, 2), own_sum, True)

    sent2 = move_core(down(h_own, at(1, 1, 2), [], [SIDE])[0])
    (h_other,), t1 = up([other_a, other_b], at(-1, 1, 2), other_sum, True)
    m2a, m2b = down(h_other, at(1, 0, 2), [(sent2, 0)], [two, two])
    step_a, step_b = move_bulk(m2a, 1), move_bulk(m2b, 3)
    sent1 = move_core(down(h_own, at(1, 1, 1), [], [SIDE], BF, [m2a])[0])
    sent3 = move_core(down(h_own, at(1, 1, 3), [], [SIDE], BF, [m2a])[0])
    (m1b,) = down(h_other, at(1, 0, 1, last), [(sent1, two)], [two])
    (m3a,) = down(h_other, at(1, 0, 3, first), [(sent3, 0)], [two])
    n1b, n3a = move_bulk(m1b, 1), move_bulk(m3a, 3)
    sent0 = move_core(down(h_own, at(1, 1, 0), [], [SIDE], BF, [m1b, m3a])[0])
    step_a, step_b = after(step_a, m1b, m3a), after(step_b, m1b, m3a)
    (m1a,) = down(h_other, at(1, 0, 1, first), [(sent1, 0), (step_a, 0)], [two])
    (m3b,) = down(h_other, at(1, 0, 3, last), [(sent3, two), (step_b, 0)], [two])
    n1a, n3b = move_bulk(m1a, 1), move_bulk(m3b, 3)
    (m0a,) = down(h_other, at(1, 0, 0, first), [(sent0, 0), (n3a, 0)], [two], F32, [m1a, m3b])
    (m0b,) = down(h_other, at(1, 0, 0, last), [(sent0, two), (n1b, 0)], [two], F32, [m1a, m3b])
    s0, s1 = add_call(m0a, n1a)
    s2, s3 = add_call(m0b, n3b)
    plane = fsum([s0, move_small(s1, 1), move_small(s3, 3), move_small(s2, 2)]).astype(BF)
    plane = plane.reshape(SIDE, rows, 2 * half)

    total = 0.0
    for d in range(SIDE):
        back = plane[d] if d == 0 else move_expert(plane[d], -d)
        total = total + factors[d][:, None] * back.astype(F32)
    total = total.astype(BF)
    low, high = total[:, :half], total[:, half:]
    keep = jnp.where(c == 0, low, high)
    came = move_core(jnp.where(c == 0, high, low))
    return jnp.stack([jnp.where(c == 0, came, keep), jnp.where(c == 0, keep, came)])


def solution(mesh):
    return jax.shard_map(
        body,
        mesh=mesh,
        in_specs=(
            P(None, "expert", "blk"),
            P(None, "expert", None),
            P(None, "expert"),
            P("expert", None, "blk"),
            P("expert", None, "blk"),
            P("expert", "blk", None),
        ),
        out_specs=P(None, "expert", "blk"),
        check_vma=False,
    )
```

time: 188 us -> 147 us (0.78)
  Pallas kernels: 51.7 us -> 33.8 us
  local copies, waits for them, and re-layouts: 10.3 us -> 1.78 us
  starting transfers between devices: 50.5 us -> 42.2 us
  other arithmetic: 5.37 us -> 2.24 us
    pallas_call x16 -> x24, Pallas kernels: 51.7 us -> 33.8 us  [the longest x7 17.2 us: up_call(): pl.pallas_call(kernel, in_specs=[SMEM] + [VMEM] * len(args) + [ANY] * len...]
    ppermute x6, starting transfers between devices: 18.5 us -> 7.28 us  [move_small(): return lax.ppermute(v, 'blk', blk_perm(False, shift))]
    unnamed x20 -> x0, local copies, waits for them, and re-layouts: 8.61 us -> none
    ppermute x6, waiting for transfers between devices: 11.8 us -> 4.75 us  [move_expert(): lax.ppermute(v, 'expert', [(i, (i + shift) % SIDE) for i in range(SIDE)])]
    ppermute x10 -> x14, waiting for transfers between devices: 1.83 us -> 8.46 us  [move_core(): return lax.ppermute(v, 'blk', [(i, i ^ 1) for i in range(2 * SIDE * SIDE)])]
    ppermute x6 -> x12, starting transfers between devices: 7.87 us -> 13.1 us  [move_bulk(): return lax.ppermute(v, 'blk', blk_perm(True, shift))]
    ppermute x10 -> x14, starting transfers between devices: 18.2 us -> 14.2 us  [move_core(): return lax.ppermute(v, 'blk', [(i, i ^ 1) for i in range(2 * SIDE * SIDE)])]
    convert_element_type x2 -> x1, other arithmetic: 3.33 us -> 0.23 us  [body(): fsum([s0, move_small(s1, 1), move_small(s3, 3), move_small(s2, 2)])]
  transfers between devices with their start and end apart: 28 -> 38, of which waited for: 15 -> 23; matrix products, arithmetic and copies ran while one was open for 1% -> 1% of each run, Pallas kernels for 28% -> 19%
where the time goes in v2:
time: 147 us
  waiting for transfers between devices  66.5 us (45%)
  starting transfers between devices  42.2 us (29%)
  Pallas kernels  33.8 us (23%)
  other arithmetic  2.24 us (2%)
  local copies, waits for them, and re-layouts  1.78 us (1%)
    ppermute x12, waiting for transfers between devices, move_bulk(): return lax.ppermute(v, 'blk', blk_perm(True, shift))  40.1 us
    pallas_call x7, Pallas kernels, up_call(): pl.pallas_call(kernel, in_specs=[SMEM] + [VMEM] * len(args) + [ANY] * len...  17.2 us
    ppermute x14, starting transfers between devices, move_core(): return lax.ppermute(v, 'blk', [(i, i ^ 1) for i in range(2 * SIDE * SIDE)])  14.2 us
    ppermute x6, waiting for transfers between devices, move_small(): return lax.ppermute(v, 'blk', blk_perm(False, shift))  13.3 us
    ppermute x12, starting transfers between devices, move_bulk(): return lax.ppermute(v, 'blk', blk_perm(True, shift))  13.1 us
    pallas_call x11, Pallas kernels, down_call(): pl.pallas_call(kernel, in_specs=[SMEM] + [VMEM] * len(args) + [ANY] * len...  8.72 us
    ppermute x14, waiting for transfers between devices, move_core(): return lax.ppermute(v, 'blk', [(i, i ^ 1) for i in range(2 * SIDE * SIDE)])  8.46 us
    ppermute x6, starting transfers between devices, move_expert(): lax.ppermute(v, 'expert', [(i, (i + shift) % SIDE) for i in range(SIDE)])  7.56 us
  transfers between devices with their start and end apart: 38, of which 23 were waited for; matrix products, arithmetic and copies ran while one was open for 1% of the time, Pallas kernels for 19%

profile of v2, /device:TPU:1, one launch (start us, length us, event | category | flops | bytes accessed | tf_op | source)
XLA Modules:
  0.0 146.9 jit_solution(13678599895475875060)
XLA Ops:
  0.0 1.0 copy.7
  1.0 1.5 %collective-permute-start = (bf16[128,192]{1,0:T(8,128)(2,1)S(1)}, bf16[128,192]{1,0:T(8,128)(2,1)S(1)}, u32[]{:S(2)}, u32[]{:S(2)}) collective-permute-start(bf16[128,192]{1,0:T(8,128)(2,1)S(1)} %get-tuple-element.87), channel_id=1, source_target_pairs={{0,1},{1,0},{2,3},{3,2},{4,5},{5,4},{6,7},{7,6},{8,9},{9,8},{10,11... | collective-permute-start | bytes 147464 | tf_op jit(solution)/shard_map/ppermute | solution.py:34
  2.5 0.7 select_bitcast_fusion.4
  3.2 0.8 broadcast_subtract_fusion
  4.1 1.4 collective-permute-start.1
  5.6 2.6 %collective-permute-start.2 = (bf16[128,384]{1,0:T(8,128)(2,1)S(1)}, bf16[128,384]{1,0:T(8,128)(2,1)S(1)}, u32[]{:S(2)}, u32[]{:S(2)}) collective-permute-start(bf16[128,384]{1,0:T(8,128)(2,1)S(1)} %maximum_select_fusion.refs_2_.refs_0_), channel_id=1, source_target_pairs={{0,64},{32,96},{64,0},{96,32},{1,65},{33,97},{65,1},{97,33},{2,66}... | collective-permute-start | bytes 294920 | tf_op jit(solution)/shard_map/ppermute | solution.py:38
  8.2 1.1 collective-permute-start.3
  9.3 4.6 %load.2 = (bf16[6144,512]{1,0:T(8,128)(2,1)S(1)}, bf16[6144,512]{1,0:T(8,128)(2,1)S(1)}, f32[8,128]{1,0:T(8,128)S(1)}) custom-call(bf16[6144,512]{1,0:T(8,128)(2,1)} %bitcast.30, bf16[6144,512]{1,0:T(8,128)(2,1)} %bitcast.31, bf16[128,384]{1,0:T(8,128)(2,1)S(1)} %maximum_select_fusion.refs_2_.refs_0_, f32[4,128]{1,0:T(4,128)S(1)} %select_add_fusion.refs_3_), custom_call_target="tpu_custom_call" | custom-call | bytes 25165824 | tf_op jit(solution)/shard_map/load/pallas_call | solution.py:161
  14.0 1.7 %collective-permute-start.4 = (bf16[512,384]{1,0:T(8,128)(2,1)S(1)}, bf16[512,384]{1,0:T(8,128)(2,1)S(1)}, u32[]{:S(2)}, u32[]{:S(2)}) collective-permute-start(bf16[512,384]{1,0:T(8,128)(2,1)S(1)} %gather.2.refs_1_.refs_0_), channel_id=1, source_target_pairs={{0,2},{1,9},{2,4},{3,11},{4,6},{5,13},{6,0},{7,15},{8,10},{9,17},{... | collective-permute-start | bytes 1179656 | tf_op jit(solution)/shard_map/ppermute | solution.py:30
  15.7 3.3 %collective-permute-start.5 = (bf16[512,384]{1,0:T(8,128)(2,1)S(1)}, bf16[512,384]{1,0:T(8,128)(2,1)S(1)}, u32[]{:S(2)}, u32[]{:S(2)}) collective-permute-start(bf16[512,384]{1,0:T(8,128)(2,1)S(1)} %gather.2.refs_1_.refs_0_), channel_id=1, source_target_pairs={{0,4},{1,17},{2,6},{3,19},{4,0},{5,21},{6,2},{7,23},{8,12},{9,25},... | collective-permute-start | bytes 1179656 | tf_op jit(solution)/shard_map/ppermute | solution.py:30
  19.1 0.7 collective-permute-start.6
  19.8 2.8 %load.3 = (bf16[512,6144]{1,0:T(8,128)(2,1)S(1)}, f32[8,128]{1,0:T(8,128)S(1)}) custom-call(bf16[512,6144]{1,0:T(8,128)(2,1)} %bitcast.29, bf16[512,384]{1,0:T(8,128)(2,1)S(1)} %gather.2.refs_1_.refs_0_), custom_call_target="tpu_custom_call" | custom-call | bytes 12582912 | tf_op jit(solution)/shard_map/load/pallas_call | solution.py:161
  22.6 0.7 collective-permute-done.4.refs_1_
  23.3 5.4 %collective-permute-done.5.refs_2_ = bf16[512,384]{1,0:T(8,128)(2,1)S(1)} collective-permute-done((bf16[512,384]{1,0:T(8,128)(2,1)S(1)}, bf16[512,384]{1,0:T(8,128)(2,1)S(1)}, u32[]{:S(2)}, u32[]{:S(2)}) %collective-permute-start.5) | collective-permute-done | bytes 393248 | tf_op jit(solution)/shard_map/ppermute | solution.py:30
  28.9 1.0 collective-permute-start.7
  29.9 1.8 %collective-permute-start.11 = (bf16[2,512,384]{2,1,0:T(8,128)(2,1)S(1)}, bf16[2,512,384]{2,1,0:T(8,128)(2,1)S(1)}, u32[]{:S(2)}, u32[]{:S(2)}) collective-permute-start(bf16[2,512,384]{2,1,0:T(8,128)(2,1)S(1)} %get-tuple-element.47.refs_1_), channel_id=1, source_target_pairs={{0,24},{1,7},{2,26},{3,1},{4,28},{5,3},{6,30},{7,5},{8,0},{9,15},{... | collective-permute-start | bytes 2359304 | tf_op jit(solution)/shard_map/ppermute | solution.py:26
  31.6 1.9 %collective-permute-start.13 = (bf16[2,512,384]{2,1,0:T(8,128)(2,1)S(1)}, bf16[2,512,384]{2,1,0:T(8,128)(2,1)S(1)}, u32[]{:S(2)}, u32[]{:S(2)}) collective-permute-start(bf16[2,512,384]{2,1,0:T(8,128)(2,1)S(1)} %get-tuple-element.46.refs_0_), channel_id=1, source_target_pairs={{0,1},{1,0},{2,3},{3,2},{4,5},{5,4},{6,7},{7,6},{8,9},{9,8},{10,11... | collective-permute-start | bytes 2359304 | tf_op jit(solution)/shard_map/ppermute | solution.py:34
  33.5 7.8 %collective-permute-done.7.refs_0_ = bf16[2,512,384]{2,1,0:T(8,128)(2,1)S(1)} collective-permute-done((bf16[2,512,384]{2,1,0:T(8,128)(2,1)S(1)}, bf16[2,512,384]{2,1,0:T(8,128)(2,1)S(1)}, u32[]{:S(2)}, u32[]{:S(2)}) %collective-permute-start.7) | collective-permute-done | bytes 786464 | tf_op jit(solution)/shard_map/ppermute | solution.py:26
  41.3 2.1 %collective-permute-start.10 = (bf16[2,512,384]{2,1,0:T(8,128)(2,1)S(1)}, bf16[2,512,384]{2,1,0:T(8,128)(2,1)S(1)}, u32[]{:S(2)}, u32[]{:S(2)}) collective-permute-start(bf16[2,512,384]{2,1,0:T(8,128)(2,1)S(1)} %collective-permute-done.7.refs_0_), channel_id=1, source_target_pairs={{0,1},{1,0},{2,3},{3,2},{4,5},{5,4},{6,7},{7,6},{8,9},{9,8},{10,11... | collective-permute-start | bytes 2359304 | tf_op jit(solution)/shard_map/ppermute | solution.py:34
  43.4 2.3 %collective-permute-start.16 = (bf16[2,512,384]{2,1,0:T(8,128)(2,1)S(1)}, bf16[2,512,384]{2,1,0:T(8,128)(2,1)S(1)}, u32[]{:S(2)}, u32[]{:S(2)}) collective-permute-start(bf16[2,512,384]{2,1,0:T(8,128)(2,1)S(1)} %get-tuple-element.46.refs_0_), channel_id=1, source_target_pairs={{0,24},{1,7},{2,26},{3,1},{4,28},{5,3},{6,30},{7,5},{8,0},{9,15},{... | collective-permute-start | bytes 2359304 | tf_op jit(solution)/shard_map/ppermute | solution.py:26
  45.7 1.8 %up.7 = (f32[512,512]{1,0:T(8,128)S(1)}, f32[512,512]{1,0:T(8,128)S(1)}, f32[8,128]{1,0:T(8,128)S(1)}) custom-call(s32[1]{0:T(128)} %bitcast.5.place_ref, bf16[2,512,384]{2,1,0:T(8,128)(2,1)S(1)} %get-tuple-element.46.refs_0_, bf16[2,512,384]{2,1,0:T(8,128)(2,1)S(1)} %get-tuple-element.47.refs_1_, bf16[6144,512]{1,0:T(8,128)(2,1)S(1)} %get-tuple-element.48.refs_2_.refs_4_, ...), custom_call_target="tpu_custom_call" | custom-call | flops 1610612736 | bytes 6815744 | tf_op jit(solution)/shard_map/up/pallas_call | solution.py:97
  47.5 2.3 %up.8 = (f32[512,512]{1,0:T(8,128)S(1)}, f32[512,512]{1,0:T(8,128)S(1)}, f32[8,128]{1,0:T(8,128)}) custom-call(s32[1]{0:T(128)} %bitcast.5.place_ref, bf16[2,512,384]{2,1,0:T(8,128)(2,1)S(1)} %collective-permute-done.13.refs_0_, bf16[2,512,384]{2,1,0:T(8,128)(2,1)S(1)} %collective-permute-done.14.refs_1_, ...), custom_call_target="tpu_custom_call" | custom-call | flops 1610612736 | bytes 6815744 | tf_op jit(solution)/shard_map/up/pallas_call | solution.py:97
  49.8 2.3 %up.9 = (f32[512,512]{1,0:T(8,128)S(1)}, f32[512,512]{1,0:T(8,128)S(1)}, f32[8,128]{1,0:T(8,128)}) custom-call(s32[1]{0:T(128)} %bitcast.5.place_ref, bf16[2,512,384]{2,1,0:T(8,128)(2,1)S(1)} %collective-permute-done.10.refs_0_, bf16[2,512,384]{2,1,0:T(8,128)(2,1)S(1)} %collective-permute-done.12.refs_1_, ...), custom_call_target="tpu_custom_call" | custom-call | flops 1610612736 | bytes 6815744 | tf_op jit(solution)/shard_map/up/pallas_call | solution.py:97
  52.1 2.5 %collective-permute-done.16.refs_3_ = bf16[2,512,384]{2,1,0:T(8,128)(2,1)S(1)} collective-permute-done((bf16[2,512,384]{2,1,0:T(8,128)(2,1)S(1)}, bf16[2,512,384]{2,1,0:T(8,128)(2,1)S(1)}, u32[]{:S(2)}, u32[]{:S(2)}) %collective-permute-start.16) | collective-permute-done | bytes 786464 | tf_op jit(solution)/shard_map/ppermute | solution.py:26
  54.7 3.3 %collective-permute-done.9.refs_2_ = bf16[2,512,384]{2,1,0:T(8,128)(2,1)S(1)} collective-permute-done((bf16[2,512,384]{2,1,0:T(8,128)(2,1)S(1)}, bf16[2,512,384]{2,1,0:T(8,128)(2,1)S(1)}, u32[]{:S(2)}, u32[]{:S(2)}) %collective-permute-start.9) | collective-permute-done | bytes 786464 | tf_op jit(solution)/shard_map/ppermute | solution.py:26
  58.0 1.9 %collective-permute-start.17 = (bf16[2,512,384]{2,1,0:T(8,128)(2,1)S(1)}, bf16[2,512,384]{2,1,0:T(8,128)(2,1)S(1)}, u32[]{:S(2)}, u32[]{:S(2)}) collective-permute-start(bf16[2,512,384]{2,1,0:T(8,128)(2,1)S(1)} %collective-permute-done.16.refs_3_), channel_id=1, source_target_pairs={{0,1},{1,0},{2,3},{3,2},{4,5},{5,4},{6,7},{7,6},{8,9},{9,8},{10,11... | collective-permute-start | bytes 2359304 | tf_op jit(solution)/shard_map/ppermute | solution.py:34
  59.9 2.3 %collective-permute-start.19 = (bf16[2,512,384]{2,1,0:T(8,128)(2,1)S(1)}, bf16[2,512,384]{2,1,0:T(8,128)(2,1)S(1)}, u32[]{:S(2)}, u32[]{:S(2)}) collective-permute-start(bf16[2,512,384]{2,1,0:T(8,128)(2,1)S(1)} %collective-permute-done.11.refs_1_), channel_id=1, source_target_pairs={{0,24},{1,7},{2,26},{3,1},{4,28},{5,3},{6,30},{7,5},{8,0},{9,15},{... | collective-permute-start | bytes 2359304 | tf_op jit(solution)/shard_map/ppermute | solution.py:26
  62.2 3.5 %up.10 = (f32[512,512]{1,0:T(8,128)S(1)}, f32[512,512]{1,0:T(8,128)S(1)}, f32[8,128]{1,0:T(8,128)S(1)}) custom-call(s32[1]{0:T(128)} %bitcast.5.place_ref, bf16[2,512,384]{2,1,0:T(8,128)(2,1)S(1)} %collective-permute-done.7.refs_0_, bf16[2,512,384]{2,1,0:T(8,128)(2,1)S(1)} %collective-permute-done.11.refs_1_, ...), custom_call_target="tpu_custom_call" | custom-call | flops 3221225472 | bytes 11534336 | tf_op jit(solution)/shard_map/up/pallas_call | solution.py:97
  65.7 2.3 %up.11 = (f32[512,512]{1,0:T(8,128)S(1)}, f32[512,512]{1,0:T(8,128)S(1)}, f32[8,128]{1,0:T(8,128)}) custom-call(s32[1]{0:T(128)} %bitcast.5.place_ref, bf16[2,512,384]{2,1,0:T(8,128)(2,1)S(1)} %collective-permute-done.15.refs_0_, bf16[2,512,384]{2,1,0:T(8,128)(2,1)S(1)} %collective-permute-done.17.refs_1_, ...), custom_call_target="tpu_custom_call" | custom-call | flops 1610612736 | bytes 6815744 | tf_op jit(solution)/shard_map/up/pallas_call | solution.py:97
  68.0 3.2 %collective-permute-done.19.refs_1_ = bf16[2,512,384]{2,1,0:T(8,128)(2,1)S(1)} collective-permute-done((bf16[2,512,384]{2,1,0:T(8,128)(2,1)S(1)}, bf16[2,512,384]{2,1,0:T(8,128)(2,1)S(1)}, u32[]{:S(2)}, u32[]{:S(2)}) %collective-permute-start.19) | collective-permute-done | bytes 786464 | tf_op jit(solution)/shard_map/ppermute | solution.py:26
  71.2 3.1 %collective-permute-done.8.refs_0_ = bf16[2,512,384]{2,1,0:T(8,128)(2,1)S(1)} collective-permute-done((bf16[2,512,384]{2,1,0:T(8,128)(2,1)S(1)}, bf16[2,512,384]{2,1,0:T(8,128)(2,1)S(1)}, u32[]{:S(2)}, u32[]{:S(2)}) %collective-permute-start.8) | collective-permute-done | bytes 786464 | tf_op jit(solution)/shard_map/ppermute | solution.py:26
  74.3 2.4 %up.13 = (bf16[512,512]{1,0:T(8,128)(2,1)S(1)}, f32[8,128]{1,0:T(8,128)}) custom-call(s32[1]{0:T(128)} %bitcast.5.place_ref, bf16[2,512,384]{2,1,0:T(8,128)(2,1)S(1)} %collective-permute-done.8.refs_0_, bf16[2,512,384]{2,1,0:T(8,128)(2,1)S(1)} %collective-permute-done.19.refs_1_, bf16[6144,512]{1,0:T(8,128)(2,1)S(1)} %get-tuple-element.48.refs_2_.refs_4_, ...), custom_call_target="tpu_custom_call" | custom-call | flops 1610612736 | bytes 6815744 | tf_op jit(solution)/shard_map/up/pallas_call | solution.py:97
  76.8 1.0 down.11
  78.8 3.7 %collective-permute-done.20.refs_1_ = bf16[2,512,384]{2,1,0:T(8,128)(2,1)S(1)} collective-permute-done((bf16[2,512,384]{2,1,0:T(8,128)(2,1)S(1)}, bf16[2,512,384]{2,1,0:T(8,128)(2,1)S(1)}, u32[]{:S(2)}, u32[]{:S(2)}) %collective-permute-start.20) | collective-permute-done | bytes 786464 | tf_op jit(solution)/shard_map/ppermute | solution.py:34
  82.4 1.1 collective-permute-done.18.refs_0_
  83.5 2.5 %up.12 = (bf16[512,512]{1,0:T(8,128)(2,1)S(1)}, f32[8,128]{1,0:T(8,128)}) custom-call(s32[1]{0:T(128)} %bitcast.5.place_ref, bf16[2,512,384]{2,1,0:T(8,128)(2,1)S(1)} %collective-permute-done.18.refs_0_, bf16[2,512,384]{2,1,0:T(8,128)(2,1)S(1)} %collective-permute-done.20.refs_1_, bf16[6144,512]{1,0:T(8,128)(2,1)S(1)} %get-tuple-element.48.refs_2_.refs_4_, ...), custom_call_target="tpu_custom_call" | custom-call | flops 1610612736 | bytes 6815744 | tf_op jit(solution)/shard_map/up/pallas_call | solution.py:97
  86.0 1.0 down.12
  87.0 1.0 down.15
  88.5 1.0 down.13
  89.7 0.7 collective-permute-start.26
  90.4 1.1 collective-permute-done.23.rest_0_
  92.1 1.7 %collective-permute-done.22.rest_0_ = bf16[4,512,384]{2,1,0:T(8,128)(2,1)S(1)} collective-permute-done((bf16[4,512,384]{2,1,0:T(8,128)(2,1)S(1)}, bf16[4,512,384]{2,1,0:T(8,128)(2,1)S(1)}, u32[]{:S(2)}, u32[]{:S(2)}) %collective-permute-start.22) | collective-permute-done | bytes 1572896 | tf_op jit(solution)/shard_map/ppermute | solution.py:34
  94.4 1.0 down.17
  95.9 1.2 collective-permute-start.27
  97.0 0.7 collective-permute-start.25
  97.7 0.8 collective-permute-start.30
  98.5 3.8 %collective-permute-done.26.rest_1_ = bf16[2,512,384]{2,1,0:T(8,128)(2,1)S(1)} collective-permute-done((bf16[2,512,384]{2,1,0:T(8,128)(2,1)S(1)}, bf16[2,512,384]{2,1,0:T(8,128)(2,1)S(1)}, u32[]{:S(2)}, u32[]{:S(2)}) %collective-permute-start.26) | collective-permute-done | bytes 786464 | tf_op jit(solution)/shard_map/ppermute | solution.py:26
  103.0 4.0 %collective-permute-done.27.rest_1_ = bf16[2,512,384]{2,1,0:T(8,128)(2,1)S(1)} collective-permute-done((bf16[2,512,384]{2,1,0:T(8,128)(2,1)S(1)}, bf16[2,512,384]{2,1,0:T(8,128)(2,1)S(1)}, u32[]{:S(2)}, u32[]{:S(2)}) %collective-permute-start.27) | collective-permute-done | bytes 786464 | tf_op jit(solution)/shard_map/ppermute | solution.py:26
  107.7 2.4 %collective-permute-start.31 = (bf16[2,512,384]{2,1,0:T(8,128)(2,1)S(1)}, bf16[2,512,384]{2,1,0:T(8,128)(2,1)S(1)}, u32[]{:S(2)}, u32[]{:S(2)}) collective-permute-start(bf16[2,512,384]{2,1,0:T(8,128)(2,1)S(1)} %down.19.rest_3_), channel_id=1, source_target_pairs={{0,24},{1,7},{2,26},{3,1},{4,28},{5,3},{6,30},{7,5},{8,0},{9,15},{... | collective-permute-start | bytes 2359304 | tf_op jit(solution)/shard_map/ppermute | solution.py:26
  110.1 5.4 %collective-permute-done.25.rest_1_ = bf16[2,512,384]{2,1,0:T(8,128)(2,1)S(1)} collective-permute-done((bf16[2,512,384]{2,1,0:T(8,128)(2,1)S(1)}, bf16[2,512,384]{2,1,0:T(8,128)(2,1)S(1)}, u32[]{:S(2)}, u32[]{:S(2)}) %collective-permute-start.25) | collective-permute-done | bytes 786464 | tf_op jit(solution)/shard_map/ppermute | solution.py:26
  116.0 3.1 %collective-permute-done.28.arrived_ref = bf16[2,512,384]{2,1,0:T(8,128)(2,1)S(1)} collective-permute-done((bf16[2,512,384]{2,1,0:T(8,128)(2,1)S(1)}, bf16[2,512,384]{2,1,0:T(8,128)(2,1)S(1)}, u32[]{:S(2)}, u32[]{:S(2)}) %collective-permute-start.28) | collective-permute-done | bytes 786464 | tf_op jit(solution)/shard_map/ppermute | solution.py:26
  120.0 3.9 %collective-permute-done.31.arrived_ref = bf16[2,512,384]{2,1,0:T(8,128)(2,1)S(1)} collective-permute-done((bf16[2,512,384]{2,1,0:T(8,128)(2,1)S(1)}, bf16[2,512,384]{2,1,0:T(8,128)(2,1)S(1)}, u32[]{:S(2)}, u32[]{:S(2)}) %collective-permute-start.31) | collective-permute-done | bytes 786464 | tf_op jit(solution)/shard_map/ppermute | solution.py:26
  124.1 1.4 collective-permute-start.33
  125.5 1.9 %collective-permute-done.29 = bf16[512,384]{1,0:T(8,128)(2,1)S(1)} collective-permute-done((bf16[512,384]{1,0:T(8,128)(2,1)S(1)}, bf16[512,384]{1,0:T(8,128)(2,1)S(1)}, u32[]{:S(2)}, u32[]{:S(2)}) %collective-permute-start.29) | collective-permute-done | bytes 393248 | tf_op jit(solution)/shard_map/ppermute | solution.py:30
  127.5 3.6 %collective-permute-done.32 = bf16[512,384]{1,0:T(8,128)(2,1)S(1)} collective-permute-done((bf16[512,384]{1,0:T(8,128)(2,1)S(1)}, bf16[512,384]{1,0:T(8,128)(2,1)S(1)}, u32[]{:S(2)}, u32[]{:S(2)}) %collective-permute-start.32) | collective-permute-done | bytes 393248 | tf_op jit(solution)/shard_map/ppermute | solution.py:30
  131.0 1.6 %collective-permute-done.33 = bf16[512,384]{1,0:T(8,128)(2,1)S(1)} collective-permute-done((bf16[512,384]{1,0:T(8,128)(2,1)S(1)}, bf16[512,384]{1,0:T(8,128)(2,1)S(1)}, u32[]{:S(2)}, u32[]{:S(2)}) %collective-permute-start.33) | collective-permute-done | bytes 393248 | tf_op jit(solution)/shard_map/ppermute | solution.py:30
  132.9 1.1 collective-permute-start.34
  134.0 1.1 collective-permute-start.35
  135.3 1.1 collective-permute-done.34
  136.4 2.6 %collective-permute-done.35 = bf16[128,384]{1,0:T(8,128)(2,1)S(1)} collective-permute-done((bf16[128,384]{1,0:T(8,128)(2,1)S(1)}, bf16[128,384]{1,0:T(8,128)(2,1)S(1)}, u32[]{:S(2)}, u32[]{:S(2)}) %collective-permute-start.35) | collective-permute-done | bytes 98336 | tf_op jit(solution)/shard_map/ppermute | solution.py:38
  139.0 1.0 collective-permute-done.36
  140.3 4.8 %collective-permute-start.37 = (bf16[128,192]{1,0:T(8,128)(2,1)S(1)}, bf16[128,192]{1,0:T(8,128)(2,1)S(1)}, u32[]{:S(2)}, u32[]{:S(2)}) collective-permute-start(bf16[128,192]{1,0:T(8,128)(2,1)S(1)} %broadcast_select_fusion.1), channel_id=1, source_target_pairs={{0,1},{1,0},{2,3},{3,2},{4,5},{5,4},{6,7},{7,6},{8,9},{9,8},{10,11... | collective-permute-start | bytes 147464 | tf_op jit(solution)/shard_map/ppermute | solution.py:34
  145.1 0.9 collective-permute-done.37
  146.1 0.7 copy.9
  (52 shorter events, 7.5 us)
Async XLA Ops:
  1.0 3.0 %collective-permute-start = (bf16[128,192]{1,0:T(8,128)(2,1)S(1)}, bf16[128,192]{1,0:T(8,128)(2,1)S(1)}, u32[]{:S(2)}, u32[]{:S(2)}) collective-permute-start(bf16[128,192]{1,0:T(8,128)(2,1)S(1)} %get-tuple-element.87), channel_id=1, source_target_pairs={{0,1},{1,0},{2,3},{3,2},{4,5},{5,4},{6,7},{7,6},{8,9},{9,8},{10,11... | collective-permute-start | bytes 147464 | tf_op jit(solution)/shard_map/ppermute | solution.py:34
  4.1 9.8 %collective-permute-start.1 = (bf16[128,384]{1,0:T(8,128)(2,1)S(1)}, bf16[128,384]{1,0:T(8,128)(2,1)S(1)}, u32[]{:S(2)}, u32[]{:S(2)}) collective-permute-start(bf16[128,384]{1,0:T(8,128)(2,1)S(1)} %maximum_select_fusion.refs_2_.refs_0_), channel_id=1, source_target_pairs={{0,32},{32,64},{64,96},{96,0},{1,33},{33,65},{65,97},{97,1},{2,34}... | collective-permute-start | bytes 294920 | tf_op jit(solution)/shard_map/ppermute | solution.py:38
  5.6 8.4 %collective-permute-start.2 = (bf16[128,384]{1,0:T(8,128)(2,1)S(1)}, bf16[128,384]{1,0:T(8,128)(2,1)S(1)}, u32[]{:S(2)}, u32[]{:S(2)}) collective-permute-start(bf16[128,384]{1,0:T(8,128)(2,1)S(1)} %maximum_select_fusion.refs_2_.refs_0_), channel_id=1, source_target_pairs={{0,64},{32,96},{64,0},{96,32},{1,65},{33,97},{65,1},{97,33},{2,66}... | collective-permute-start | bytes 294920 | tf_op jit(solution)/shard_map/ppermute | solution.py:38
  8.2 5.8 %collective-permute-start.3 = (bf16[128,384]{1,0:T(8,128)(2,1)S(1)}, bf16[128,384]{1,0:T(8,128)(2,1)S(1)}, u32[]{:S(2)}, u32[]{:S(2)}) collective-permute-start(bf16[128,384]{1,0:T(8,128)(2,1)S(1)} %maximum_select_fusion.refs_2_.refs_0_), channel_id=1, source_target_pairs={{0,96},{32,0},{64,32},{96,64},{1,97},{33,1},{65,33},{97,65},{2,98}... | collective-permute-start | bytes 294920 | tf_op jit(solution)/shard_map/ppermute | solution.py:38
  14.0 9.3 %collective-permute-start.4 = (bf16[512,384]{1,0:T(8,128)(2,1)S(1)}, bf16[512,384]{1,0:T(8,128)(2,1)S(1)}, u32[]{:S(2)}, u32[]{:S(2)}) collective-permute-start(bf16[512,384]{1,0:T(8,128)(2,1)S(1)} %gather.2.refs_1_.refs_0_), channel_id=1, source_target_pairs={{0,2},{1,9},{2,4},{3,11},{4,6},{5,13},{6,0},{7,15},{8,10},{9,17},{... | collective-permute-start | bytes 1179656 | tf_op jit(solution)/shard_map/ppermute | solution.py:30
  15.7 13.0 %collective-permute-start.5 = (bf16[512,384]{1,0:T(8,128)(2,1)S(1)}, bf16[512,384]{1,0:T(8,128)(2,1)S(1)}, u32[]{:S(2)}, u32[]{:S(2)}) collective-permute-start(bf16[512,384]{1,0:T(8,128)(2,1)S(1)} %gather.2.refs_1_.refs_0_), channel_id=1, source_target_pairs={{0,4},{1,17},{2,6},{3,19},{4,0},{5,21},{6,2},{7,23},{8,12},{9,25},... | collective-permute-start | bytes 1179656 | tf_op jit(solution)/shard_map/ppermute | solution.py:30
  19.1 9.7 %collective-permute-start.6 = (bf16[512,384]{1,0:T(8,128)(2,1)S(1)}, bf16[512,384]{1,0:T(8,128)(2,1)S(1)}, u32[]{:S(2)}, u32[]{:S(2)}) collective-permute-start(bf16[512,384]{1,0:T(8,128)(2,1)S(1)} %gather.2.refs_1_.refs_0_), channel_id=1, source_target_pairs={{0,6},{1,25},{2,0},{3,27},{4,2},{5,29},{6,4},{7,31},{8,14},{9,1},{... | collective-permute-start | bytes 1179656 | tf_op jit(solution)/shard_map/ppermute | solution.py:30
  28.9 12.4 %collective-permute-start.7 = (bf16[2,512,384]{2,1,0:T(8,128)(2,1)S(1)}, bf16[2,512,384]{2,1,0:T(8,128)(2,1)S(1)}, u32[]{:S(2)}, u32[]{:S(2)}) collective-permute-start(bf16[2,512,384]{2,1,0:T(8,128)(2,1)S(1)} %get-tuple-element.46.refs_0_), channel_id=1, source_target_pairs={{0,8},{1,3},{2,10},{3,5},{4,12},{5,7},{6,14},{7,1},{8,16},{9,11},{... | collective-permute-start | bytes 2359304 | tf_op jit(solution)/shard_map/ppermute | solution.py:26
  29.9 13.5 %collective-permute-start.11 = (bf16[2,512,384]{2,1,0:T(8,128)(2,1)S(1)}, bf16[2,512,384]{2,1,0:T(8,128)(2,1)S(1)}, u32[]{:S(2)}, u32[]{:S(2)}) collective-permute-start(bf16[2,512,384]{2,1,0:T(8,128)(2,1)S(1)} %get-tuple-element.47.refs_1_), channel_id=1, source_target_pairs={{0,24},{1,7},{2,26},{3,1},{4,28},{5,3},{6,30},{7,5},{8,0},{9,15},{... | collective-permute-start | bytes 2359304 | tf_op jit(solution)/shard_map/ppermute | solution.py:26
  31.6 14.0 %collective-permute-start.13 = (bf16[2,512,384]{2,1,0:T(8,128)(2,1)S(1)}, bf16[2,512,384]{2,1,0:T(8,128)(2,1)S(1)}, u32[]{:S(2)}, u32[]{:S(2)}) collective-permute-start(bf16[2,512,384]{2,1,0:T(8,128)(2,1)S(1)} %get-tuple-element.46.refs_0_), channel_id=1, source_target_pairs={{0,1},{1,0},{2,3},{3,2},{4,5},{5,4},{6,7},{7,6},{8,9},{9,8},{10,11... | collective-permute-start | bytes 2359304 | tf_op jit(solution)/shard_map/ppermute | solution.py:34
  33.5 14.0 %collective-permute-start.14 = (bf16[2,512,384]{2,1,0:T(8,128)(2,1)S(1)}, bf16[2,512,384]{2,1,0:T(8,128)(2,1)S(1)}, u32[]{:S(2)}, u32[]{:S(2)}) collective-permute-start(bf16[2,512,384]{2,1,0:T(8,128)(2,1)S(1)} %get-tuple-element.47.refs_1_), channel_id=1, source_target_pairs={{0,1},{1,0},{2,3},{3,2},{4,5},{5,4},{6,7},{7,6},{8,9},{9,8},{10,11... | collective-permute-start | bytes 2359304 | tf_op jit(solution)/shard_map/ppermute | solution.py:34
  41.3 8.5 %collective-permute-start.10 = (bf16[2,512,384]{2,1,0:T(8,128)(2,1)S(1)}, bf16[2,512,384]{2,1,0:T(8,128)(2,1)S(1)}, u32[]{:S(2)}, u32[]{:S(2)}) collective-permute-start(bf16[2,512,384]{2,1,0:T(8,128)(2,1)S(1)} %collective-permute-done.7.refs_0_), channel_id=1, source_target_pairs={{0,1},{1,0},{2,3},{3,2},{4,5},{5,4},{6,7},{7,6},{8,9},{9,8},{10,11... | collective-permute-start | bytes 2359304 | tf_op jit(solution)/shard_map/ppermute | solution.py:34
  43.4 6.4 %collective-permute-start.12 = (bf16[2,512,384]{2,1,0:T(8,128)(2,1)S(1)}, bf16[2,512,384]{2,1,0:T(8,128)(2,1)S(1)}, u32[]{:S(2)}, u32[]{:S(2)}) collective-permute-start(bf16[2,512,384]{2,1,0:T(8,128)(2,1)S(1)} %collective-permute-done.11.refs_1_), channel_id=1, source_target_pairs={{0,1},{1,0},{2,3},{3,2},{4,5},{5,4},{6,7},{7,6},{8,9},{9,8},{10,11... | collective-permute-start | bytes 2359304 | tf_op jit(solution)/shard_map/ppermute | solution.py:34
  43.4 11.3 %collective-permute-start.16 = (bf16[2,512,384]{2,1,0:T(8,128)(2,1)S(1)}, bf16[2,512,384]{2,1,0:T(8,128)(2,1)S(1)}, u32[]{:S(2)}, u32[]{:S(2)}) collective-permute-start(bf16[2,512,384]{2,1,0:T(8,128)(2,1)S(1)} %get-tuple-element.46.refs_0_), channel_id=1, source_target_pairs={{0,24},{1,7},{2,26},{3,1},{4,28},{5,3},{6,30},{7,5},{8,0},{9,15},{... | collective-permute-start | bytes 2359304 | tf_op jit(solution)/shard_map/ppermute | solution.py:26
  45.6 12.3 %collective-permute-start.9 = (bf16[2,512,384]{2,1,0:T(8,128)(2,1)S(1)}, bf16[2,512,384]{2,1,0:T(8,128)(2,1)S(1)}, u32[]{:S(2)}, u32[]{:S(2)}) collective-permute-start(bf16[2,512,384]{2,1,0:T(8,128)(2,1)S(1)} %get-tuple-element.47.refs_1_), channel_id=1, source_target_pairs={{0,8},{1,3},{2,10},{3,5},{4,12},{5,7},{6,14},{7,1},{8,16},{9,11},{... | collective-permute-start | bytes 2359304 | tf_op jit(solution)/shard_map/ppermute | solution.py:26
  58.0 7.7 %collective-permute-start.17 = (bf16[2,512,384]{2,1,0:T(8,128)(2,1)S(1)}, bf16[2,512,384]{2,1,0:T(8,128)(2,1)S(1)}, u32[]{:S(2)}, u32[]{:S(2)}) collective-permute-start(bf16[2,512,384]{2,1,0:T(8,128)(2,1)S(1)} %collective-permute-done.16.refs_3_), channel_id=1, source_target_pairs={{0,1},{1,0},{2,3},{3,2},{4,5},{5,4},{6,7},{7,6},{8,9},{9,8},{10,11... | collective-permute-start | bytes 2359304 | tf_op jit(solution)/shard_map/ppermute | solution.py:34
  59.9 5.8 %collective-permute-start.15 = (bf16[2,512,384]{2,1,0:T(8,128)(2,1)S(1)}, bf16[2,512,384]{2,1,0:T(8,128)(2,1)S(1)}, u32[]{:S(2)}, u32[]{:S(2)}) collective-permute-start(bf16[2,512,384]{2,1,0:T(8,128)(2,1)S(1)} %collective-permute-done.9.refs_2_), channel_id=1, source_target_pairs={{0,1},{1,0},{2,3},{3,2},{4,5},{5,4},{6,7},{7,6},{8,9},{9,8},{10,11... | collective-permute-start | bytes 2359304 | tf_op jit(solution)/shard_map/ppermute | solution.py:34
  59.9 11.3 %collective-permute-start.19 = (bf16[2,512,384]{2,1,0:T(8,128)(2,1)S(1)}, bf16[2,512,384]{2,1,0:T(8,128)(2,1)S(1)}, u32[]{:S(2)}, u32[]{:S(2)}) collective-permute-start(bf16[2,512,384]{2,1,0:T(8,128)(2,1)S(1)} %collective-permute-done.11.refs_1_), channel_id=1, source_target_pairs={{0,24},{1,7},{2,26},{3,1},{4,28},{5,3},{6,30},{7,5},{8,0},{9,15},{... | collective-permute-start | bytes 2359304 | tf_op jit(solution)/shard_map/ppermute | solution.py:26
  62.2 12.2 %collective-permute-start.8 = (bf16[2,512,384]{2,1,0:T(8,128)(2,1)S(1)}, bf16[2,512,384]{2,1,0:T(8,128)(2,1)S(1)}, u32[]{:S(2)}, u32[]{:S(2)}) collective-permute-start(bf16[2,512,384]{2,1,0:T(8,128)(2,1)S(1)} %collective-permute-done.7.refs_0_), channel_id=1, source_target_pairs={{0,8},{1,3},{2,10},{3,5},{4,12},{5,7},{6,14},{7,1},{8,16},{9,11},{... | collective-permute-start | bytes 2359304 | tf_op jit(solution)/shard_map/ppermute | solution.py:26
  77.8 8.2 %collective-permute-start.21 = (bf16[4,512,384]{2,1,0:T(8,128)(2,1)S(1)}, bf16[4,512,384]{2,1,0:T(8,128)(2,1)S(1)}, u32[]{:S(2)}, u32[]{:S(2)}) collective-permute-start(bf16[4,512,384]{2,1,0:T(8,128)(2,1)S(1)} %down.11), channel_id=1, source_target_pairs={{0,1},{1,0},{2,3},{3,2},{4,5},{5,4},{6,7},{7,6},{8,9},{9,8},{10,11... | collective-permute-start | bytes 4718600 | tf_op jit(solution)/shard_map/ppermute | solution.py:34
  78.2 4.2 %collective-permute-start.20 = (bf16[2,512,384]{2,1,0:T(8,128)(2,1)S(1)}, bf16[2,512,384]{2,1,0:T(8,128)(2,1)S(1)}, u32[]{:S(2)}, u32[]{:S(2)}) collective-permute-start(bf16[2,512,384]{2,1,0:T(8,128)(2,1)S(1)} %collective-permute-done.19.refs_1_), channel_id=1, source_target_pairs={{0,1},{1,0},{2,3},{3,2},{4,5},{5,4},{6,7},{7,6},{8,9},{9,8},{10,11... | collective-permute-start | bytes 2359304 | tf_op jit(solution)/shard_map/ppermute | solution.py:34
  78.4 5.2 %collective-permute-start.18 = (bf16[2,512,384]{2,1,0:T(8,128)(2,1)S(1)}, bf16[2,512,384]{2,1,0:T(8,128)(2,1)S(1)}, u32[]{:S(2)}, u32[]{:S(2)}) collective-permute-start(bf16[2,512,384]{2,1,0:T(8,128)(2,1)S(1)} %collective-permute-done.8.refs_0_), channel_id=1, source_target_pairs={{0,1},{1,0},{2,3},{3,2},{4,5},{5,4},{6,7},{7,6},{8,9},{9,8},{10,11... | collective-permute-start | bytes 2359304 | tf_op jit(solution)/shard_map/ppermute | solution.py:34
  88.1 3.5 %collective-permute-start.23 = (bf16[4,512,384]{2,1,0:T(8,128)(2,1)S(1)}, bf16[4,512,384]{2,1,0:T(8,128)(2,1)S(1)}, u32[]{:S(2)}, u32[]{:S(2)}) collective-permute-start(bf16[4,512,384]{2,1,0:T(8,128)(2,1)S(1)} %down.15), channel_id=1, source_target_pairs={{0,1},{1,0},{2,3},{3,2},{4,5},{5,4},{6,7},{7,6},{8,9},{9,8},{10,11... | collective-permute-start | bytes 4718600 | tf_op jit(solution)/shard_map/ppermute | solution.py:34
  89.5 4.3 %collective-permute-start.22 = (bf16[4,512,384]{2,1,0:T(8,128)(2,1)S(1)}, bf16[4,512,384]{2,1,0:T(8,128)(2,1)S(1)}, u32[]{:S(2)}, u32[]{:S(2)}) collective-permute-start(bf16[4,512,384]{2,1,0:T(8,128)(2,1)S(1)} %down.13), channel_id=1, source_target_pairs={{0,1},{1,0},{2,3},{3,2},{4,5},{5,4},{6,7},{7,6},{8,9},{9,8},{10,11... | collective-permute-start | bytes 4718600 | tf_op jit(solution)/shard_map/ppermute | solution.py:34
  89.7 12.5 %collective-permute-start.26 = (bf16[2,512,384]{2,1,0:T(8,128)(2,1)S(1)}, bf16[2,512,384]{2,1,0:T(8,128)(2,1)S(1)}, u32[]{:S(2)}, u32[]{:S(2)}) collective-permute-start(bf16[2,512,384]{2,1,0:T(8,128)(2,1)S(1)} %get-tuple-element.71.rest_0_), channel_id=1, source_target_pairs={{0,8},{1,3},{2,10},{3,5},{4,12},{5,7},{6,14},{7,1},{8,16},{9,11},{... | collective-permute-start | bytes 2359304 | tf_op jit(solution)/shard_map/ppermute | solution.py:26
  95.4 20.0 %collective-permute-start.24 = (bf16[4,512,384]{2,1,0:T(8,128)(2,1)S(1)}, bf16[4,512,384]{2,1,0:T(8,128)(2,1)S(1)}, u32[]{:S(2)}, u32[]{:S(2)}) collective-permute-start(bf16[4,512,384]{2,1,0:T(8,128)(2,1)S(1)} %down.17), channel_id=1, source_target_pairs={{0,1},{1,0},{2,3},{3,2},{4,5},{5,4},{6,7},{7,6},{8,9},{9,8},{10,11... | collective-permute-start | bytes 4718600 | tf_op jit(solution)/shard_map/ppermute | solution.py:34
  95.9 11.1 %collective-permute-start.27 = (bf16[2,512,384]{2,1,0:T(8,128)(2,1)S(1)}, bf16[2,512,384]{2,1,0:T(8,128)(2,1)S(1)}, u32[]{:S(2)}, u32[]{:S(2)}) collective-permute-start(bf16[2,512,384]{2,1,0:T(8,128)(2,1)S(1)} %get-tuple-element.73), channel_id=1, source_target_pairs={{0,24},{1,7},{2,26},{3,1},{4,28},{5,3},{6,30},{7,5},{8,0},{9,15},{... | collective-permute-start | bytes 2359304 | tf_op jit(solution)/shard_map/ppermute | solution.py:26
  97.0 18.4 %collective-permute-start.25 = (bf16[2,512,384]{2,1,0:T(8,128)(2,1)S(1)}, bf16[2,512,384]{2,1,0:T(8,128)(2,1)S(1)}, u32[]{:S(2)}, u32[]{:S(2)}) collective-permute-start(bf16[2,512,384]{2,1,0:T(8,128)(2,1)S(1)} %down.16.rest_1_), channel_id=1, source_target_pairs={{0,24},{1,7},{2,26},{3,1},{4,28},{5,3},{6,30},{7,5},{8,0},{9,15},{... | collective-permute-start | bytes 2359304 | tf_op jit(solution)/shard_map/ppermute | solution.py:26
  97.7 21.6 %collective-permute-start.30 = (bf16[2,512,384]{2,1,0:T(8,128)(2,1)S(1)}, bf16[2,512,384]{2,1,0:T(8,128)(2,1)S(1)}, u32[]{:S(2)}, u32[]{:S(2)}) collective-permute-start(bf16[2,512,384]{2,1,0:T(8,128)(2,1)S(1)} %down.14.rest_0_), channel_id=1, source_target_pairs={{0,8},{1,3},{2,10},{3,5},{4,12},{5,7},{6,14},{7,1},{8,16},{9,11},{... | collective-permute-start | bytes 2359304 | tf_op jit(solution)/shard_map/ppermute | solution.py:26
  102.9 16.2 %collective-permute-start.28 = (bf16[2,512,384]{2,1,0:T(8,128)(2,1)S(1)}, bf16[2,512,384]{2,1,0:T(8,128)(2,1)S(1)}, u32[]{:S(2)}, u32[]{:S(2)}) collective-permute-start(bf16[2,512,384]{2,1,0:T(8,128)(2,1)S(1)} %down.18.rest_2_), channel_id=1, source_target_pairs={{0,8},{1,3},{2,10},{3,5},{4,12},{5,7},{6,14},{7,1},{8,16},{9,11},{... | collective-permute-start | bytes 2359304 | tf_op jit(solution)/shard_map/ppermute | solution.py:26
  107.7 16.2 %collective-permute-start.31 = (bf16[2,512,384]{2,1,0:T(8,128)(2,1)S(1)}, bf16[2,512,384]{2,1,0:T(8,128)(2,1)S(1)}, u32[]{:S(2)}, u32[]{:S(2)}) collective-permute-start(bf16[2,512,384]{2,1,0:T(8,128)(2,1)S(1)} %down.19.rest_3_), channel_id=1, source_target_pairs={{0,24},{1,7},{2,26},{3,1},{4,28},{5,3},{6,30},{7,5},{8,0},{9,15},{... | collective-permute-start | bytes 2359304 | tf_op jit(solution)/shard_map/ppermute | solution.py:26
  119.2 8.2 %collective-permute-start.29 = (bf16[512,384]{1,0:T(8,128)(2,1)S(1)}, bf16[512,384]{1,0:T(8,128)(2,1)S(1)}, u32[]{:S(2)}, u32[]{:S(2)}) collective-permute-start(bf16[512,384]{1,0:T(8,128)(2,1)S(1)} %get-tuple-element.76), channel_id=1, source_target_pairs={{0,2},{1,9},{2,4},{3,11},{4,6},{5,13},{6,0},{7,15},{8,10},{9,17},{... | collective-permute-start | bytes 1179656 | tf_op jit(solution)/shard_map/ppermute | solution.py:30
  124.0 7.0 %collective-permute-start.32 = (bf16[512,384]{1,0:T(8,128)(2,1)S(1)}, bf16[512,384]{1,0:T(8,128)(2,1)S(1)}, u32[]{:S(2)}, u32[]{:S(2)}) collective-permute-start(bf16[512,384]{1,0:T(8,128)(2,1)S(1)} %get-tuple-element.77), channel_id=1, source_target_pairs={{0,6},{1,25},{2,0},{3,27},{4,2},{5,29},{6,4},{7,31},{8,14},{9,1},{... | collective-permute-start | bytes 1179656 | tf_op jit(solution)/shard_map/ppermute | solution.py:30
  124.1 8.5 %collective-permute-start.33 = (bf16[512,384]{1,0:T(8,128)(2,1)S(1)}, bf16[512,384]{1,0:T(8,128)(2,1)S(1)}, u32[]{:S(2)}, u32[]{:S(2)}) collective-permute-start(bf16[512,384]{1,0:T(8,128)(2,1)S(1)} %get-tuple-element.78), channel_id=1, source_target_pairs={{0,4},{1,17},{2,6},{3,19},{4,0},{5,21},{6,2},{7,23},{8,12},{9,25},... | collective-permute-start | bytes 1179656 | tf_op jit(solution)/shard_map/ppermute | solution.py:30
  132.9 3.5 %collective-permute-start.34 = (bf16[128,384]{1,0:T(8,128)(2,1)S(1)}, bf16[128,384]{1,0:T(8,128)(2,1)S(1)}, u32[]{:S(2)}, u32[]{:S(2)}) collective-permute-start(bf16[128,384]{1,0:T(8,128)(2,1)S(1)} %get-tuple-element.81), channel_id=1, source_target_pairs={{0,96},{32,0},{64,32},{96,64},{1,97},{33,1},{65,33},{97,65},{2,98}... | collective-permute-start | bytes 294920 | tf_op jit(solution)/shard_map/ppermute | solution.py:38
  134.0 5.0 %collective-permute-start.35 = (bf16[128,384]{1,0:T(8,128)(2,1)S(1)}, bf16[128,384]{1,0:T(8,128)(2,1)S(1)}, u32[]{:S(2)}, u32[]{:S(2)}) collective-permute-start(bf16[128,384]{1,0:T(8,128)(2,1)S(1)} %get-tuple-element.83), channel_id=1, source_target_pairs={{0,64},{32,96},{64,0},{96,32},{1,65},{33,97},{65,1},{97,33},{2,66}... | collective-permute-start | bytes 294920 | tf_op jit(solution)/shard_map/ppermute | solution.py:38
  135.2 4.9 %collective-permute-start.36 = (bf16[128,384]{1,0:T(8,128)(2,1)S(1)}, bf16[128,384]{1,0:T(8,128)(2,1)S(1)}, u32[]{:S(2)}, u32[]{:S(2)}) collective-permute-start(bf16[128,384]{1,0:T(8,128)(2,1)S(1)} %get-tuple-element.82), channel_id=1, source_target_pairs={{0,32},{32,64},{64,96},{96,0},{1,33},{33,65},{65,97},{97,1},{2,34}... | collective-permute-start | bytes 294920 | tf_op jit(solution)/shard_map/ppermute | solution.py:38
  140.3 5.7 %collective-permute-start.37 = (bf16[128,192]{1,0:T(8,128)(2,1)S(1)}, bf16[128,192]{1,0:T(8,128)(2,1)S(1)}, u32[]{:S(2)}, u32[]{:S(2)}) collective-permute-start(bf16[128,192]{1,0:T(8,128)(2,1)S(1)} %broadcast_select_fusion.1), channel_id=1, source_target_pairs={{0,1},{1,0},{2,3},{3,2},{4,5},{5,4},{6,7},{7,6},{8,9},{9,8},{10,11... | collective-permute-start | bytes 147464 | tf_op jit(solution)/shard_map/ppermute | solution.py:34

commit v3 on v2

--- a/solution.py
+++ b/solution.py
@@ -6,6 +6,7 @@
 from jax.sharding import PartitionSpec as P
 
 SIDE = 4
+FAR_FIRST = (2, 1, 3)
 BF = jnp.bfloat16
 F32 = jnp.float32
 
@@ -122,10 +123,11 @@
             at = [pl.multiple_of(feature_block(place_ref[0], *b) * width, width) for b in blocks[j : j + 2]]
             w = jnp.concatenate([w_ref[:, pl.ds(s, width)] for s in at], axis=1)
             y = jnp.dot(h, w, preferred_element_type=F32)
-            for k in range(2):
+            for k in range(len(at)):
                 part = y[:, k * width : (k + 1) * width]
-                for ref, (_, first) in zip(rest, adds):
-                    part = part + ref[j + k + first].astype(F32)
+                for ref, (v, first) in zip(rest, adds):
+                    if 0 <= j + k + first < v.shape[0]:
+                        part = part + ref[j + k + first].astype(F32)
                 out, place = outs[j + k]
                 out[place] = part.astype(dtype)
 
@@ -176,12 +178,13 @@
     n = len(pieces)
 
     def kernel(*refs):
-        for ref, (k, index) in zip(refs[:n], places):
-            refs[n + 1 + k][index] = ref[...]
-
-    return pl.pallas_call(
-        kernel,
-        in_specs=[VMEM] * n + [ANY],
+        for ref, to in zip(refs[:n], places):
+            for k, index, part in to:
+                refs[n + len(behind) + k][index] = ref[part]
+
+    return pl.pallas_call(
+        kernel,
+        in_specs=[VMEM] * n + [ANY] * len(behind),
         out_specs=[VMEM] * len(out_shapes),
         out_shape=[pltpu.VMEM(shape, BF) for shape in out_shapes],
         compiler_params=pltpu.CompilerParams(vmem_limit_bytes=8 << 20),
@@ -189,25 +192,29 @@
             flops=0, bytes_accessed=4 * sum(p.size for p in pieces), transcendentals=0
         ),
         name="gather",
-    )(*in_vmem(pieces), behind)
-
-
-def add_call(total, arrived):
+    )(*in_vmem(pieces), *behind)
+
+
+def add_call(total, *arrived):
     n = total.shape[0]
 
-    def kernel(total_ref, arrived_ref, *outs):
+    def kernel(total_ref, *refs):
         for k in range(n):
-            outs[k][...] = (total_ref[k] + arrived_ref[k].astype(F32)).astype(BF)
-
-    return pl.pallas_call(
-        kernel,
-        in_specs=[VMEM] * 2,
+            out = total_ref[k]
+            for ref in refs[: len(arrived)]:
+                out = out + ref[k].astype(F32)
+            refs[len(arrived) + k][...] = out.astype(BF)
+
+    args = in_vmem([total, *arrived])
+    return pl.pallas_call(
+        kernel,
+        in_specs=[VMEM] * len(args),
         out_specs=[VMEM] * n,
         out_shape=[pltpu.VMEM(total.shape[1:], BF)] * n,
-        compiler_params=pltpu.CompilerParams(vmem_limit_bytes=8 << 20),
-        cost_estimate=pl.CostEstimate(flops=total.size, bytes_accessed=8 * total.size, transcendentals=0),
+        compiler_params=pltpu.CompilerParams(vmem_limit_bytes=12 << 20),
+        cost_estimate=pl.CostEstimate(flops=2 * total.size, bytes_accessed=10 * total.size, transcendentals=0),
         name="add",
-    )(*in_vmem([total, arrived]))
+    )(*args)
 
 
 def fsum(parts):
@@ -240,22 +247,22 @@
     factors = jnp.where(ids[:, 0] == names[:, None], share, 0.0) + jnp.where(ids[:, 1] == names[:, None], 1.0 - share, 0.0)
     gate_w, up_w, t0 = load_call([gate_w, up_w], [pair, factors])
     (owners,) = gather_call(
-        [pair] + [move_expert(pair, d) for d in range(1, SIDE)],
-        [(SIDE * rows, 2 * half)],
-        [(0, slice(d * rows, (d + 1) * rows)) for d in range(SIDE)],
-        t0,
+        [pair] + [move_expert(pair, d) for d in FAR_FIRST],
+        [(1, SIDE * rows, 2 * half)],
+        [[(0, (0, slice(d * rows, (d + 1) * rows)), ...)] for d in (0, *FAR_FIRST)],
+        [t0],
     )
     down_w, t1 = load_call([down_w], [owners])
-    line_a, line_b = gather_call(
-        [owners] + [move_small(owners, d) for d in range(1, SIDE)],
-        [(two, SIDE * rows, 2 * half)] * 2,
-        [(d // two, d % two) for d in range(SIDE)],
-        t1,
+    (line,) = gather_call(
+        [owners] + [move_small(owners, d) for d in FAR_FIRST],
+        [(SIDE, SIDE * rows, 2 * half)],
+        [[(0, slice(d, d + 1), ...)] for d in (0, *FAR_FIRST)],
+        [t1],
     )
+
     def at(sign, other, d, blocks=range(SIDE)):
         return [(sign, other, d, k) for k in blocks]
 
-    first, last = range(two), range(two, SIDE)
 
     def up(pieces, blocks, carry, final=False, behind=()):
         *sums, token = up_call(pieces, where, blocks, gate_w, up_w, carry, final, behind)
@@ -264,51 +271,47 @@
     def down(h, blocks, adds, splits, dtype=BF, behind=()):
         return down_call(h, where, blocks, down_w, adds, splits, dtype, behind)
 
-    right_a, left_b = move_bulk(line_a, 1), move_bulk(line_b, 3)
-    right_b, left_a = move_bulk(line_b, 1), move_bulk(line_a, 3)
-    far_a, far_b = move_bulk(right_a, 1), move_bulk(left_b, 3)
-    other_line = [move_core(line_a), move_core(line_b)]
-    other_early = [move_core(right_a), move_core(left_b)]
-    own_sum, t0 = up([line_a, line_b], at(-1, 0, 0), None)
-    other_sum, t1 = up(other_line, at(-1, 1, 0), None, False, [t0])
-    early = [(1, first), (3, last)]
-    late = [(1, last), (3, first)]
-
-    def near(other, parts):
-        return [b for d, blocks in parts for b in at(-1, other, d, blocks)]
-
-    other_sum, t1 = up(other_early, near(1, early), other_sum)
-    right_b, left_a = after(right_b, t1), after(left_a, t1)
-    other_late = [move_core(right_b), move_core(left_a)]
-    own_sum, t0 = up([right_a, left_b, right_b, left_a], near(0, early + late), own_sum)
-    other_sum, t1 = up(other_late, near(1, late), other_sum, False, [t0])
+    right, left = move_bulk(line, 1), move_bulk(line, 3)
+    other_line = move_core(line)
+    own_sum, t0 = up([line], at(-1, 0, 0), None)
+    other_sum, t1 = up([other_line], at(-1, 1, 0), None, False, [t0])
+    right, left = after(right, t1), after(left, t1)
+    shape = (two,) + line.shape[1:]
+    (send_a,) = gather_call([right], [shape], [[(0, slice(None), slice(two))]], [t1])
+    (send_b,) = gather_call([left], [shape], [[(0, slice(None), slice(two, SIDE))]], [t1])
+    far_a, far_b = move_bulk(send_a, 1), move_bulk(send_b, 3)
+    other_near = [move_core(after(right, send_a, send_b)), move_core(after(left, send_a, send_b))]
+    own_sum, t0 = up([right, left], at(-1, 0, 1) + at(-1, 0, 3), own_sum, False, [send_a, send_b])
+    other_sum, t1 = up(other_near, at(-1, 1, 1) + at(-1, 1, 3), other_sum, False, [t0])
     far_a, far_b = after(far_a, t1), after(far_b, t1)
-    other_a, other_b = move_core(far_a), move_core(far_b)
+    other_far = [move_core(far_a), move_core(far_b)]
     (h_own,), t0 = up([far_a, far_b], at(-1, 0, 2), own_sum, True)
 
-    sent2 = move_core(down(h_own, at(1, 1, 2), [], [SIDE])[0])
-    (h_other,), t1 = up([other_a, other_b], at(-1, 1, 2), other_sum, True)
-    m2a, m2b = down(h_other, at(1, 0, 2), [(sent2, 0)], [two, two])
+    (send2,) = down(h_own, at(1, 1, 2), [], [SIDE])
+    sent2 = move_core(send2)
+    (h_other,), t1 = up(other_far, at(-1, 1, 2), other_sum, True, [send2])
+    (send1,) = down(h_own, at(1, 1, 1), [], [SIDE], BF, [t1])
+    (send3,) = down(h_own, at(1, 1, 3), [], [SIDE], BF, [t1])
+    sent1, sent3 = move_core(send1), move_core(send3)
+    m2a, m2b = down(h_other, at(1, 0, 2), [(sent2, 0)], [two, two], BF, [send1, send3])
     step_a, step_b = move_bulk(m2a, 1), move_bulk(m2b, 3)
-    sent1 = move_core(down(h_own, at(1, 1, 1), [], [SIDE], BF, [m2a])[0])
-    sent3 = move_core(down(h_own, at(1, 1, 3), [], [SIDE], BF, [m2a])[0])
-    (m1b,) = down(h_other, at(1, 0, 1, last), [(sent1, two)], [two])
-    (m3a,) = down(h_other, at(1, 0, 3, first), [(sent3, 0)], [two])
-    n1b, n3a = move_bulk(m1b, 1), move_bulk(m3a, 3)
-    sent0 = move_core(down(h_own, at(1, 1, 0), [], [SIDE], BF, [m1b, m3a])[0])
-    step_a, step_b = after(step_a, m1b, m3a), after(step_b, m1b, m3a)
-    (m1a,) = down(h_other, at(1, 0, 1, first), [(sent1, 0), (step_a, 0)], [two])
-    (m3b,) = down(h_other, at(1, 0, 3, last), [(sent3, two), (step_b, 0)], [two])
-    n1a, n3b = move_bulk(m1a, 1), move_bulk(m3b, 3)
-    (m0a,) = down(h_other, at(1, 0, 0, first), [(sent0, 0), (n3a, 0)], [two], F32, [m1a, m3b])
-    (m0b,) = down(h_other, at(1, 0, 0, last), [(sent0, two), (n1b, 0)], [two], F32, [m1a, m3b])
-    s0, s1 = add_call(m0a, n1a)
-    s2, s3 = add_call(m0b, n3b)
-    plane = fsum([s0, move_small(s1, 1), move_small(s3, 3), move_small(s2, 2)]).astype(BF)
+    sent0 = move_core(down(h_own, at(1, 1, 0), [], [SIDE], BF, [m2a])[0])
+    others = range(1, SIDE)
+    (m1,) = down(h_other, at(1, 0, 1, others), [(sent1, 1), (step_a, 1)], [SIDE - 1])
+    (m3,) = down(h_other, at(1, 0, 3, others), [(sent3, 1), (step_b, 1 - two)], [SIDE - 1])
+    n1, n3 = move_bulk(m1, 1), move_bulk(m3, 3)
+    (m1_own,) = down(h_other, at(1, 0, 1, [0]), [(sent1, 0), (step_a, 0)], [1], BF, [m1, m3])
+    (m3_own,) = down(h_other, at(1, 0, 3, [0]), [(sent3, 0)], [1], BF, [m1, m3])
+    m0_own, m0 = down(h_other, at(1, 0, 0), [(sent0, 0)], [1, SIDE - 1], F32, [m1, m3])
+    s1, s2, s3 = add_call(m0, n1, n3)
+    moved = [move_small(s2, 2), move_small(s1, 1), move_small(s3, 3)]
+    own1, own3 = gather_call([m1_own, m3_own], [m1_own.shape] * 2, [[(0, ..., ...)], [(1, ..., ...)]], [s1])
+    n1_own, n3_own = move_bulk(own1, 1), move_bulk(own3, 3)
+    plane = fsum([m0_own[0], n1_own[0], n3_own[0]] + moved).astype(BF)
     plane = plane.reshape(SIDE, rows, 2 * half)
 
     total = 0.0
-    for d in range(SIDE):
+    for d in (0, *FAR_FIRST):
         back = plane[d] if d == 0 else move_expert(plane[d], -d)
         total = total + factors[d][:, None] * back.astype(F32)
     total = total.astype(BF)

time: 147 us -> 143 us (0.973)
  starting transfers between devices: 42.2 us -> 37.1 us
  waiting for transfers between devices: 66.5 us -> 69 us
    ppermute x14 -> x11, waiting for transfers between devices: 8.46 us -> 1.22 us  [move_core(): return lax.ppermute(v, 'blk', [(i, i ^ 1) for i in range(2 * SIDE * SIDE)])]
    ppermute x12 -> x10, waiting for transfers between devices: 40.1 us -> 46.8 us  [move_bulk(): return lax.ppermute(v, 'blk', blk_perm(True, shift))]
    ppermute x14 -> x11, starting transfers between devices: 14.2 us -> 9.77 us  [move_core(): return lax.ppermute(v, 'blk', [(i, i ^ 1) for i in range(2 * SIDE * SIDE)])]
    pallas_call x7 -> x6, Pallas kernels: 17.2 us -> 15.3 us  [up_call(): pl.pallas_call(kernel, in_specs=[SMEM] + [VMEM] * len(args) + [ANY] * len...]
    ppermute x6, waiting for transfers between devices: 4.75 us -> 6.63 us  [move_expert(): lax.ppermute(v, 'expert', [(i, (i + shift) % SIDE) for i in range(SIDE)])]
    ppermute x12 -> x10, starting transfers between devices: 13.1 us -> 12 us  [move_bulk(): return lax.ppermute(v, 'blk', blk_perm(True, shift))]
    pallas_call x11 -> x10, Pallas kernels: 8.72 us -> 8.92 us  [down_call(): pl.pallas_call(kernel, in_specs=[SMEM] + [VMEM] * len(args) + [ANY] * len...]
  transfers between devices with their start and end apart: 38 -> 33, of which waited for: 23 -> 19; matrix products, arithmetic and copies ran while one was open for 1% -> 1% of each run, Pallas kernels for 19% -> 22%
where the time goes in v3:
time: 143 us
  waiting for transfers between devices  69 us (48%)
  starting transfers between devices  37.1 us (26%)
  Pallas kernels  32.4 us (23%)
  other arithmetic  2.34 us (2%)
  local copies, waits for them, and re-layouts  1.78 us (1%)
    ppermute x10, waiting for transfers between devices, move_bulk(): return lax.ppermute(v, 'blk', blk_perm(True, shift))  46.8 us
    pallas_call x6, Pallas kernels, up_call(): pl.pallas_call(kernel, in_specs=[SMEM] + [VMEM] * len(args) + [ANY] * len...  15.3 us
    ppermute x6, waiting for transfers between devices, move_small(): return lax.ppermute(v, 'blk', blk_perm(False, shift))  14.4 us
    ppermute x10, starting transfers between devices, move_bulk(): return lax.ppermute(v, 'blk', blk_perm(True, shift))  12 us
    ppermute x11, starting transfers between devices, move_core(): return lax.ppermute(v, 'blk', [(i, i ^ 1) for i in range(2 * SIDE * SIDE)])  9.77 us
    pallas_call x10, Pallas kernels, down_call(): pl.pallas_call(kernel, in_specs=[SMEM] + [VMEM] * len(args) + [ANY] * len...  8.92 us
    ppermute x6, starting transfers between devices, move_small(): return lax.ppermute(v, 'blk', blk_perm(False, shift))  7.76 us
    ppermute x6, starting transfers between devices, move_expert(): lax.ppermute(v, 'expert', [(i, (i + shift) % SIDE) for i in range(SIDE)])  7.6 us
  transfers between devices with their start and end apart: 33, of which 19 were waited for; matrix products, arithmetic and copies ran while one was open for 1% of the time, Pallas kernels for 22%

profile of v3, /device:TPU:1, one launch (start us, length us, event | category | flops | bytes accessed | tf_op | source)
XLA Modules:
  0.0 142.8 jit_solution(6483019368008426409)
XLA Ops:
  0.0 1.0 copy.7
  1.0 1.5 %collective-permute-start = (bf16[128,192]{1,0:T(8,128)(2,1)S(1)}, bf16[128,192]{1,0:T(8,128)(2,1)S(1)}, u32[]{:S(2)}, u32[]{:S(2)}) collective-permute-start(bf16[128,192]{1,0:T(8,128)(2,1)S(1)} %get-tuple-element.87), channel_id=1, source_target_pairs={{0,1},{1,0},{2,3},{3,2},{4,5},{5,4},{6,7},{7,6},{8,9},{9,8},{10,11... | collective-permute-start | bytes 147464 | tf_op jit(solution)/shard_map/ppermute | solution.py:35
  2.5 0.7 select_bitcast_fusion.4
  3.2 0.8 broadcast_subtract_fusion
  4.1 2.9 %collective-permute-start.3 = (bf16[128,384]{1,0:T(8,128)(2,1)S(1)}, bf16[128,384]{1,0:T(8,128)(2,1)S(1)}, u32[]{:S(2)}, u32[]{:S(2)}) collective-permute-start(bf16[128,384]{1,0:T(8,128)(2,1)S(1)} %maximum_select_fusion.refs_2_.refs_0_), channel_id=1, source_target_pairs={{0,96},{32,0},{64,32},{96,64},{1,97},{33,1},{65,33},{97,65},{2,98}... | collective-permute-start | bytes 294920 | tf_op jit(solution)/shard_map/ppermute | solution.py:39
  7.0 1.6 %collective-permute-start.1 = (bf16[128,384]{1,0:T(8,128)(2,1)S(1)}, bf16[128,384]{1,0:T(8,128)(2,1)S(1)}, u32[]{:S(2)}, u32[]{:S(2)}) collective-permute-start(bf16[128,384]{1,0:T(8,128)(2,1)S(1)} %maximum_select_fusion.refs_2_.refs_0_), channel_id=1, source_target_pairs={{0,64},{32,96},{64,0},{96,32},{1,65},{33,97},{65,1},{97,33},{2,66}... | collective-permute-start | bytes 294920 | tf_op jit(solution)/shard_map/ppermute | solution.py:39
  8.7 4.6 %load.2 = (bf16[6144,512]{1,0:T(8,128)(2,1)S(1)}, bf16[6144,512]{1,0:T(8,128)(2,1)S(1)}, f32[8,128]{1,0:T(8,128)S(1)}) custom-call(bf16[6144,512]{1,0:T(8,128)(2,1)} %bitcast.38, bf16[6144,512]{1,0:T(8,128)(2,1)} %bitcast.39, bf16[128,384]{1,0:T(8,128)(2,1)S(1)} %maximum_select_fusion.refs_2_.refs_0_, f32[4,128]{1,0:T(4,128)S(1)} %select_add_fusion.refs_3_), custom_call_target="tpu_custom_call" | custom-call | bytes 25165824 | tf_op jit(solution)/shard_map/load/pallas_call | solution.py:163
  13.4 1.3 collective-permute-done.2.refs_2_
  14.7 3.8 %collective-permute-start.6 = (bf16[1,512,384]{2,1,0:T(8,128)(2,1)S(1)}, bf16[1,512,384]{2,1,0:T(8,128)(2,1)S(1)}, u32[]{:S(2)}, u32[]{:S(2)}) collective-permute-start(bf16[1,512,384]{2,1,0:T(8,128)(2,1)S(1)} %gather.5.refs_1_.refs_0_), channel_id=1, source_target_pairs={{0,6},{1,25},{2,0},{3,27},{4,2},{5,29},{6,4},{7,31},{8,14},{9,1},{... | collective-permute-start | bytes 1179656 | tf_op jit(solution)/shard_map/ppermute | solution.py:31
  18.5 1.3 collective-permute-start.4
  19.8 2.8 %load.3 = (bf16[512,6144]{1,0:T(8,128)(2,1)S(1)}, f32[8,128]{1,0:T(8,128)S(1)}) custom-call(bf16[512,6144]{1,0:T(8,128)(2,1)} %bitcast.37, bf16[1,512,384]{2,1,0:T(8,128)(2,1)S(1)} %gather.5.refs_1_.refs_0_), custom_call_target="tpu_custom_call" | custom-call | bytes 12582912 | tf_op jit(solution)/shard_map/load/pallas_call | solution.py:163
  22.6 4.8 %collective-permute-done.6.refs_3_ = bf16[1,512,384]{2,1,0:T(8,128)(2,1)S(1)} collective-permute-done((bf16[1,512,384]{2,1,0:T(8,128)(2,1)S(1)}, bf16[1,512,384]{2,1,0:T(8,128)(2,1)S(1)}, u32[]{:S(2)}, u32[]{:S(2)}) %collective-permute-start.6) | collective-permute-done | bytes 393248 | tf_op jit(solution)/shard_map/ppermute | solution.py:31
  27.4 3.4 %collective-permute-done.5.refs_2_ = bf16[1,512,384]{2,1,0:T(8,128)(2,1)S(1)} collective-permute-done((bf16[1,512,384]{2,1,0:T(8,128)(2,1)S(1)}, bf16[1,512,384]{2,1,0:T(8,128)(2,1)S(1)}, u32[]{:S(2)}, u32[]{:S(2)}) %collective-permute-start.5) | collective-permute-done | bytes 393248 | tf_op jit(solution)/shard_map/ppermute | solution.py:31
  31.0 0.9 collective-permute-start.8
  31.8 1.5 %collective-permute-start.10 = (bf16[4,512,384]{2,1,0:T(8,128)(2,1)S(1)}, bf16[4,512,384]{2,1,0:T(8,128)(2,1)S(1)}, u32[]{:S(2)}, u32[]{:S(2)}) collective-permute-start(bf16[4,512,384]{2,1,0:T(8,128)(2,1)S(1)} %gather.6.refs_0_), channel_id=1, source_target_pairs={{0,24},{1,7},{2,26},{3,1},{4,28},{5,3},{6,30},{7,5},{8,0},{9,15},{... | collective-permute-start | bytes 4718600 | tf_op jit(solution)/shard_map/ppermute | solution.py:27
  33.3 1.8 %up.6 = (f32[512,512]{1,0:T(8,128)S(1)}, f32[512,512]{1,0:T(8,128)S(1)}, f32[8,128]{1,0:T(8,128)S(1)}) custom-call(s32[1]{0:T(128)} %bitcast.5.place_ref, bf16[4,512,384]{2,1,0:T(8,128)(2,1)S(1)} %gather.6.refs_0_, bf16[6144,512]{1,0:T(8,128)(2,1)S(1)} %get-tuple-element.46.refs_1_.refs_2_, bf16[6144,512]{1,0:T(8,128)(2,1)S(1)} %get-tuple-element.47.refs_2_.refs_3_), custom_call_target="tpu_custom_call" | custom-call | flops 1610612736 | bytes 6815744 | tf_op jit(solution)/shard_map/up/pallas_call | solution.py:98
  35.2 1.8 %up.7 = (f32[512,512]{1,0:T(8,128)S(1)}, f32[512,512]{1,0:T(8,128)S(1)}, f32[8,128]{1,0:T(8,128)S(1)}) custom-call(s32[1]{0:T(128)} %bitcast.5.place_ref, bf16[4,512,384]{2,1,0:T(8,128)(2,1)S(1)} %collective-permute-done.8.refs_0_, bf16[6144,512]{1,0:T(8,128)(2,1)S(1)} %get-tuple-element.46.refs_1_.refs_2_, ...), custom_call_target="tpu_custom_call" | custom-call | flops 1610612736 | bytes 6815744 | tf_op jit(solution)/shard_map/up/pallas_call | solution.py:98
  37.0 14.4 %collective-permute-done.10.refs_0_.refs_1_ = bf16[4,512,384]{2,1,0:T(8,128)(2,1)S(1)} collective-permute-done((bf16[4,512,384]{2,1,0:T(8,128)(2,1)S(1)}, bf16[4,512,384]{2,1,0:T(8,128)(2,1)S(1)}, u32[]{:S(2)}, u32[]{:S(2)}) %collective-permute-start.10) | collective-permute-done | bytes 1572896 | tf_op jit(solution)/shard_map/ppermute | solution.py:27
  51.4 2.7 %collective-permute-done.7.refs_0_ = bf16[4,512,384]{2,1,0:T(8,128)(2,1)S(1)} collective-permute-done((bf16[4,512,384]{2,1,0:T(8,128)(2,1)S(1)}, bf16[4,512,384]{2,1,0:T(8,128)(2,1)S(1)}, u32[]{:S(2)}, u32[]{:S(2)}) %collective-permute-start.7) | collective-permute-done | bytes 1572896 | tf_op jit(solution)/shard_map/ppermute | solution.py:27
  54.3 3.6 %collective-permute-start.11 = (bf16[4,512,384]{2,1,0:T(8,128)(2,1)S(1)}, bf16[4,512,384]{2,1,0:T(8,128)(2,1)S(1)}, u32[]{:S(2)}, u32[]{:S(2)}) collective-permute-start(bf16[4,512,384]{2,1,0:T(8,128)(2,1)S(1)} %collective-permute-done.7.refs_0_), channel_id=1, source_target_pairs={{0,1},{1,0},{2,3},{3,2},{4,5},{5,4},{6,7},{7,6},{8,9},{9,8},{10,11... | collective-permute-start | bytes 4718600 | tf_op jit(solution)/shard_map/ppermute | solution.py:35
  57.9 1.5 %collective-permute-start.9 = (bf16[2,512,384]{2,1,0:T(8,128)(2,1)S(1)}, bf16[2,512,384]{2,1,0:T(8,128)(2,1)S(1)}, u32[]{:S(2)}, u32[]{:S(2)}) collective-permute-start(bf16[2,512,384]{2,1,0:T(8,128)(2,1)S(1)} %gather.7.refs_6_), channel_id=1, source_target_pairs={{0,8},{1,3},{2,10},{3,5},{4,12},{5,7},{6,14},{7,1},{8,16},{9,11},{... | collective-permute-start | bytes 2359304 | tf_op jit(solution)/shard_map/ppermute | solution.py:27
  59.4 3.4 %up.8 = (f32[512,512]{1,0:T(8,128)S(1)}, f32[512,512]{1,0:T(8,128)S(1)}, f32[8,128]{1,0:T(8,128)S(1)}) custom-call(s32[1]{0:T(128)} %bitcast.5.place_ref, bf16[4,512,384]{2,1,0:T(8,128)(2,1)S(1)} %collective-permute-done.7.refs_0_, bf16[4,512,384]{2,1,0:T(8,128)(2,1)S(1)} %collective-permute-done.10.refs_0_.refs_1_, ...), custom_call_target="tpu_custom_call" | custom-call | flops 3221225472 | bytes 11534336 | tf_op jit(solution)/shard_map/up/pallas_call | solution.py:98
  62.8 0.3 collective-permute-done.12.refs_1_
  63.1 3.9 %up.9 = (f32[512,512]{1,0:T(8,128)S(1)}, f32[512,512]{1,0:T(8,128)S(1)}, f32[8,128]{1,0:T(8,128)}) custom-call(s32[1]{0:T(128)} %bitcast.5.place_ref, bf16[4,512,384]{2,1,0:T(8,128)(2,1)S(1)} %collective-permute-done.11.refs_0_, bf16[4,512,384]{2,1,0:T(8,128)(2,1)S(1)} %collective-permute-done.12.refs_1_, ...), custom_call_target="tpu_custom_call" | custom-call | flops 3221225472 | bytes 11534336 | tf_op jit(solution)/shard_map/up/pallas_call | solution.py:98
  67.0 2.0 %collective-permute-done.14.refs_1_ = bf16[2,512,384]{2,1,0:T(8,128)(2,1)S(1)} collective-permute-done((bf16[2,512,384]{2,1,0:T(8,128)(2,1)S(1)}, bf16[2,512,384]{2,1,0:T(8,128)(2,1)S(1)}, u32[]{:S(2)}, u32[]{:S(2)}) %collective-permute-start.14) | collective-permute-done | bytes 786464 | tf_op jit(solution)/shard_map/ppermute | solution.py:27
  69.0 1.2 collective-permute-done.9.refs_0_
  70.3 1.3 collective-permute-start.13
  71.5 2.4 %up.10 = (bf16[512,512]{1,0:T(8,128)(2,1)S(1)}, f32[8,128]{1,0:T(8,128)}) custom-call(s32[1]{0:T(128)} %bitcast.5.place_ref, bf16[2,512,384]{2,1,0:T(8,128)(2,1)S(1)} %collective-permute-done.9.refs_0_, bf16[2,512,384]{2,1,0:T(8,128)(2,1)S(1)} %collective-permute-done.14.refs_1_, bf16[6144,512]{1,0:T(8,128)(2,1)S(1)} %get-tuple-element.46.refs_1_.refs_2_, ...), custom_call_target="tpu_custom_call" | custom-call | flops 1610612736 | bytes 6815744 | tf_op jit(solution)/shard_map/up/pallas_call | solution.py:98
  74.0 1.0 down.10.refs_6_
  75.0 0.6 collective-permute-start.16
  75.6 1.9 %up.11 = (bf16[512,512]{1,0:T(8,128)(2,1)S(1)}, f32[8,128]{1,0:T(8,128)S(1)}) custom-call(s32[1]{0:T(128)} %bitcast.5.place_ref, bf16[2,512,384]{2,1,0:T(8,128)(2,1)S(1)} %collective-permute-done.13.refs_0_, bf16[2,512,384]{2,1,0:T(8,128)(2,1)S(1)} %collective-permute-done.15.refs_1_, bf16[6144,512]{1,0:T(8,128)(2,1)S(1)} %get-tuple-element.46.refs_1_.refs_2_, ...), custom_call_target="tpu_custom_call" | custom-call | flops 1610612736 | bytes 6815744 | tf_op jit(solution)/shard_map/up/pallas_call | solution.py:98
  77.5 1.0 down.11.rest_1_
  78.6 1.0 down.12.rest_2_
  79.6 0.6 collective-permute-start.20
  80.2 1.0 down.13
  81.3 2.7 %collective-permute-start.21 = (bf16[2,512,384]{2,1,0:T(8,128)(2,1)S(1)}, bf16[2,512,384]{2,1,0:T(8,128)(2,1)S(1)}, u32[]{:S(2)}, u32[]{:S(2)}) collective-permute-start(bf16[2,512,384]{2,1,0:T(8,128)(2,1)S(1)} %get-tuple-element.71), channel_id=1, source_target_pairs={{0,24},{1,7},{2,26},{3,1},{4,28},{5,3},{6,30},{7,5},{8,0},{9,15},{... | collective-permute-start | bytes 2359304 | tf_op jit(solution)/shard_map/ppermute | solution.py:27
  83.9 1.0 down.14
  84.9 0.7 collective-permute-start.17
  85.6 8.0 %collective-permute-done.19.rest_1_ = bf16[2,512,384]{2,1,0:T(8,128)(2,1)S(1)} collective-permute-done((bf16[2,512,384]{2,1,0:T(8,128)(2,1)S(1)}, bf16[2,512,384]{2,1,0:T(8,128)(2,1)S(1)}, u32[]{:S(2)}, u32[]{:S(2)}) %collective-permute-start.19) | collective-permute-done | bytes 786464 | tf_op jit(solution)/shard_map/ppermute | solution.py:27
  93.6 0.9 down.15.rest_1_.rest_2_
  94.6 1.1 down.16.rest_2_.rest_3_
  95.7 2.9 %collective-permute-start.23 = (bf16[3,512,384]{2,1,0:T(8,128)(2,1)S(1)}, bf16[3,512,384]{2,1,0:T(8,128)(2,1)S(1)}, u32[]{:S(2)}, u32[]{:S(2)}) collective-permute-start(bf16[3,512,384]{2,1,0:T(8,128)(2,1)S(1)} %down.16.rest_2_.rest_3_), channel_id=1, source_target_pairs={{0,24},{1,7},{2,26},{3,1},{4,28},{5,3},{6,30},{7,5},{8,0},{9,15},{... | collective-permute-start | bytes 3538952 | tf_op jit(solution)/shard_map/ppermute | solution.py:27
  98.6 0.4 down.18.refs_0_
  99.0 0.5 down.19.refs_1_
  99.5 1.0 down.17
  100.5 10.6 %collective-permute-done.22.refs_0_ = bf16[3,512,384]{2,1,0:T(8,128)(2,1)S(1)} collective-permute-done((bf16[3,512,384]{2,1,0:T(8,128)(2,1)S(1)}, bf16[3,512,384]{2,1,0:T(8,128)(2,1)S(1)}, u32[]{:S(2)}, u32[]{:S(2)}) %collective-permute-start.22) | collective-permute-done | bytes 1179680 | tf_op jit(solution)/shard_map/ppermute | solution.py:27
  111.1 0.6 collective-permute-done.23.refs_1_
  111.7 0.4 add.94
  112.3 3.2 %collective-permute-start.25 = (bf16[1,512,384]{2,1,0:T(8,128)(2,1)S(1)}, bf16[1,512,384]{2,1,0:T(8,128)(2,1)S(1)}, u32[]{:S(2)}, u32[]{:S(2)}) collective-permute-start(bf16[1,512,384]{2,1,0:T(8,128)(2,1)S(1)} %get-tuple-element.76), channel_id=1, source_target_pairs={{0,24},{1,7},{2,26},{3,1},{4,28},{5,3},{6,30},{7,5},{8,0},{9,15},{... | collective-permute-start | bytes 1179656 | tf_op jit(solution)/shard_map/ppermute | solution.py:27
  115.7 2.3 %collective-permute-start.28 = (bf16[512,384]{1,0:T(8,128)(2,1)S(1)}, bf16[512,384]{1,0:T(8,128)(2,1)S(1)}, u32[]{:S(2)}, u32[]{:S(2)}) collective-permute-start(bf16[512,384]{1,0:T(8,128)(2,1)S(1)} %get-tuple-element.78), channel_id=1, source_target_pairs={{0,6},{1,25},{2,0},{3,27},{4,2},{5,29},{6,4},{7,31},{8,14},{9,1},{... | collective-permute-start | bytes 1179656 | tf_op jit(solution)/shard_map/ppermute | solution.py:31
  118.1 2.7 %collective-permute-done.24 = bf16[1,512,384]{2,1,0:T(8,128)(2,1)S(1)} collective-permute-done((bf16[1,512,384]{2,1,0:T(8,128)(2,1)S(1)}, bf16[1,512,384]{2,1,0:T(8,128)(2,1)S(1)}, u32[]{:S(2)}, u32[]{:S(2)}) %collective-permute-start.24) | collective-permute-done | bytes 393248 | tf_op jit(solution)/shard_map/ppermute | solution.py:27
  120.8 4.5 %collective-permute-done.25 = bf16[1,512,384]{2,1,0:T(8,128)(2,1)S(1)} collective-permute-done((bf16[1,512,384]{2,1,0:T(8,128)(2,1)S(1)}, bf16[1,512,384]{2,1,0:T(8,128)(2,1)S(1)}, u32[]{:S(2)}, u32[]{:S(2)}) %collective-permute-start.25) | collective-permute-done | bytes 393248 | tf_op jit(solution)/shard_map/ppermute | solution.py:27
  125.3 1.6 %collective-permute-done.26 = bf16[512,384]{1,0:T(8,128)(2,1)S(1)} collective-permute-done((bf16[512,384]{1,0:T(8,128)(2,1)S(1)}, bf16[512,384]{1,0:T(8,128)(2,1)S(1)}, u32[]{:S(2)}, u32[]{:S(2)}) %collective-permute-start.26) | collective-permute-done | bytes 393248 | tf_op jit(solution)/shard_map/ppermute | solution.py:31
  127.0 3.0 %collective-permute-done.28 = bf16[512,384]{1,0:T(8,128)(2,1)S(1)} collective-permute-done((bf16[512,384]{1,0:T(8,128)(2,1)S(1)}, bf16[512,384]{1,0:T(8,128)(2,1)S(1)}, u32[]{:S(2)}, u32[]{:S(2)}) %collective-permute-start.28) | collective-permute-done | bytes 393248 | tf_op jit(solution)/shard_map/ppermute | solution.py:31
  129.9 1.5 %collective-permute-done.27 = bf16[512,384]{1,0:T(8,128)(2,1)S(1)} collective-permute-done((bf16[512,384]{1,0:T(8,128)(2,1)S(1)}, bf16[512,384]{1,0:T(8,128)(2,1)S(1)}, u32[]{:S(2)}, u32[]{:S(2)}) %collective-permute-start.27) | collective-permute-done | bytes 393248 | tf_op jit(solution)/shard_map/ppermute | solution.py:31
  131.5 0.3 fusion.2
  131.8 0.4 collective-permute-start.29
  132.2 1.1 collective-permute-start.31
  133.4 1.5 %collective-permute-start.30 = (bf16[128,384]{1,0:T(8,128)(2,1)S(1)}, bf16[128,384]{1,0:T(8,128)(2,1)S(1)}, u32[]{:S(2)}, u32[]{:S(2)}) collective-permute-start(bf16[128,384]{1,0:T(8,128)(2,1)S(1)} %get-tuple-element.83), channel_id=1, source_target_pairs={{0,96},{32,0},{64,32},{96,64},{1,97},{33,1},{65,33},{97,65},{2,98}... | collective-permute-start | bytes 294920 | tf_op jit(solution)/shard_map/ppermute | solution.py:39
  134.9 2.9 %collective-permute-done.29 = bf16[128,384]{1,0:T(8,128)(2,1)S(1)} collective-permute-done((bf16[128,384]{1,0:T(8,128)(2,1)S(1)}, bf16[128,384]{1,0:T(8,128)(2,1)S(1)}, u32[]{:S(2)}, u32[]{:S(2)}) %collective-permute-start.29) | collective-permute-done | bytes 98336 | tf_op jit(solution)/shard_map/ppermute | solution.py:39
  137.8 2.5 %collective-permute-done.31 = bf16[128,384]{1,0:T(8,128)(2,1)S(1)} collective-permute-done((bf16[128,384]{1,0:T(8,128)(2,1)S(1)}, bf16[128,384]{1,0:T(8,128)(2,1)S(1)}, u32[]{:S(2)}, u32[]{:S(2)}) %collective-permute-start.31) | collective-permute-done | bytes 98336 | tf_op jit(solution)/shard_map/ppermute | solution.py:39
  140.5 0.6 collective-permute-start.32
  141.1 0.9 collective-permute-done.32
  142.1 0.7 copy.9
  (42 shorter events, 1.7 us)
Async XLA Ops:
  1.0 3.0 %collective-permute-start = (bf16[128,192]{1,0:T(8,128)(2,1)S(1)}, bf16[128,192]{1,0:T(8,128)(2,1)S(1)}, u32[]{:S(2)}, u32[]{:S(2)}) collective-permute-start(bf16[128,192]{1,0:T(8,128)(2,1)S(1)} %get-tuple-element.87), channel_id=1, source_target_pairs={{0,1},{1,0},{2,3},{3,2},{4,5},{5,4},{6,7},{7,6},{8,9},{9,8},{10,11... | collective-permute-start | bytes 147464 | tf_op jit(solution)/shard_map/ppermute | solution.py:35
  4.1 9.2 %collective-permute-start.3 = (bf16[128,384]{1,0:T(8,128)(2,1)S(1)}, bf16[128,384]{1,0:T(8,128)(2,1)S(1)}, u32[]{:S(2)}, u32[]{:S(2)}) collective-permute-start(bf16[128,384]{1,0:T(8,128)(2,1)S(1)} %maximum_select_fusion.refs_2_.refs_0_), channel_id=1, source_target_pairs={{0,96},{32,0},{64,32},{96,64},{1,97},{33,1},{65,33},{97,65},{2,98}... | collective-permute-start | bytes 294920 | tf_op jit(solution)/shard_map/ppermute | solution.py:39
  7.0 7.6 %collective-permute-start.2 = (bf16[128,384]{1,0:T(8,128)(2,1)S(1)}, bf16[128,384]{1,0:T(8,128)(2,1)S(1)}, u32[]{:S(2)}, u32[]{:S(2)}) collective-permute-start(bf16[128,384]{1,0:T(8,128)(2,1)S(1)} %maximum_select_fusion.refs_2_.refs_0_), channel_id=1, source_target_pairs={{0,32},{32,64},{64,96},{96,0},{1,33},{33,65},{65,97},{97,1},{2,34}... | collective-permute-start | bytes 294920 | tf_op jit(solution)/shard_map/ppermute | solution.py:39
  7.0 7.6 %collective-permute-start.1 = (bf16[128,384]{1,0:T(8,128)(2,1)S(1)}, bf16[128,384]{1,0:T(8,128)(2,1)S(1)}, u32[]{:S(2)}, u32[]{:S(2)}) collective-permute-start(bf16[128,384]{1,0:T(8,128)(2,1)S(1)} %maximum_select_fusion.refs_2_.refs_0_), channel_id=1, source_target_pairs={{0,64},{32,96},{64,0},{96,32},{1,65},{33,97},{65,1},{97,33},{2,66}... | collective-permute-start | bytes 294920 | tf_op jit(solution)/shard_map/ppermute | solution.py:39
  14.7 12.8 %collective-permute-start.6 = (bf16[1,512,384]{2,1,0:T(8,128)(2,1)S(1)}, bf16[1,512,384]{2,1,0:T(8,128)(2,1)S(1)}, u32[]{:S(2)}, u32[]{:S(2)}) collective-permute-start(bf16[1,512,384]{2,1,0:T(8,128)(2,1)S(1)} %gather.5.refs_1_.refs_0_), channel_id=1, source_target_pairs={{0,6},{1,25},{2,0},{3,27},{4,2},{5,29},{6,4},{7,31},{8,14},{9,1},{... | collective-permute-start | bytes 1179656 | tf_op jit(solution)/shard_map/ppermute | solution.py:31
  18.5 12.3 %collective-permute-start.5 = (bf16[1,512,384]{2,1,0:T(8,128)(2,1)S(1)}, bf16[1,512,384]{2,1,0:T(8,128)(2,1)S(1)}, u32[]{:S(2)}, u32[]{:S(2)}) collective-permute-start(bf16[1,512,384]{2,1,0:T(8,128)(2,1)S(1)} %gather.5.refs_1_.refs_0_), channel_id=1, source_target_pairs={{0,2},{1,9},{2,4},{3,11},{4,6},{5,13},{6,0},{7,15},{8,10},{9,17},{... | collective-permute-start | bytes 1179656 | tf_op jit(solution)/shard_map/ppermute | solution.py:31
  18.5 12.3 %collective-permute-start.4 = (bf16[1,512,384]{2,1,0:T(8,128)(2,1)S(1)}, bf16[1,512,384]{2,1,0:T(8,128)(2,1)S(1)}, u32[]{:S(2)}, u32[]{:S(2)}) collective-permute-start(bf16[1,512,384]{2,1,0:T(8,128)(2,1)S(1)} %gather.5.refs_1_.refs_0_), channel_id=1, source_target_pairs={{0,4},{1,17},{2,6},{3,19},{4,0},{5,21},{6,2},{7,23},{8,12},{9,25},... | collective-permute-start | bytes 1179656 | tf_op jit(solution)/shard_map/ppermute | solution.py:31
  31.0 4.2 %collective-permute-start.8 = (bf16[4,512,384]{2,1,0:T(8,128)(2,1)S(1)}, bf16[4,512,384]{2,1,0:T(8,128)(2,1)S(1)}, u32[]{:S(2)}, u32[]{:S(2)}) collective-permute-start(bf16[4,512,384]{2,1,0:T(8,128)(2,1)S(1)} %gather.6.refs_0_), channel_id=1, source_target_pairs={{0,1},{1,0},{2,3},{3,2},{4,5},{5,4},{6,7},{7,6},{8,9},{9,8},{10,11... | collective-permute-start | bytes 4718600 | tf_op jit(solution)/shard_map/ppermute | solution.py:35
  31.8 19.6 %collective-permute-start.10 = (bf16[4,512,384]{2,1,0:T(8,128)(2,1)S(1)}, bf16[4,512,384]{2,1,0:T(8,128)(2,1)S(1)}, u32[]{:S(2)}, u32[]{:S(2)}) collective-permute-start(bf16[4,512,384]{2,1,0:T(8,128)(2,1)S(1)} %gather.6.refs_0_), channel_id=1, source_target_pairs={{0,24},{1,7},{2,26},{3,1},{4,28},{5,3},{6,30},{7,5},{8,0},{9,15},{... | collective-permute-start | bytes 4718600 | tf_op jit(solution)/shard_map/ppermute | solution.py:27
  33.3 20.8 %collective-permute-start.7 = (bf16[4,512,384]{2,1,0:T(8,128)(2,1)S(1)}, bf16[4,512,384]{2,1,0:T(8,128)(2,1)S(1)}, u32[]{:S(2)}, u32[]{:S(2)}) collective-permute-start(bf16[4,512,384]{2,1,0:T(8,128)(2,1)S(1)} %gather.6.refs_0_), channel_id=1, source_target_pairs={{0,8},{1,3},{2,10},{3,5},{4,12},{5,7},{6,14},{7,1},{8,16},{9,11},{... | collective-permute-start | bytes 4718600 | tf_op jit(solution)/shard_map/ppermute | solution.py:27
  54.3 8.5 %collective-permute-start.11 = (bf16[4,512,384]{2,1,0:T(8,128)(2,1)S(1)}, bf16[4,512,384]{2,1,0:T(8,128)(2,1)S(1)}, u32[]{:S(2)}, u32[]{:S(2)}) collective-permute-start(bf16[4,512,384]{2,1,0:T(8,128)(2,1)S(1)} %collective-permute-done.7.refs_0_), channel_id=1, source_target_pairs={{0,1},{1,0},{2,3},{3,2},{4,5},{5,4},{6,7},{7,6},{8,9},{9,8},{10,11... | collective-permute-start | bytes 4718600 | tf_op jit(solution)/shard_map/ppermute | solution.py:35
  57.8 5.3 %collective-permute-start.12 = (bf16[4,512,384]{2,1,0:T(8,128)(2,1)S(1)}, bf16[4,512,384]{2,1,0:T(8,128)(2,1)S(1)}, u32[]{:S(2)}, u32[]{:S(2)}) collective-permute-start(bf16[4,512,384]{2,1,0:T(8,128)(2,1)S(1)} %collective-permute-done.10.refs_0_.refs_1_), channel_id=1, source_target_pairs={{0,1},{1,0},{2,3},{3,2},{4,5},{5,4},{6,7},{7,6},{8,9},{9,8},{10,11... | collective-permute-start | bytes 4718600 | tf_op jit(solution)/shard_map/ppermute | solution.py:35
  57.9 11.1 %collective-permute-start.14 = (bf16[2,512,384]{2,1,0:T(8,128)(2,1)S(1)}, bf16[2,512,384]{2,1,0:T(8,128)(2,1)S(1)}, u32[]{:S(2)}, u32[]{:S(2)}) collective-permute-start(bf16[2,512,384]{2,1,0:T(8,128)(2,1)S(1)} %gather.8.refs_7_), channel_id=1, source_target_pairs={{0,24},{1,7},{2,26},{3,1},{4,28},{5,3},{6,30},{7,5},{8,0},{9,15},{... | collective-permute-start | bytes 2359304 | tf_op jit(solution)/shard_map/ppermute | solution.py:27
  57.9 12.3 %collective-permute-start.9 = (bf16[2,512,384]{2,1,0:T(8,128)(2,1)S(1)}, bf16[2,512,384]{2,1,0:T(8,128)(2,1)S(1)}, u32[]{:S(2)}, u32[]{:S(2)}) collective-permute-start(bf16[2,512,384]{2,1,0:T(8,128)(2,1)S(1)} %gather.7.refs_6_), channel_id=1, source_target_pairs={{0,8},{1,3},{2,10},{3,5},{4,12},{5,7},{6,14},{7,1},{8,16},{9,11},{... | collective-permute-start | bytes 2359304 | tf_op jit(solution)/shard_map/ppermute | solution.py:27
  70.3 5.3 %collective-permute-start.13 = (bf16[2,512,384]{2,1,0:T(8,128)(2,1)S(1)}, bf16[2,512,384]{2,1,0:T(8,128)(2,1)S(1)}, u32[]{:S(2)}, u32[]{:S(2)}) collective-permute-start(bf16[2,512,384]{2,1,0:T(8,128)(2,1)S(1)} %collective-permute-done.9.refs_0_), channel_id=1, source_target_pairs={{0,1},{1,0},{2,3},{3,2},{4,5},{5,4},{6,7},{7,6},{8,9},{9,8},{10,11... | collective-permute-start | bytes 2359304 | tf_op jit(solution)/shard_map/ppermute | solution.py:35
  71.5 4.0 %collective-permute-start.15 = (bf16[2,512,384]{2,1,0:T(8,128)(2,1)S(1)}, bf16[2,512,384]{2,1,0:T(8,128)(2,1)S(1)}, u32[]{:S(2)}, u32[]{:S(2)}) collective-permute-start(bf16[2,512,384]{2,1,0:T(8,128)(2,1)S(1)} %collective-permute-done.14.refs_1_), channel_id=1, source_target_pairs={{0,1},{1,0},{2,3},{3,2},{4,5},{5,4},{6,7},{7,6},{8,9},{9,8},{10,11... | collective-permute-start | bytes 2359304 | tf_op jit(solution)/shard_map/ppermute | solution.py:35
  75.0 5.2 %collective-permute-start.16 = (bf16[4,512,384]{2,1,0:T(8,128)(2,1)S(1)}, bf16[4,512,384]{2,1,0:T(8,128)(2,1)S(1)}, u32[]{:S(2)}, u32[]{:S(2)}) collective-permute-start(bf16[4,512,384]{2,1,0:T(8,128)(2,1)S(1)} %down.10.refs_6_), channel_id=1, source_target_pairs={{0,1},{1,0},{2,3},{3,2},{4,5},{5,4},{6,7},{7,6},{8,9},{9,8},{10,11... | collective-permute-start | bytes 4718600 | tf_op jit(solution)/shard_map/ppermute | solution.py:35
  78.5 7.1 %collective-permute-start.18 = (bf16[4,512,384]{2,1,0:T(8,128)(2,1)S(1)}, bf16[4,512,384]{2,1,0:T(8,128)(2,1)S(1)}, u32[]{:S(2)}, u32[]{:S(2)}) collective-permute-start(bf16[4,512,384]{2,1,0:T(8,128)(2,1)S(1)} %down.11.rest_1_), channel_id=1, source_target_pairs={{0,1},{1,0},{2,3},{3,2},{4,5},{5,4},{6,7},{7,6},{8,9},{9,8},{10,11... | collective-permute-start | bytes 4718600 | tf_op jit(solution)/shard_map/ppermute | solution.py:35
  79.6 15.0 %collective-permute-start.20 = (bf16[4,512,384]{2,1,0:T(8,128)(2,1)S(1)}, bf16[4,512,384]{2,1,0:T(8,128)(2,1)S(1)}, u32[]{:S(2)}, u32[]{:S(2)}) collective-permute-start(bf16[4,512,384]{2,1,0:T(8,128)(2,1)S(1)} %down.12.rest_2_), channel_id=1, source_target_pairs={{0,1},{1,0},{2,3},{3,2},{4,5},{5,4},{6,7},{7,6},{8,9},{9,8},{10,11... | collective-permute-start | bytes 4718600 | tf_op jit(solution)/shard_map/ppermute | solution.py:35
  81.2 12.4 %collective-permute-start.19 = (bf16[2,512,384]{2,1,0:T(8,128)(2,1)S(1)}, bf16[2,512,384]{2,1,0:T(8,128)(2,1)S(1)}, u32[]{:S(2)}, u32[]{:S(2)}) collective-permute-start(bf16[2,512,384]{2,1,0:T(8,128)(2,1)S(1)} %get-tuple-element.70.rest_0_), channel_id=1, source_target_pairs={{0,8},{1,3},{2,10},{3,5},{4,12},{5,7},{6,14},{7,1},{8,16},{9,11},{... | collective-permute-start | bytes 2359304 | tf_op jit(solution)/shard_map/ppermute | solution.py:27
  81.3 13.3 %collective-permute-start.21 = (bf16[2,512,384]{2,1,0:T(8,128)(2,1)S(1)}, bf16[2,512,384]{2,1,0:T(8,128)(2,1)S(1)}, u32[]{:S(2)}, u32[]{:S(2)}) collective-permute-start(bf16[2,512,384]{2,1,0:T(8,128)(2,1)S(1)} %get-tuple-element.71), channel_id=1, source_target_pairs={{0,24},{1,7},{2,26},{3,1},{4,28},{5,3},{6,30},{7,5},{8,0},{9,15},{... | collective-permute-start | bytes 2359304 | tf_op jit(solution)/shard_map/ppermute | solution.py:27
  84.9 14.6 %collective-permute-start.17 = (bf16[4,512,384]{2,1,0:T(8,128)(2,1)S(1)}, bf16[4,512,384]{2,1,0:T(8,128)(2,1)S(1)}, u32[]{:S(2)}, u32[]{:S(2)}) collective-permute-start(bf16[4,512,384]{2,1,0:T(8,128)(2,1)S(1)} %down.14), channel_id=1, source_target_pairs={{0,1},{1,0},{2,3},{3,2},{4,5},{5,4},{6,7},{7,6},{8,9},{9,8},{10,11... | collective-permute-start | bytes 4718600 | tf_op jit(solution)/shard_map/ppermute | solution.py:35
  94.5 16.6 %collective-permute-start.22 = (bf16[3,512,384]{2,1,0:T(8,128)(2,1)S(1)}, bf16[3,512,384]{2,1,0:T(8,128)(2,1)S(1)}, u32[]{:S(2)}, u32[]{:S(2)}) collective-permute-start(bf16[3,512,384]{2,1,0:T(8,128)(2,1)S(1)} %down.15.rest_1_.rest_2_), channel_id=1, source_target_pairs={{0,8},{1,3},{2,10},{3,5},{4,12},{5,7},{6,14},{7,1},{8,16},{9,11},{... | collective-permute-start | bytes 3538952 | tf_op jit(solution)/shard_map/ppermute | solution.py:27
  95.7 16.1 %collective-permute-start.23 = (bf16[3,512,384]{2,1,0:T(8,128)(2,1)S(1)}, bf16[3,512,384]{2,1,0:T(8,128)(2,1)S(1)}, u32[]{:S(2)}, u32[]{:S(2)}) collective-permute-start(bf16[3,512,384]{2,1,0:T(8,128)(2,1)S(1)} %down.16.rest_2_.rest_3_), channel_id=1, source_target_pairs={{0,24},{1,7},{2,26},{3,1},{4,28},{5,3},{6,30},{7,5},{8,0},{9,15},{... | collective-permute-start | bytes 3538952 | tf_op jit(solution)/shard_map/ppermute | solution.py:27
  112.2 8.6 %collective-permute-start.24 = (bf16[1,512,384]{2,1,0:T(8,128)(2,1)S(1)}, bf16[1,512,384]{2,1,0:T(8,128)(2,1)S(1)}, u32[]{:S(2)}, u32[]{:S(2)}) collective-permute-start(bf16[1,512,384]{2,1,0:T(8,128)(2,1)S(1)} %get-tuple-element.75), channel_id=1, source_target_pairs={{0,8},{1,3},{2,10},{3,5},{4,12},{5,7},{6,14},{7,1},{8,16},{9,11},{... | collective-permute-start | bytes 1179656 | tf_op jit(solution)/shard_map/ppermute | solution.py:27
  112.3 13.1 %collective-permute-start.25 = (bf16[1,512,384]{2,1,0:T(8,128)(2,1)S(1)}, bf16[1,512,384]{2,1,0:T(8,128)(2,1)S(1)}, u32[]{:S(2)}, u32[]{:S(2)}) collective-permute-start(bf16[1,512,384]{2,1,0:T(8,128)(2,1)S(1)} %get-tuple-element.76), channel_id=1, source_target_pairs={{0,24},{1,7},{2,26},{3,1},{4,28},{5,3},{6,30},{7,5},{8,0},{9,15},{... | collective-permute-start | bytes 1179656 | tf_op jit(solution)/shard_map/ppermute | solution.py:27
  115.4 11.5 %collective-permute-start.26 = (bf16[512,384]{1,0:T(8,128)(2,1)S(1)}, bf16[512,384]{1,0:T(8,128)(2,1)S(1)}, u32[]{:S(2)}, u32[]{:S(2)}) collective-permute-start(bf16[512,384]{1,0:T(8,128)(2,1)S(1)} %get-tuple-element.77), channel_id=1, source_target_pairs={{0,4},{1,17},{2,6},{3,19},{4,0},{5,21},{6,2},{7,23},{8,12},{9,25},... | collective-permute-start | bytes 1179656 | tf_op jit(solution)/shard_map/ppermute | solution.py:31
  115.7 14.2 %collective-permute-start.28 = (bf16[512,384]{1,0:T(8,128)(2,1)S(1)}, bf16[512,384]{1,0:T(8,128)(2,1)S(1)}, u32[]{:S(2)}, u32[]{:S(2)}) collective-permute-start(bf16[512,384]{1,0:T(8,128)(2,1)S(1)} %get-tuple-element.78), channel_id=1, source_target_pairs={{0,6},{1,25},{2,0},{3,27},{4,2},{5,29},{6,4},{7,31},{8,14},{9,1},{... | collective-permute-start | bytes 1179656 | tf_op jit(solution)/shard_map/ppermute | solution.py:31
  118.1 13.4 %collective-permute-start.27 = (bf16[512,384]{1,0:T(8,128)(2,1)S(1)}, bf16[512,384]{1,0:T(8,128)(2,1)S(1)}, u32[]{:S(2)}, u32[]{:S(2)}) collective-permute-start(bf16[512,384]{1,0:T(8,128)(2,1)S(1)} %get-tuple-element.74.refs_2_), channel_id=1, source_target_pairs={{0,2},{1,9},{2,4},{3,11},{4,6},{5,13},{6,0},{7,15},{8,10},{9,17},{... | collective-permute-start | bytes 1179656 | tf_op jit(solution)/shard_map/ppermute | solution.py:31
  131.8 6.0 %collective-permute-start.29 = (bf16[128,384]{1,0:T(8,128)(2,1)S(1)}, bf16[128,384]{1,0:T(8,128)(2,1)S(1)}, u32[]{:S(2)}, u32[]{:S(2)}) collective-permute-start(bf16[128,384]{1,0:T(8,128)(2,1)S(1)} %get-tuple-element.81), channel_id=1, source_target_pairs={{0,64},{32,96},{64,0},{96,32},{1,65},{33,97},{65,1},{97,33},{2,66}... | collective-permute-start | bytes 294920 | tf_op jit(solution)/shard_map/ppermute | solution.py:39
  132.2 8.1 %collective-permute-start.31 = (bf16[128,384]{1,0:T(8,128)(2,1)S(1)}, bf16[128,384]{1,0:T(8,128)(2,1)S(1)}, u32[]{:S(2)}, u32[]{:S(2)}) collective-permute-start(bf16[128,384]{1,0:T(8,128)(2,1)S(1)} %get-tuple-element.82), channel_id=1, source_target_pairs={{0,32},{32,64},{64,96},{96,0},{1,33},{33,65},{65,97},{97,1},{2,34}... | collective-permute-start | bytes 294920 | tf_op jit(solution)/shard_map/ppermute | solution.py:39
  133.4 6.9 %collective-permute-start.30 = (bf16[128,384]{1,0:T(8,128)(2,1)S(1)}, bf16[128,384]{1,0:T(8,128)(2,1)S(1)}, u32[]{:S(2)}, u32[]{:S(2)}) collective-permute-start(bf16[128,384]{1,0:T(8,128)(2,1)S(1)} %get-tuple-element.83), channel_id=1, source_target_pairs={{0,96},{32,0},{64,32},{96,64},{1,97},{33,1},{65,33},{97,65},{2,98}... | collective-permute-start | bytes 294920 | tf_op jit(solution)/shard_map/ppermute | solution.py:39
  140.5 1.5 %collective-permute-start.32 = (bf16[128,192]{1,0:T(8,128)(2,1)S(1)}, bf16[128,192]{1,0:T(8,128)(2,1)S(1)}, u32[]{:S(2)}, u32[]{:S(2)}) collective-permute-start(bf16[128,192]{1,0:T(8,128)(2,1)S(1)} %broadcast_select_fusion.1), channel_id=1, source_target_pairs={{0,1},{1,0},{2,3},{3,2},{4,5},{5,4},{6,7},{7,6},{8,9},{9,8},{10,11... | collective-permute-start | bytes 147464 | tf_op jit(solution)/shard_map/ppermute | solution.py:35

commit v4 on v3

--- a/solution.py
+++ b/solution.py
@@ -277,8 +277,12 @@
     other_sum, t1 = up([other_line], at(-1, 1, 0), None, False, [t0])
     right, left = after(right, t1), after(left, t1)
     shape = (two,) + line.shape[1:]
-    (send_a,) = gather_call([right], [shape], [[(0, slice(None), slice(two))]], [t1])
-    (send_b,) = gather_call([left], [shape], [[(0, slice(None), slice(two, SIDE))]], [t1])
+    send_a, send_b = gather_call(
+        [right, left],
+        [shape] * 2,
+        [[(0, slice(None), slice(two))], [(1, slice(None), slice(two, SIDE))]],
+        [t1],
+    )
     far_a, far_b = move_bulk(send_a, 1), move_bulk(send_b, 3)
     other_near = [move_core(after(right, send_a, send_b)), move_core(after(left, send_a, send_b))]
     own_sum, t0 = up([right, left], at(-1, 0, 1) + at(-1, 0, 3), own_sum, False, [send_a, send_b])
@@ -292,10 +296,11 @@
     (h_other,), t1 = up(other_far, at(-1, 1, 2), other_sum, True, [send2])
     (send1,) = down(h_own, at(1, 1, 1), [], [SIDE], BF, [t1])
     (send3,) = down(h_own, at(1, 1, 3), [], [SIDE], BF, [t1])
+    (send0,) = down(h_own, at(1, 1, 0), [], [SIDE], BF, [send1, send3])
     sent1, sent3 = move_core(send1), move_core(send3)
     m2a, m2b = down(h_other, at(1, 0, 2), [(sent2, 0)], [two, two], BF, [send1, send3])
     step_a, step_b = move_bulk(m2a, 1), move_bulk(m2b, 3)
-    sent0 = move_core(down(h_own, at(1, 1, 0), [], [SIDE], BF, [m2a])[0])
+    sent0 = move_core(after(send0, m2a))
     others = range(1, SIDE)
     (m1,) = down(h_other, at(1, 0, 1, others), [(sent1, 1), (step_a, 1)], [SIDE - 1])
     (m3,) = down(h_other, at(1, 0, 3, others), [(sent3, 1), (step_b, 1 - two)], [SIDE - 1])
@@ -305,8 +310,7 @@
     m0_own, m0 = down(h_other, at(1, 0, 0), [(sent0, 0)], [1, SIDE - 1], F32, [m1, m3])
     s1, s2, s3 = add_call(m0, n1, n3)
     moved = [move_small(s2, 2), move_small(s1, 1), move_small(s3, 3)]
-    own1, own3 = gather_call([m1_own, m3_own], [m1_own.shape] * 2, [[(0, ..., ...)], [(1, ..., ...)]], [s1])
-    n1_own, n3_own = move_bulk(own1, 1), move_bulk(own3, 3)
+    n1_own, n3_own = move_bulk(after(m1_own, n1), 1), move_bulk(after(m3_own, n3), 3)
     plane = fsum([m0_own[0], n1_own[0], n3_own[0]] + moved).astype(BF)
     plane = plane.reshape(SIDE, rows, 2 * half)
 

time: 143 us -> 141 us (0.986)
  waiting for transfers between devices: 69 us -> 65.2 us
  starting transfers between devices: 37.1 us -> 39.3 us
    ppermute x11, starting transfers between devices: 9.77 us -> 11.7 us  [move_core(): return lax.ppermute(v, 'blk', [(i, i ^ 1) for i in range(2 * SIDE * SIDE)])]
    ppermute x6, waiting for transfers between devices: 6.63 us -> 4.71 us  [move_expert(): lax.ppermute(v, 'expert', [(i, (i + shift) % SIDE) for i in range(SIDE)])]
    ppermute x10, waiting for transfers between devices: 46.8 us -> 45.3 us  [move_bulk(): return lax.ppermute(v, 'blk', blk_perm(True, shift))]
  transfers between devices with their start and end apart: 33 -> 33, of which waited for: 19 -> 17; matrix products, arithmetic and copies ran while one was open for 1% -> 1% of each run, Pallas kernels for 22% -> 23%
where the time goes in v4:
time: 141 us
  waiting for transfers between devices  65.2 us (46%)
  starting transfers between devices  39.3 us (28%)
  Pallas kernels  32.4 us (23%)
  other arithmetic  2.31 us (2%)
  local copies, waits for them, and re-layouts  1.78 us (1%)
    ppermute x10, waiting for transfers between devices, move_bulk(): return lax.ppermute(v, 'blk', blk_perm(True, shift))  45.3 us
    pallas_call x6, Pallas kernels, up_call(): pl.pallas_call(kernel, in_specs=[SMEM] + [VMEM] * len(args) + [ANY] * len...  15.5 us
    ppermute x6, waiting for transfers between devices, move_small(): return lax.ppermute(v, 'blk', blk_perm(False, shift))  14 us
    ppermute x10, starting transfers between devices, move_bulk(): return lax.ppermute(v, 'blk', blk_perm(True, shift))  11.8 us
    ppermute x11, starting transfers between devices, move_core(): return lax.ppermute(v, 'blk', [(i, i ^ 1) for i in range(2 * SIDE * SIDE)])  11.7 us
    pallas_call x10, Pallas kernels, down_call(): pl.pallas_call(kernel, in_specs=[SMEM] + [VMEM] * len(args) + [ANY] * len...  8.9 us
    ppermute x6, starting transfers between devices, move_small(): return lax.ppermute(v, 'blk', blk_perm(False, shift))  8.18 us
    ppermute x6, starting transfers between devices, move_expert(): lax.ppermute(v, 'expert', [(i, (i + shift) % SIDE) for i in range(SIDE)])  7.58 us
  transfers between devices with their start and end apart: 33, of which 17 were waited for; matrix products, arithmetic and copies ran while one was open for 1% of the time, Pallas kernels for 23%

profile of v4, /device:TPU:1, one launch (start us, length us, event | category | flops | bytes accessed | tf_op | source)
XLA Modules:
  0.0 141.3 jit_solution(13393475118298574722)
XLA Ops:
  0.0 1.0 copy.7
  1.0 1.5 %collective-permute-start = (bf16[128,192]{1,0:T(8,128)(2,1)S(1)}, bf16[128,192]{1,0:T(8,128)(2,1)S(1)}, u32[]{:S(2)}, u32[]{:S(2)}) collective-permute-start(bf16[128,192]{1,0:T(8,128)(2,1)S(1)} %get-tuple-element.93), channel_id=1, source_target_pairs={{0,1},{1,0},{2,3},{3,2},{4,5},{5,4},{6,7},{7,6},{8,9},{9,8},{10,11... | collective-permute-start | bytes 147464 | tf_op jit(solution)/shard_map/ppermute | solution.py:35
  2.5 0.7 select_bitcast_fusion.4
  3.2 0.8 broadcast_subtract_fusion
  4.1 2.9 %collective-permute-start.3 = (bf16[128,384]{1,0:T(8,128)(2,1)S(1)}, bf16[128,384]{1,0:T(8,128)(2,1)S(1)}, u32[]{:S(2)}, u32[]{:S(2)}) collective-permute-start(bf16[128,384]{1,0:T(8,128)(2,1)S(1)} %maximum_select_fusion.refs_2_.refs_0_), channel_id=1, source_target_pairs={{0,96},{32,0},{64,32},{96,64},{1,97},{33,1},{65,33},{97,65},{2,98}... | collective-permute-start | bytes 294920 | tf_op jit(solution)/shard_map/ppermute | solution.py:39
  7.0 1.6 %collective-permute-start.1 = (bf16[128,384]{1,0:T(8,128)(2,1)S(1)}, bf16[128,384]{1,0:T(8,128)(2,1)S(1)}, u32[]{:S(2)}, u32[]{:S(2)}) collective-permute-start(bf16[128,384]{1,0:T(8,128)(2,1)S(1)} %maximum_select_fusion.refs_2_.refs_0_), channel_id=1, source_target_pairs={{0,64},{32,96},{64,0},{96,32},{1,65},{33,97},{65,1},{97,33},{2,66}... | collective-permute-start | bytes 294920 | tf_op jit(solution)/shard_map/ppermute | solution.py:39
  8.7 4.6 %load.2 = (bf16[6144,512]{1,0:T(8,128)(2,1)S(1)}, bf16[6144,512]{1,0:T(8,128)(2,1)S(1)}, f32[8,128]{1,0:T(8,128)S(1)}) custom-call(bf16[6144,512]{1,0:T(8,128)(2,1)} %bitcast.38, bf16[6144,512]{1,0:T(8,128)(2,1)} %bitcast.39, bf16[128,384]{1,0:T(8,128)(2,1)S(1)} %maximum_select_fusion.refs_2_.refs_0_, f32[4,128]{1,0:T(4,128)S(1)} %select_add_fusion.refs_3_), custom_call_target="tpu_custom_call" | custom-call | bytes 25165824 | tf_op jit(solution)/shard_map/load/pallas_call | solution.py:163
  13.4 1.3 collective-permute-done.2.refs_2_
  14.7 3.8 %collective-permute-start.6 = (bf16[1,512,384]{2,1,0:T(8,128)(2,1)S(1)}, bf16[1,512,384]{2,1,0:T(8,128)(2,1)S(1)}, u32[]{:S(2)}, u32[]{:S(2)}) collective-permute-start(bf16[1,512,384]{2,1,0:T(8,128)(2,1)S(1)} %gather.3.refs_1_.refs_0_), channel_id=1, source_target_pairs={{0,6},{1,25},{2,0},{3,27},{4,2},{5,29},{6,4},{7,31},{8,14},{9,1},{... | collective-permute-start | bytes 1179656 | tf_op jit(solution)/shard_map/ppermute | solution.py:31
  18.5 1.3 collective-permute-start.4
  19.8 2.8 %load.3 = (bf16[512,6144]{1,0:T(8,128)(2,1)S(1)}, f32[8,128]{1,0:T(8,128)S(1)}) custom-call(bf16[512,6144]{1,0:T(8,128)(2,1)} %bitcast.37, bf16[1,512,384]{2,1,0:T(8,128)(2,1)S(1)} %gather.3.refs_1_.refs_0_), custom_call_target="tpu_custom_call" | custom-call | bytes 12582912 | tf_op jit(solution)/shard_map/load/pallas_call | solution.py:163
  22.6 4.8 %collective-permute-done.6.refs_3_ = bf16[1,512,384]{2,1,0:T(8,128)(2,1)S(1)} collective-permute-done((bf16[1,512,384]{2,1,0:T(8,128)(2,1)S(1)}, bf16[1,512,384]{2,1,0:T(8,128)(2,1)S(1)}, u32[]{:S(2)}, u32[]{:S(2)}) %collective-permute-start.6) | collective-permute-done | bytes 393248 | tf_op jit(solution)/shard_map/ppermute | solution.py:31
  27.4 3.4 %collective-permute-done.5.refs_2_ = bf16[1,512,384]{2,1,0:T(8,128)(2,1)S(1)} collective-permute-done((bf16[1,512,384]{2,1,0:T(8,128)(2,1)S(1)}, bf16[1,512,384]{2,1,0:T(8,128)(2,1)S(1)}, u32[]{:S(2)}, u32[]{:S(2)}) %collective-permute-start.5) | collective-permute-done | bytes 393248 | tf_op jit(solution)/shard_map/ppermute | solution.py:31
  31.0 0.9 collective-permute-start.8
  31.8 1.5 %collective-permute-start.9 = (bf16[4,512,384]{2,1,0:T(8,128)(2,1)S(1)}, bf16[4,512,384]{2,1,0:T(8,128)(2,1)S(1)}, u32[]{:S(2)}, u32[]{:S(2)}) collective-permute-start(bf16[4,512,384]{2,1,0:T(8,128)(2,1)S(1)} %gather.4.refs_0_), channel_id=1, source_target_pairs={{0,24},{1,7},{2,26},{3,1},{4,28},{5,3},{6,30},{7,5},{8,0},{9,15},{... | collective-permute-start | bytes 4718600 | tf_op jit(solution)/shard_map/ppermute | solution.py:27
  33.3 1.8 %up.6 = (f32[512,512]{1,0:T(8,128)S(1)}, f32[512,512]{1,0:T(8,128)S(1)}, f32[8,128]{1,0:T(8,128)S(1)}) custom-call(s32[1]{0:T(128)} %bitcast.5.place_ref, bf16[4,512,384]{2,1,0:T(8,128)(2,1)S(1)} %gather.4.refs_0_, bf16[6144,512]{1,0:T(8,128)(2,1)S(1)} %get-tuple-element.49.refs_1_.refs_2_, bf16[6144,512]{1,0:T(8,128)(2,1)S(1)} %get-tuple-element.50.refs_2_.refs_3_), custom_call_target="tpu_custom_call" | custom-call | flops 1610612736 | bytes 6815744 | tf_op jit(solution)/shard_map/up/pallas_call | solution.py:98
  35.2 1.8 %up.7 = (f32[512,512]{1,0:T(8,128)S(1)}, f32[512,512]{1,0:T(8,128)S(1)}, f32[8,128]{1,0:T(8,128)S(1)}) custom-call(s32[1]{0:T(128)} %bitcast.5.place_ref, bf16[4,512,384]{2,1,0:T(8,128)(2,1)S(1)} %collective-permute-done.8.refs_0_, bf16[6144,512]{1,0:T(8,128)(2,1)S(1)} %get-tuple-element.49.refs_1_.refs_2_, ...), custom_call_target="tpu_custom_call" | custom-call | flops 1610612736 | bytes 6815744 | tf_op jit(solution)/shard_map/up/pallas_call | solution.py:98
  37.0 14.4 %collective-permute-done.9.refs_1_ = bf16[4,512,384]{2,1,0:T(8,128)(2,1)S(1)} collective-permute-done((bf16[4,512,384]{2,1,0:T(8,128)(2,1)S(1)}, bf16[4,512,384]{2,1,0:T(8,128)(2,1)S(1)}, u32[]{:S(2)}, u32[]{:S(2)}) %collective-permute-start.9) | collective-permute-done | bytes 1572896 | tf_op jit(solution)/shard_map/ppermute | solution.py:27
  51.4 2.7 %collective-permute-done.7.refs_0_ = bf16[4,512,384]{2,1,0:T(8,128)(2,1)S(1)} collective-permute-done((bf16[4,512,384]{2,1,0:T(8,128)(2,1)S(1)}, bf16[4,512,384]{2,1,0:T(8,128)(2,1)S(1)}, u32[]{:S(2)}, u32[]{:S(2)}) %collective-permute-start.7) | collective-permute-done | bytes 1572896 | tf_op jit(solution)/shard_map/ppermute | solution.py:27
  54.2 3.6 %collective-permute-start.11 = (bf16[4,512,384]{2,1,0:T(8,128)(2,1)S(1)}, bf16[4,512,384]{2,1,0:T(8,128)(2,1)S(1)}, u32[]{:S(2)}, u32[]{:S(2)}) collective-permute-start(bf16[4,512,384]{2,1,0:T(8,128)(2,1)S(1)} %collective-permute-done.7.refs_0_), channel_id=1, source_target_pairs={{0,1},{1,0},{2,3},{3,2},{4,5},{5,4},{6,7},{7,6},{8,9},{9,8},{10,11... | collective-permute-start | bytes 4718600 | tf_op jit(solution)/shard_map/ppermute | solution.py:35
  57.9 1.5 %collective-permute-start.10 = (bf16[2,512,384]{2,1,0:T(8,128)(2,1)S(1)}, bf16[2,512,384]{2,1,0:T(8,128)(2,1)S(1)}, u32[]{:S(2)}, u32[]{:S(2)}) collective-permute-start(bf16[2,512,384]{2,1,0:T(8,128)(2,1)S(1)} %get-tuple-element.55.refs_6_), channel_id=1, source_target_pairs={{0,8},{1,3},{2,10},{3,5},{4,12},{5,7},{6,14},{7,1},{8,16},{9,11},{... | collective-permute-start | bytes 2359304 | tf_op jit(solution)/shard_map/ppermute | solution.py:27
  59.4 3.5 %up.8 = (f32[512,512]{1,0:T(8,128)S(1)}, f32[512,512]{1,0:T(8,128)S(1)}, f32[8,128]{1,0:T(8,128)S(1)}) custom-call(s32[1]{0:T(128)} %bitcast.5.place_ref, bf16[4,512,384]{2,1,0:T(8,128)(2,1)S(1)} %collective-permute-done.7.refs_0_, bf16[4,512,384]{2,1,0:T(8,128)(2,1)S(1)} %collective-permute-done.9.refs_1_, ...), custom_call_target="tpu_custom_call" | custom-call | flops 3221225472 | bytes 11534336 | tf_op jit(solution)/shard_map/up/pallas_call | solution.py:98
  62.9 0.2 collective-permute-done.12.refs_1_
  63.1 4.0 %up.9 = (f32[512,512]{1,0:T(8,128)S(1)}, f32[512,512]{1,0:T(8,128)S(1)}, f32[8,128]{1,0:T(8,128)}) custom-call(s32[1]{0:T(128)} %bitcast.5.place_ref, bf16[4,512,384]{2,1,0:T(8,128)(2,1)S(1)} %collective-permute-done.11.refs_0_, bf16[4,512,384]{2,1,0:T(8,128)(2,1)S(1)} %collective-permute-done.12.refs_1_, ...), custom_call_target="tpu_custom_call" | custom-call | flops 3221225472 | bytes 11534336 | tf_op jit(solution)/shard_map/up/pallas_call | solution.py:98
  67.1 2.0 %collective-permute-done.14.refs_1_ = bf16[2,512,384]{2,1,0:T(8,128)(2,1)S(1)} collective-permute-done((bf16[2,512,384]{2,1,0:T(8,128)(2,1)S(1)}, bf16[2,512,384]{2,1,0:T(8,128)(2,1)S(1)}, u32[]{:S(2)}, u32[]{:S(2)}) %collective-permute-start.14) | collective-permute-done | bytes 786464 | tf_op jit(solution)/shard_map/ppermute | solution.py:27
  69.0 1.2 collective-permute-done.10.refs_0_
  70.2 1.3 collective-permute-start.13
  71.5 2.5 %up.10 = (bf16[512,512]{1,0:T(8,128)(2,1)S(1)}, f32[8,128]{1,0:T(8,128)}) custom-call(s32[1]{0:T(128)} %bitcast.5.place_ref, bf16[2,512,384]{2,1,0:T(8,128)(2,1)S(1)} %collective-permute-done.10.refs_0_, bf16[2,512,384]{2,1,0:T(8,128)(2,1)S(1)} %collective-permute-done.14.refs_1_, bf16[6144,512]{1,0:T(8,128)(2,1)S(1)} %get-tuple-element.49.refs_1_.refs_2_, ...), custom_call_target="tpu_custom_call" | custom-call | flops 1610612736 | bytes 6815744 | tf_op jit(solution)/shard_map/up/pallas_call | solution.py:98
  74.0 1.0 down.10.refs_6_
  75.0 0.6 collective-permute-start.16
  75.6 1.9 %up.11 = (bf16[512,512]{1,0:T(8,128)(2,1)S(1)}, f32[8,128]{1,0:T(8,128)S(1)}) custom-call(s32[1]{0:T(128)} %bitcast.5.place_ref, bf16[2,512,384]{2,1,0:T(8,128)(2,1)S(1)} %collective-permute-done.13.refs_0_, bf16[2,512,384]{2,1,0:T(8,128)(2,1)S(1)} %collective-permute-done.15.refs_1_, bf16[6144,512]{1,0:T(8,128)(2,1)S(1)} %get-tuple-element.49.refs_1_.refs_2_, ...), custom_call_target="tpu_custom_call" | custom-call | flops 1610612736 | bytes 6815744 | tf_op jit(solution)/shard_map/up/pallas_call | solution.py:98
  77.5 1.0 down.11.rest_0_.rest_1_
  78.6 1.0 down.12.rest_1_.rest_2_
  79.6 0.5 collective-permute-start.20
  80.2 1.0 down.14
  81.3 2.7 %collective-permute-start.21 = (bf16[2,512,384]{2,1,0:T(8,128)(2,1)S(1)}, bf16[2,512,384]{2,1,0:T(8,128)(2,1)S(1)}, u32[]{:S(2)}, u32[]{:S(2)}) collective-permute-start(bf16[2,512,384]{2,1,0:T(8,128)(2,1)S(1)} %get-tuple-element.77), channel_id=1, source_target_pairs={{0,24},{1,7},{2,26},{3,1},{4,28},{5,3},{6,30},{7,5},{8,0},{9,15},{... | collective-permute-start | bytes 2359304 | tf_op jit(solution)/shard_map/ppermute | solution.py:27
  84.0 1.0 down.13
  85.0 0.7 collective-permute-start.17
  85.7 7.9 %collective-permute-done.19.rest_1_ = bf16[2,512,384]{2,1,0:T(8,128)(2,1)S(1)} collective-permute-done((bf16[2,512,384]{2,1,0:T(8,128)(2,1)S(1)}, bf16[2,512,384]{2,1,0:T(8,128)(2,1)S(1)}, u32[]{:S(2)}, u32[]{:S(2)}) %collective-permute-start.19) | collective-permute-done | bytes 786464 | tf_op jit(solution)/shard_map/ppermute | solution.py:27
  93.6 0.9 down.15.rest_1_.rest_2_
  94.6 1.0 down.16.rest_2_.rest_3_
  95.7 2.9 %collective-permute-start.24 = (bf16[3,512,384]{2,1,0:T(8,128)(2,1)S(1)}, bf16[3,512,384]{2,1,0:T(8,128)(2,1)S(1)}, u32[]{:S(2)}, u32[]{:S(2)}) collective-permute-start(bf16[3,512,384]{2,1,0:T(8,128)(2,1)S(1)} %down.16.rest_2_.rest_3_), channel_id=1, source_target_pairs={{0,24},{1,7},{2,26},{3,1},{4,28},{5,3},{6,30},{7,5},{8,0},{9,15},{... | collective-permute-start | bytes 3538952 | tf_op jit(solution)/shard_map/ppermute | solution.py:27
  98.6 0.4 down.18
  99.0 0.5 down.19
  99.5 1.0 down.17
  100.5 10.6 %collective-permute-done.22.refs_0_ = bf16[3,512,384]{2,1,0:T(8,128)(2,1)S(1)} collective-permute-done((bf16[3,512,384]{2,1,0:T(8,128)(2,1)S(1)}, bf16[3,512,384]{2,1,0:T(8,128)(2,1)S(1)}, u32[]{:S(2)}, u32[]{:S(2)}) %collective-permute-start.22) | collective-permute-done | bytes 1179680 | tf_op jit(solution)/shard_map/ppermute | solution.py:27
  111.2 0.6 collective-permute-done.24.refs_1_
  111.7 3.1 %collective-permute-start.25 = (bf16[1,512,384]{2,1,0:T(8,128)(2,1)S(1)}, bf16[1,512,384]{2,1,0:T(8,128)(2,1)S(1)}, u32[]{:S(2)}, u32[]{:S(2)}) collective-permute-start(bf16[1,512,384]{2,1,0:T(8,128)(2,1)S(1)} %down.19), channel_id=1, source_target_pairs={{0,24},{1,7},{2,26},{3,1},{4,28},{5,3},{6,30},{7,5},{8,0},{9,15},{... | collective-permute-start | bytes 1179656 | tf_op jit(solution)/shard_map/ppermute | solution.py:27
  114.9 0.4 add.94
  115.2 0.4 collective-permute-start.26
  115.6 0.3 collective-permute-start.27
  115.9 2.4 %collective-permute-start.28 = (bf16[512,384]{1,0:T(8,128)(2,1)S(1)}, bf16[512,384]{1,0:T(8,128)(2,1)S(1)}, u32[]{:S(2)}, u32[]{:S(2)}) collective-permute-start(bf16[512,384]{1,0:T(8,128)(2,1)S(1)} %get-tuple-element.84), channel_id=1, source_target_pairs={{0,6},{1,25},{2,0},{3,27},{4,2},{5,29},{6,4},{7,31},{8,14},{9,1},{... | collective-permute-start | bytes 1179656 | tf_op jit(solution)/shard_map/ppermute | solution.py:31
  118.3 1.0 collective-permute-done.23
  119.3 4.8 %collective-permute-done.25 = bf16[1,512,384]{2,1,0:T(8,128)(2,1)S(1)} collective-permute-done((bf16[1,512,384]{2,1,0:T(8,128)(2,1)S(1)}, bf16[1,512,384]{2,1,0:T(8,128)(2,1)S(1)}, u32[]{:S(2)}, u32[]{:S(2)}) %collective-permute-start.25) | collective-permute-done | bytes 393248 | tf_op jit(solution)/shard_map/ppermute | solution.py:27
  124.1 5.8 %collective-permute-done.27 = bf16[512,384]{1,0:T(8,128)(2,1)S(1)} collective-permute-done((bf16[512,384]{1,0:T(8,128)(2,1)S(1)}, bf16[512,384]{1,0:T(8,128)(2,1)S(1)}, u32[]{:S(2)}, u32[]{:S(2)}) %collective-permute-start.27) | collective-permute-done | bytes 393248 | tf_op jit(solution)/shard_map/ppermute | solution.py:31
  129.9 0.3 fusion.2
  130.3 0.4 collective-permute-start.29
  130.6 1.1 collective-permute-start.31
  131.8 1.5 %collective-permute-start.30 = (bf16[128,384]{1,0:T(8,128)(2,1)S(1)}, bf16[128,384]{1,0:T(8,128)(2,1)S(1)}, u32[]{:S(2)}, u32[]{:S(2)}) collective-permute-start(bf16[128,384]{1,0:T(8,128)(2,1)S(1)} %get-tuple-element.89), channel_id=1, source_target_pairs={{0,96},{32,0},{64,32},{96,64},{1,97},{33,1},{65,33},{97,65},{2,98}... | collective-permute-start | bytes 294920 | tf_op jit(solution)/shard_map/ppermute | solution.py:39
  133.3 2.1 %collective-permute-done.29 = bf16[128,384]{1,0:T(8,128)(2,1)S(1)} collective-permute-done((bf16[128,384]{1,0:T(8,128)(2,1)S(1)}, bf16[128,384]{1,0:T(8,128)(2,1)S(1)}, u32[]{:S(2)}, u32[]{:S(2)}) %collective-permute-start.29) | collective-permute-done | bytes 98336 | tf_op jit(solution)/shard_map/ppermute | solution.py:39
  135.4 1.3 collective-permute-done.31
  137.0 2.5 %collective-permute-start.32 = (bf16[128,192]{1,0:T(8,128)(2,1)S(1)}, bf16[128,192]{1,0:T(8,128)(2,1)S(1)}, u32[]{:S(2)}, u32[]{:S(2)}) collective-permute-start(bf16[128,192]{1,0:T(8,128)(2,1)S(1)} %broadcast_select_fusion.1), channel_id=1, source_target_pairs={{0,1},{1,0},{2,3},{3,2},{4,5},{5,4},{6,7},{7,6},{8,9},{9,8},{10,11... | collective-permute-start | bytes 147464 | tf_op jit(solution)/shard_map/ppermute | solution.py:35
  139.5 0.9 collective-permute-done.32
  140.5 0.7 copy.9
  (40 shorter events, 1.3 us)
Async XLA Ops:
  1.0 3.0 %collective-permute-start = (bf16[128,192]{1,0:T(8,128)(2,1)S(1)}, bf16[128,192]{1,0:T(8,128)(2,1)S(1)}, u32[]{:S(2)}, u32[]{:S(2)}) collective-permute-start(bf16[128,192]{1,0:T(8,128)(2,1)S(1)} %get-tuple-element.93), channel_id=1, source_target_pairs={{0,1},{1,0},{2,3},{3,2},{4,5},{5,4},{6,7},{7,6},{8,9},{9,8},{10,11... | collective-permute-start | bytes 147464 | tf_op jit(solution)/shard_map/ppermute | solution.py:35
  4.1 9.2 %collective-permute-start.3 = (bf16[128,384]{1,0:T(8,128)(2,1)S(1)}, bf16[128,384]{1,0:T(8,128)(2,1)S(1)}, u32[]{:S(2)}, u32[]{:S(2)}) collective-permute-start(bf16[128,384]{1,0:T(8,128)(2,1)S(1)} %maximum_select_fusion.refs_2_.refs_0_), channel_id=1, source_target_pairs={{0,96},{32,0},{64,32},{96,64},{1,97},{33,1},{65,33},{97,65},{2,98}... | collective-permute-start | bytes 294920 | tf_op jit(solution)/shard_map/ppermute | solution.py:39
  7.0 7.6 %collective-permute-start.2 = (bf16[128,384]{1,0:T(8,128)(2,1)S(1)}, bf16[128,384]{1,0:T(8,128)(2,1)S(1)}, u32[]{:S(2)}, u32[]{:S(2)}) collective-permute-start(bf16[128,384]{1,0:T(8,128)(2,1)S(1)} %maximum_select_fusion.refs_2_.refs_0_), channel_id=1, source_target_pairs={{0,32},{32,64},{64,96},{96,0},{1,33},{33,65},{65,97},{97,1},{2,34}... | collective-permute-start | bytes 294920 | tf_op jit(solution)/shard_map/ppermute | solution.py:39
  7.0 7.6 %collective-permute-start.1 = (bf16[128,384]{1,0:T(8,128)(2,1)S(1)}, bf16[128,384]{1,0:T(8,128)(2,1)S(1)}, u32[]{:S(2)}, u32[]{:S(2)}) collective-permute-start(bf16[128,384]{1,0:T(8,128)(2,1)S(1)} %maximum_select_fusion.refs_2_.refs_0_), channel_id=1, source_target_pairs={{0,64},{32,96},{64,0},{96,32},{1,65},{33,97},{65,1},{97,33},{2,66}... | collective-permute-start | bytes 294920 | tf_op jit(solution)/shard_map/ppermute | solution.py:39
  14.7 12.8 %collective-permute-start.6 = (bf16[1,512,384]{2,1,0:T(8,128)(2,1)S(1)}, bf16[1,512,384]{2,1,0:T(8,128)(2,1)S(1)}, u32[]{:S(2)}, u32[]{:S(2)}) collective-permute-start(bf16[1,512,384]{2,1,0:T(8,128)(2,1)S(1)} %gather.3.refs_1_.refs_0_), channel_id=1, source_target_pairs={{0,6},{1,25},{2,0},{3,27},{4,2},{5,29},{6,4},{7,31},{8,14},{9,1},{... | collective-permute-start | bytes 1179656 | tf_op jit(solution)/shard_map/ppermute | solution.py:31
  18.5 12.3 %collective-permute-start.5 = (bf16[1,512,384]{2,1,0:T(8,128)(2,1)S(1)}, bf16[1,512,384]{2,1,0:T(8,128)(2,1)S(1)}, u32[]{:S(2)}, u32[]{:S(2)}) collective-permute-start(bf16[1,512,384]{2,1,0:T(8,128)(2,1)S(1)} %gather.3.refs_1_.refs_0_), channel_id=1, source_target_pairs={{0,2},{1,9},{2,4},{3,11},{4,6},{5,13},{6,0},{7,15},{8,10},{9,17},{... | collective-permute-start | bytes 1179656 | tf_op jit(solution)/shard_map/ppermute | solution.py:31
  18.5 12.3 %collective-permute-start.4 = (bf16[1,512,384]{2,1,0:T(8,128)(2,1)S(1)}, bf16[1,512,384]{2,1,0:T(8,128)(2,1)S(1)}, u32[]{:S(2)}, u32[]{:S(2)}) collective-permute-start(bf16[1,512,384]{2,1,0:T(8,128)(2,1)S(1)} %gather.3.refs_1_.refs_0_), channel_id=1, source_target_pairs={{0,4},{1,17},{2,6},{3,19},{4,0},{5,21},{6,2},{7,23},{8,12},{9,25},... | collective-permute-start | bytes 1179656 | tf_op jit(solution)/shard_map/ppermute | solution.py:31
  31.0 4.2 %collective-permute-start.8 = (bf16[4,512,384]{2,1,0:T(8,128)(2,1)S(1)}, bf16[4,512,384]{2,1,0:T(8,128)(2,1)S(1)}, u32[]{:S(2)}, u32[]{:S(2)}) collective-permute-start(bf16[4,512,384]{2,1,0:T(8,128)(2,1)S(1)} %gather.4.refs_0_), channel_id=1, source_target_pairs={{0,1},{1,0},{2,3},{3,2},{4,5},{5,4},{6,7},{7,6},{8,9},{9,8},{10,11... | collective-permute-start | bytes 4718600 | tf_op jit(solution)/shard_map/ppermute | solution.py:35
  31.8 19.6 %collective-permute-start.9 = (bf16[4,512,384]{2,1,0:T(8,128)(2,1)S(1)}, bf16[4,512,384]{2,1,0:T(8,128)(2,1)S(1)}, u32[]{:S(2)}, u32[]{:S(2)}) collective-permute-start(bf16[4,512,384]{2,1,0:T(8,128)(2,1)S(1)} %gather.4.refs_0_), channel_id=1, source_target_pairs={{0,24},{1,7},{2,26},{3,1},{4,28},{5,3},{6,30},{7,5},{8,0},{9,15},{... | collective-permute-start | bytes 4718600 | tf_op jit(solution)/shard_map/ppermute | solution.py:27
  33.3 20.8 %collective-permute-start.7 = (bf16[4,512,384]{2,1,0:T(8,128)(2,1)S(1)}, bf16[4,512,384]{2,1,0:T(8,128)(2,1)S(1)}, u32[]{:S(2)}, u32[]{:S(2)}) collective-permute-start(bf16[4,512,384]{2,1,0:T(8,128)(2,1)S(1)} %gather.4.refs_0_), channel_id=1, source_target_pairs={{0,8},{1,3},{2,10},{3,5},{4,12},{5,7},{6,14},{7,1},{8,16},{9,11},{... | collective-permute-start | bytes 4718600 | tf_op jit(solution)/shard_map/ppermute | solution.py:27
  54.2 8.6 %collective-permute-start.11 = (bf16[4,512,384]{2,1,0:T(8,128)(2,1)S(1)}, bf16[4,512,384]{2,1,0:T(8,128)(2,1)S(1)}, u32[]{:S(2)}, u32[]{:S(2)}) collective-permute-start(bf16[4,512,384]{2,1,0:T(8,128)(2,1)S(1)} %collective-permute-done.7.refs_0_), channel_id=1, source_target_pairs={{0,1},{1,0},{2,3},{3,2},{4,5},{5,4},{6,7},{7,6},{8,9},{9,8},{10,11... | collective-permute-start | bytes 4718600 | tf_op jit(solution)/shard_map/ppermute | solution.py:35
  57.8 5.3 %collective-permute-start.12 = (bf16[4,512,384]{2,1,0:T(8,128)(2,1)S(1)}, bf16[4,512,384]{2,1,0:T(8,128)(2,1)S(1)}, u32[]{:S(2)}, u32[]{:S(2)}) collective-permute-start(bf16[4,512,384]{2,1,0:T(8,128)(2,1)S(1)} %collective-permute-done.9.refs_1_), channel_id=1, source_target_pairs={{0,1},{1,0},{2,3},{3,2},{4,5},{5,4},{6,7},{7,6},{8,9},{9,8},{10,11... | collective-permute-start | bytes 4718600 | tf_op jit(solution)/shard_map/ppermute | solution.py:35
  57.9 11.1 %collective-permute-start.14 = (bf16[2,512,384]{2,1,0:T(8,128)(2,1)S(1)}, bf16[2,512,384]{2,1,0:T(8,128)(2,1)S(1)}, u32[]{:S(2)}, u32[]{:S(2)}) collective-permute-start(bf16[2,512,384]{2,1,0:T(8,128)(2,1)S(1)} %get-tuple-element.56.refs_7_), channel_id=1, source_target_pairs={{0,24},{1,7},{2,26},{3,1},{4,28},{5,3},{6,30},{7,5},{8,0},{9,15},{... | collective-permute-start | bytes 2359304 | tf_op jit(solution)/shard_map/ppermute | solution.py:27
  57.9 12.3 %collective-permute-start.10 = (bf16[2,512,384]{2,1,0:T(8,128)(2,1)S(1)}, bf16[2,512,384]{2,1,0:T(8,128)(2,1)S(1)}, u32[]{:S(2)}, u32[]{:S(2)}) collective-permute-start(bf16[2,512,384]{2,1,0:T(8,128)(2,1)S(1)} %get-tuple-element.55.refs_6_), channel_id=1, source_target_pairs={{0,8},{1,3},{2,10},{3,5},{4,12},{5,7},{6,14},{7,1},{8,16},{9,11},{... | collective-permute-start | bytes 2359304 | tf_op jit(solution)/shard_map/ppermute | solution.py:27
  70.2 5.3 %collective-permute-start.13 = (bf16[2,512,384]{2,1,0:T(8,128)(2,1)S(1)}, bf16[2,512,384]{2,1,0:T(8,128)(2,1)S(1)}, u32[]{:S(2)}, u32[]{:S(2)}) collective-permute-start(bf16[2,512,384]{2,1,0:T(8,128)(2,1)S(1)} %collective-permute-done.10.refs_0_), channel_id=1, source_target_pairs={{0,1},{1,0},{2,3},{3,2},{4,5},{5,4},{6,7},{7,6},{8,9},{9,8},{10,11... | collective-permute-start | bytes 2359304 | tf_op jit(solution)/shard_map/ppermute | solution.py:35
  71.5 4.1 %collective-permute-start.15 = (bf16[2,512,384]{2,1,0:T(8,128)(2,1)S(1)}, bf16[2,512,384]{2,1,0:T(8,128)(2,1)S(1)}, u32[]{:S(2)}, u32[]{:S(2)}) collective-permute-start(bf16[2,512,384]{2,1,0:T(8,128)(2,1)S(1)} %collective-permute-done.14.refs_1_), channel_id=1, source_target_pairs={{0,1},{1,0},{2,3},{3,2},{4,5},{5,4},{6,7},{7,6},{8,9},{9,8},{10,11... | collective-permute-start | bytes 2359304 | tf_op jit(solution)/shard_map/ppermute | solution.py:35
  75.0 5.2 %collective-permute-start.16 = (bf16[4,512,384]{2,1,0:T(8,128)(2,1)S(1)}, bf16[4,512,384]{2,1,0:T(8,128)(2,1)S(1)}, u32[]{:S(2)}, u32[]{:S(2)}) collective-permute-start(bf16[4,512,384]{2,1,0:T(8,128)(2,1)S(1)} %down.10.refs_6_), channel_id=1, source_target_pairs={{0,1},{1,0},{2,3},{3,2},{4,5},{5,4},{6,7},{7,6},{8,9},{9,8},{10,11... | collective-permute-start | bytes 4718600 | tf_op jit(solution)/shard_map/ppermute | solution.py:35
  78.5 7.2 %collective-permute-start.18 = (bf16[4,512,384]{2,1,0:T(8,128)(2,1)S(1)}, bf16[4,512,384]{2,1,0:T(8,128)(2,1)S(1)}, u32[]{:S(2)}, u32[]{:S(2)}) collective-permute-start(bf16[4,512,384]{2,1,0:T(8,128)(2,1)S(1)} %down.11.rest_0_.rest_1_), channel_id=1, source_target_pairs={{0,1},{1,0},{2,3},{3,2},{4,5},{5,4},{6,7},{7,6},{8,9},{9,8},{10,11... | collective-permute-start | bytes 4718600 | tf_op jit(solution)/shard_map/ppermute | solution.py:35
  79.6 15.0 %collective-permute-start.20 = (bf16[4,512,384]{2,1,0:T(8,128)(2,1)S(1)}, bf16[4,512,384]{2,1,0:T(8,128)(2,1)S(1)}, u32[]{:S(2)}, u32[]{:S(2)}) collective-permute-start(bf16[4,512,384]{2,1,0:T(8,128)(2,1)S(1)} %down.12.rest_1_.rest_2_), channel_id=1, source_target_pairs={{0,1},{1,0},{2,3},{3,2},{4,5},{5,4},{6,7},{7,6},{8,9},{9,8},{10,11... | collective-permute-start | bytes 4718600 | tf_op jit(solution)/shard_map/ppermute | solution.py:35
  81.2 12.4 %collective-permute-start.19 = (bf16[2,512,384]{2,1,0:T(8,128)(2,1)S(1)}, bf16[2,512,384]{2,1,0:T(8,128)(2,1)S(1)}, u32[]{:S(2)}, u32[]{:S(2)}) collective-permute-start(bf16[2,512,384]{2,1,0:T(8,128)(2,1)S(1)} %get-tuple-element.75), channel_id=1, source_target_pairs={{0,8},{1,3},{2,10},{3,5},{4,12},{5,7},{6,14},{7,1},{8,16},{9,11},{... | collective-permute-start | bytes 2359304 | tf_op jit(solution)/shard_map/ppermute | solution.py:27
  81.3 13.3 %collective-permute-start.21 = (bf16[2,512,384]{2,1,0:T(8,128)(2,1)S(1)}, bf16[2,512,384]{2,1,0:T(8,128)(2,1)S(1)}, u32[]{:S(2)}, u32[]{:S(2)}) collective-permute-start(bf16[2,512,384]{2,1,0:T(8,128)(2,1)S(1)} %get-tuple-element.77), channel_id=1, source_target_pairs={{0,24},{1,7},{2,26},{3,1},{4,28},{5,3},{6,30},{7,5},{8,0},{9,15},{... | collective-permute-start | bytes 2359304 | tf_op jit(solution)/shard_map/ppermute | solution.py:27
  85.0 14.5 %collective-permute-start.17 = (bf16[4,512,384]{2,1,0:T(8,128)(2,1)S(1)}, bf16[4,512,384]{2,1,0:T(8,128)(2,1)S(1)}, u32[]{:S(2)}, u32[]{:S(2)}) collective-permute-start(bf16[4,512,384]{2,1,0:T(8,128)(2,1)S(1)} %down.13), channel_id=1, source_target_pairs={{0,1},{1,0},{2,3},{3,2},{4,5},{5,4},{6,7},{7,6},{8,9},{9,8},{10,11... | collective-permute-start | bytes 4718600 | tf_op jit(solution)/shard_map/ppermute | solution.py:35
  94.5 16.6 %collective-permute-start.22 = (bf16[3,512,384]{2,1,0:T(8,128)(2,1)S(1)}, bf16[3,512,384]{2,1,0:T(8,128)(2,1)S(1)}, u32[]{:S(2)}, u32[]{:S(2)}) collective-permute-start(bf16[3,512,384]{2,1,0:T(8,128)(2,1)S(1)} %down.15.rest_1_.rest_2_), channel_id=1, source_target_pairs={{0,8},{1,3},{2,10},{3,5},{4,12},{5,7},{6,14},{7,1},{8,16},{9,11},{... | collective-permute-start | bytes 3538952 | tf_op jit(solution)/shard_map/ppermute | solution.py:27
  95.7 16.1 %collective-permute-start.24 = (bf16[3,512,384]{2,1,0:T(8,128)(2,1)S(1)}, bf16[3,512,384]{2,1,0:T(8,128)(2,1)S(1)}, u32[]{:S(2)}, u32[]{:S(2)}) collective-permute-start(bf16[3,512,384]{2,1,0:T(8,128)(2,1)S(1)} %down.16.rest_2_.rest_3_), channel_id=1, source_target_pairs={{0,24},{1,7},{2,26},{3,1},{4,28},{5,3},{6,30},{7,5},{8,0},{9,15},{... | collective-permute-start | bytes 3538952 | tf_op jit(solution)/shard_map/ppermute | solution.py:27
  111.2 8.1 %collective-permute-start.23 = (bf16[1,512,384]{2,1,0:T(8,128)(2,1)S(1)}, bf16[1,512,384]{2,1,0:T(8,128)(2,1)S(1)}, u32[]{:S(2)}, u32[]{:S(2)}) collective-permute-start(bf16[1,512,384]{2,1,0:T(8,128)(2,1)S(1)} %down.18), channel_id=1, source_target_pairs={{0,8},{1,3},{2,10},{3,5},{4,12},{5,7},{6,14},{7,1},{8,16},{9,11},{... | collective-permute-start | bytes 1179656 | tf_op jit(solution)/shard_map/ppermute | solution.py:27
  111.7 12.4 %collective-permute-start.25 = (bf16[1,512,384]{2,1,0:T(8,128)(2,1)S(1)}, bf16[1,512,384]{2,1,0:T(8,128)(2,1)S(1)}, u32[]{:S(2)}, u32[]{:S(2)}) collective-permute-start(bf16[1,512,384]{2,1,0:T(8,128)(2,1)S(1)} %down.19), channel_id=1, source_target_pairs={{0,24},{1,7},{2,26},{3,1},{4,28},{5,3},{6,30},{7,5},{8,0},{9,15},{... | collective-permute-start | bytes 1179656 | tf_op jit(solution)/shard_map/ppermute | solution.py:27
  115.2 8.9 %collective-permute-start.26 = (bf16[512,384]{1,0:T(8,128)(2,1)S(1)}, bf16[512,384]{1,0:T(8,128)(2,1)S(1)}, u32[]{:S(2)}, u32[]{:S(2)}) collective-permute-start(bf16[512,384]{1,0:T(8,128)(2,1)S(1)} %get-tuple-element.82), channel_id=1, source_target_pairs={{0,4},{1,17},{2,6},{3,19},{4,0},{5,21},{6,2},{7,23},{8,12},{9,25},... | collective-permute-start | bytes 1179656 | tf_op jit(solution)/shard_map/ppermute | solution.py:31
  115.6 14.3 %collective-permute-start.27 = (bf16[512,384]{1,0:T(8,128)(2,1)S(1)}, bf16[512,384]{1,0:T(8,128)(2,1)S(1)}, u32[]{:S(2)}, u32[]{:S(2)}) collective-permute-start(bf16[512,384]{1,0:T(8,128)(2,1)S(1)} %get-tuple-element.83), channel_id=1, source_target_pairs={{0,2},{1,9},{2,4},{3,11},{4,6},{5,13},{6,0},{7,15},{8,10},{9,17},{... | collective-permute-start | bytes 1179656 | tf_op jit(solution)/shard_map/ppermute | solution.py:31
  115.9 14.0 %collective-permute-start.28 = (bf16[512,384]{1,0:T(8,128)(2,1)S(1)}, bf16[512,384]{1,0:T(8,128)(2,1)S(1)}, u32[]{:S(2)}, u32[]{:S(2)}) collective-permute-start(bf16[512,384]{1,0:T(8,128)(2,1)S(1)} %get-tuple-element.84), channel_id=1, source_target_pairs={{0,6},{1,25},{2,0},{3,27},{4,2},{5,29},{6,4},{7,31},{8,14},{9,1},{... | collective-permute-start | bytes 1179656 | tf_op jit(solution)/shard_map/ppermute | solution.py:31
  130.3 5.2 %collective-permute-start.29 = (bf16[128,384]{1,0:T(8,128)(2,1)S(1)}, bf16[128,384]{1,0:T(8,128)(2,1)S(1)}, u32[]{:S(2)}, u32[]{:S(2)}) collective-permute-start(bf16[128,384]{1,0:T(8,128)(2,1)S(1)} %get-tuple-element.87), channel_id=1, source_target_pairs={{0,64},{32,96},{64,0},{96,32},{1,65},{33,97},{65,1},{97,33},{2,66}... | collective-permute-start | bytes 294920 | tf_op jit(solution)/shard_map/ppermute | solution.py:39
  130.6 6.1 %collective-permute-start.31 = (bf16[128,384]{1,0:T(8,128)(2,1)S(1)}, bf16[128,384]{1,0:T(8,128)(2,1)S(1)}, u32[]{:S(2)}, u32[]{:S(2)}) collective-permute-start(bf16[128,384]{1,0:T(8,128)(2,1)S(1)} %get-tuple-element.88), channel_id=1, source_target_pairs={{0,32},{32,64},{64,96},{96,0},{1,33},{33,65},{65,97},{97,1},{2,34}... | collective-permute-start | bytes 294920 | tf_op jit(solution)/shard_map/ppermute | solution.py:39
  131.8 5.0 %collective-permute-start.30 = (bf16[128,384]{1,0:T(8,128)(2,1)S(1)}, bf16[128,384]{1,0:T(8,128)(2,1)S(1)}, u32[]{:S(2)}, u32[]{:S(2)}) collective-permute-start(bf16[128,384]{1,0:T(8,128)(2,1)S(1)} %get-tuple-element.89), channel_id=1, source_target_pairs={{0,96},{32,0},{64,32},{96,64},{1,97},{33,1},{65,33},{97,65},{2,98}... | collective-permute-start | bytes 294920 | tf_op jit(solution)/shard_map/ppermute | solution.py:39
  137.0 3.4 %collective-permute-start.32 = (bf16[128,192]{1,0:T(8,128)(2,1)S(1)}, bf16[128,192]{1,0:T(8,128)(2,1)S(1)}, u32[]{:S(2)}, u32[]{:S(2)}) collective-permute-start(bf16[128,192]{1,0:T(8,128)(2,1)S(1)} %broadcast_select_fusion.1), channel_id=1, source_target_pairs={{0,1},{1,0},{2,3},{3,2},{4,5},{5,4},{6,7},{7,6},{8,9},{9,8},{10,11... | collective-permute-start | bytes 147464 | tf_op jit(solution)/shard_map/ppermute | solution.py:35

commit v5 on v4

--- a/solution.py
+++ b/solution.py
@@ -310,7 +310,7 @@
     m0_own, m0 = down(h_other, at(1, 0, 0), [(sent0, 0)], [1, SIDE - 1], F32, [m1, m3])
     s1, s2, s3 = add_call(m0, n1, n3)
     moved = [move_small(s2, 2), move_small(s1, 1), move_small(s3, 3)]
-    n1_own, n3_own = move_bulk(after(m1_own, n1), 1), move_bulk(after(m3_own, n3), 3)
+    n1_own, n3_own = move_bulk(after(m1_own, n1), 1), move_bulk(after(m3_own, n1), 3)
     plane = fsum([m0_own[0], n1_own[0], n3_own[0]] + moved).astype(BF)
     plane = plane.reshape(SIDE, rows, 2 * half)
 

time: 141 us -> 141 us (level)
  starting transfers between devices: 39.3 us -> 36.7 us
  waiting for transfers between devices: 65.2 us -> 67.5 us
    ppermute x6, waiting for transfers between devices: 4.71 us -> 6.61 us  [move_expert(): lax.ppermute(v, 'expert', [(i, (i + shift) % SIDE) for i in range(SIDE)])]
    ppermute x11, starting transfers between devices: 11.7 us -> 9.81 us  [move_core(): return lax.ppermute(v, 'blk', [(i, i ^ 1) for i in range(2 * SIDE * SIDE)])]
  transfers between devices with their start and end apart: 33 -> 33, of which waited for: 17 -> 16; matrix products, arithmetic and copies ran while one was open for 1% -> 1% of each run, Pallas kernels for 23% -> 23%
where the time goes in v5:
time: 141 us
  waiting for transfers between devices  67.5 us (48%)
  starting transfers between devices  36.7 us (26%)
  Pallas kernels  32.4 us (23%)
  other arithmetic  2.31 us (2%)
  local copies, waits for them, and re-layouts  1.78 us (1%)
    ppermute x10, waiting for transfers between devices, move_bulk(): return lax.ppermute(v, 'blk', blk_perm(True, shift))  45.4 us
    pallas_call x6, Pallas kernels, up_call(): pl.pallas_call(kernel, in_specs=[SMEM] + [VMEM] * len(args) + [ANY] * len...  15.5 us
    ppermute x6, waiting for transfers between devices, move_small(): return lax.ppermute(v, 'blk', blk_perm(False, shift))  14.4 us
    ppermute x10, starting transfers between devices, move_bulk(): return lax.ppermute(v, 'blk', blk_perm(True, shift))  11.4 us
    ppermute x11, starting transfers between devices, move_core(): return lax.ppermute(v, 'blk', [(i, i ^ 1) for i in range(2 * SIDE * SIDE)])  9.81 us
    pallas_call x10, Pallas kernels, down_call(): pl.pallas_call(kernel, in_specs=[SMEM] + [VMEM] * len(args) + [ANY] * len...  8.9 us
    ppermute x6, starting transfers between devices, move_small(): return lax.ppermute(v, 'blk', blk_perm(False, shift))  7.96 us
    ppermute x6, starting transfers between devices, move_expert(): lax.ppermute(v, 'expert', [(i, (i + shift) % SIDE) for i in range(SIDE)])  7.58 us
  transfers between devices with their start and end apart: 33, of which 16 were waited for; matrix products, arithmetic and copies ran while one was open for 1% of the time, Pallas kernels for 23%

profile of v5, /device:TPU:1, one launch (start us, length us, event | category | flops | bytes accessed | tf_op | source)
XLA Modules:
  0.0 141.0 jit_solution(14179558463521823650)
XLA Ops:
  0.0 1.0 copy.7
  1.0 1.5 %collective-permute-start = (bf16[128,192]{1,0:T(8,128)(2,1)S(1)}, bf16[128,192]{1,0:T(8,128)(2,1)S(1)}, u32[]{:S(2)}, u32[]{:S(2)}) collective-permute-start(bf16[128,192]{1,0:T(8,128)(2,1)S(1)} %get-tuple-element.93), channel_id=1, source_target_pairs={{0,1},{1,0},{2,3},{3,2},{4,5},{5,4},{6,7},{7,6},{8,9},{9,8},{10,11... | collective-permute-start | bytes 147464 | tf_op jit(solution)/shard_map/ppermute | solution.py:35
  2.5 0.7 select_bitcast_fusion.4
  3.2 0.8 broadcast_subtract_fusion
  4.1 2.9 %collective-permute-start.3 = (bf16[128,384]{1,0:T(8,128)(2,1)S(1)}, bf16[128,384]{1,0:T(8,128)(2,1)S(1)}, u32[]{:S(2)}, u32[]{:S(2)}) collective-permute-start(bf16[128,384]{1,0:T(8,128)(2,1)S(1)} %maximum_select_fusion.refs_2_.refs_0_), channel_id=1, source_target_pairs={{0,96},{32,0},{64,32},{96,64},{1,97},{33,1},{65,33},{97,65},{2,98}... | collective-permute-start | bytes 294920 | tf_op jit(solution)/shard_map/ppermute | solution.py:39
  7.0 1.6 %collective-permute-start.1 = (bf16[128,384]{1,0:T(8,128)(2,1)S(1)}, bf16[128,384]{1,0:T(8,128)(2,1)S(1)}, u32[]{:S(2)}, u32[]{:S(2)}) collective-permute-start(bf16[128,384]{1,0:T(8,128)(2,1)S(1)} %maximum_select_fusion.refs_2_.refs_0_), channel_id=1, source_target_pairs={{0,64},{32,96},{64,0},{96,32},{1,65},{33,97},{65,1},{97,33},{2,66}... | collective-permute-start | bytes 294920 | tf_op jit(solution)/shard_map/ppermute | solution.py:39
  8.7 4.6 %load.2 = (bf16[6144,512]{1,0:T(8,128)(2,1)S(1)}, bf16[6144,512]{1,0:T(8,128)(2,1)S(1)}, f32[8,128]{1,0:T(8,128)S(1)}) custom-call(bf16[6144,512]{1,0:T(8,128)(2,1)} %bitcast.38, bf16[6144,512]{1,0:T(8,128)(2,1)} %bitcast.39, bf16[128,384]{1,0:T(8,128)(2,1)S(1)} %maximum_select_fusion.refs_2_.refs_0_, f32[4,128]{1,0:T(4,128)S(1)} %select_add_fusion.refs_3_), custom_call_target="tpu_custom_call" | custom-call | bytes 25165824 | tf_op jit(solution)/shard_map/load/pallas_call | solution.py:163
  13.4 1.3 collective-permute-done.2.refs_2_
  14.7 3.8 %collective-permute-start.6 = (bf16[1,512,384]{2,1,0:T(8,128)(2,1)S(1)}, bf16[1,512,384]{2,1,0:T(8,128)(2,1)S(1)}, u32[]{:S(2)}, u32[]{:S(2)}) collective-permute-start(bf16[1,512,384]{2,1,0:T(8,128)(2,1)S(1)} %gather.3.refs_1_.refs_0_), channel_id=1, source_target_pairs={{0,6},{1,25},{2,0},{3,27},{4,2},{5,29},{6,4},{7,31},{8,14},{9,1},{... | collective-permute-start | bytes 1179656 | tf_op jit(solution)/shard_map/ppermute | solution.py:31
  18.5 1.3 collective-permute-start.4
  19.8 2.8 %load.3 = (bf16[512,6144]{1,0:T(8,128)(2,1)S(1)}, f32[8,128]{1,0:T(8,128)S(1)}) custom-call(bf16[512,6144]{1,0:T(8,128)(2,1)} %bitcast.37, bf16[1,512,384]{2,1,0:T(8,128)(2,1)S(1)} %gather.3.refs_1_.refs_0_), custom_call_target="tpu_custom_call" | custom-call | bytes 12582912 | tf_op jit(solution)/shard_map/load/pallas_call | solution.py:163
  22.6 4.8 %collective-permute-done.6.refs_3_ = bf16[1,512,384]{2,1,0:T(8,128)(2,1)S(1)} collective-permute-done((bf16[1,512,384]{2,1,0:T(8,128)(2,1)S(1)}, bf16[1,512,384]{2,1,0:T(8,128)(2,1)S(1)}, u32[]{:S(2)}, u32[]{:S(2)}) %collective-permute-start.6) | collective-permute-done | bytes 393248 | tf_op jit(solution)/shard_map/ppermute | solution.py:31
  27.4 3.4 %collective-permute-done.5.refs_2_ = bf16[1,512,384]{2,1,0:T(8,128)(2,1)S(1)} collective-permute-done((bf16[1,512,384]{2,1,0:T(8,128)(2,1)S(1)}, bf16[1,512,384]{2,1,0:T(8,128)(2,1)S(1)}, u32[]{:S(2)}, u32[]{:S(2)}) %collective-permute-start.5) | collective-permute-done | bytes 393248 | tf_op jit(solution)/shard_map/ppermute | solution.py:31
  30.8 0.1 gather.4.refs_0_
  31.0 0.9 collective-permute-start.8
  31.8 1.5 %collective-permute-start.9 = (bf16[4,512,384]{2,1,0:T(8,128)(2,1)S(1)}, bf16[4,512,384]{2,1,0:T(8,128)(2,1)S(1)}, u32[]{:S(2)}, u32[]{:S(2)}) collective-permute-start(bf16[4,512,384]{2,1,0:T(8,128)(2,1)S(1)} %gather.4.refs_0_), channel_id=1, source_target_pairs={{0,24},{1,7},{2,26},{3,1},{4,28},{5,3},{6,30},{7,5},{8,0},{9,15},{... | collective-permute-start | bytes 4718600 | tf_op jit(solution)/shard_map/ppermute | solution.py:27
  33.3 1.8 %up.6 = (f32[512,512]{1,0:T(8,128)S(1)}, f32[512,512]{1,0:T(8,128)S(1)}, f32[8,128]{1,0:T(8,128)S(1)}) custom-call(s32[1]{0:T(128)} %bitcast.5.place_ref, bf16[4,512,384]{2,1,0:T(8,128)(2,1)S(1)} %gather.4.refs_0_, bf16[6144,512]{1,0:T(8,128)(2,1)S(1)} %get-tuple-element.49.refs_1_.refs_2_, bf16[6144,512]{1,0:T(8,128)(2,1)S(1)} %get-tuple-element.50.refs_2_.refs_3_), custom_call_target="tpu_custom_call" | custom-call | flops 1610612736 | bytes 6815744 | tf_op jit(solution)/shard_map/up/pallas_call | solution.py:98
  35.2 1.8 %up.7 = (f32[512,512]{1,0:T(8,128)S(1)}, f32[512,512]{1,0:T(8,128)S(1)}, f32[8,128]{1,0:T(8,128)S(1)}) custom-call(s32[1]{0:T(128)} %bitcast.5.place_ref, bf16[4,512,384]{2,1,0:T(8,128)(2,1)S(1)} %collective-permute-done.8.refs_0_, bf16[6144,512]{1,0:T(8,128)(2,1)S(1)} %get-tuple-element.49.refs_1_.refs_2_, ...), custom_call_target="tpu_custom_call" | custom-call | flops 1610612736 | bytes 6815744 | tf_op jit(solution)/shard_map/up/pallas_call | solution.py:98
  37.0 14.4 %collective-permute-done.9.refs_1_ = bf16[4,512,384]{2,1,0:T(8,128)(2,1)S(1)} collective-permute-done((bf16[4,512,384]{2,1,0:T(8,128)(2,1)S(1)}, bf16[4,512,384]{2,1,0:T(8,128)(2,1)S(1)}, u32[]{:S(2)}, u32[]{:S(2)}) %collective-permute-start.9) | collective-permute-done | bytes 1572896 | tf_op jit(solution)/shard_map/ppermute | solution.py:27
  51.4 2.7 %collective-permute-done.7.refs_0_ = bf16[4,512,384]{2,1,0:T(8,128)(2,1)S(1)} collective-permute-done((bf16[4,512,384]{2,1,0:T(8,128)(2,1)S(1)}, bf16[4,512,384]{2,1,0:T(8,128)(2,1)S(1)}, u32[]{:S(2)}, u32[]{:S(2)}) %collective-permute-start.7) | collective-permute-done | bytes 1572896 | tf_op jit(solution)/shard_map/ppermute | solution.py:27
  54.2 3.6 %collective-permute-start.11 = (bf16[4,512,384]{2,1,0:T(8,128)(2,1)S(1)}, bf16[4,512,384]{2,1,0:T(8,128)(2,1)S(1)}, u32[]{:S(2)}, u32[]{:S(2)}) collective-permute-start(bf16[4,512,384]{2,1,0:T(8,128)(2,1)S(1)} %collective-permute-done.7.refs_0_), channel_id=1, source_target_pairs={{0,1},{1,0},{2,3},{3,2},{4,5},{5,4},{6,7},{7,6},{8,9},{9,8},{10,11... | collective-permute-start | bytes 4718600 | tf_op jit(solution)/shard_map/ppermute | solution.py:35
  57.9 1.5 %collective-permute-start.10 = (bf16[2,512,384]{2,1,0:T(8,128)(2,1)S(1)}, bf16[2,512,384]{2,1,0:T(8,128)(2,1)S(1)}, u32[]{:S(2)}, u32[]{:S(2)}) collective-permute-start(bf16[2,512,384]{2,1,0:T(8,128)(2,1)S(1)} %get-tuple-element.55.refs_6_), channel_id=1, source_target_pairs={{0,8},{1,3},{2,10},{3,5},{4,12},{5,7},{6,14},{7,1},{8,16},{9,11},{... | collective-permute-start | bytes 2359304 | tf_op jit(solution)/shard_map/ppermute | solution.py:27
  59.4 3.5 %up.8 = (f32[512,512]{1,0:T(8,128)S(1)}, f32[512,512]{1,0:T(8,128)S(1)}, f32[8,128]{1,0:T(8,128)S(1)}) custom-call(s32[1]{0:T(128)} %bitcast.5.place_ref, bf16[4,512,384]{2,1,0:T(8,128)(2,1)S(1)} %collective-permute-done.7.refs_0_, bf16[4,512,384]{2,1,0:T(8,128)(2,1)S(1)} %collective-permute-done.9.refs_1_, ...), custom_call_target="tpu_custom_call" | custom-call | flops 3221225472 | bytes 11534336 | tf_op jit(solution)/shard_map/up/pallas_call | solution.py:98
  62.9 0.2 collective-permute-done.12.refs_1_
  63.1 4.0 %up.9 = (f32[512,512]{1,0:T(8,128)S(1)}, f32[512,512]{1,0:T(8,128)S(1)}, f32[8,128]{1,0:T(8,128)}) custom-call(s32[1]{0:T(128)} %bitcast.5.place_ref, bf16[4,512,384]{2,1,0:T(8,128)(2,1)S(1)} %collective-permute-done.11.refs_0_, bf16[4,512,384]{2,1,0:T(8,128)(2,1)S(1)} %collective-permute-done.12.refs_1_, ...), custom_call_target="tpu_custom_call" | custom-call | flops 3221225472 | bytes 11534336 | tf_op jit(solution)/shard_map/up/pallas_call | solution.py:98
  67.1 2.0 %collective-permute-done.14.refs_1_ = bf16[2,512,384]{2,1,0:T(8,128)(2,1)S(1)} collective-permute-done((bf16[2,512,384]{2,1,0:T(8,128)(2,1)S(1)}, bf16[2,512,384]{2,1,0:T(8,128)(2,1)S(1)}, u32[]{:S(2)}, u32[]{:S(2)}) %collective-permute-start.14) | collective-permute-done | bytes 786464 | tf_op jit(solution)/shard_map/ppermute | solution.py:27
  69.0 1.2 collective-permute-done.10.refs_0_
  70.2 1.3 collective-permute-start.13
  71.5 2.5 %up.10 = (bf16[512,512]{1,0:T(8,128)(2,1)S(1)}, f32[8,128]{1,0:T(8,128)}) custom-call(s32[1]{0:T(128)} %bitcast.5.place_ref, bf16[2,512,384]{2,1,0:T(8,128)(2,1)S(1)} %collective-permute-done.10.refs_0_, bf16[2,512,384]{2,1,0:T(8,128)(2,1)S(1)} %collective-permute-done.14.refs_1_, bf16[6144,512]{1,0:T(8,128)(2,1)S(1)} %get-tuple-element.49.refs_1_.refs_2_, ...), custom_call_target="tpu_custom_call" | custom-call | flops 1610612736 | bytes 6815744 | tf_op jit(solution)/shard_map/up/pallas_call | solution.py:98
  74.0 1.0 down.10.refs_6_
  75.0 0.6 collective-permute-start.16
  75.6 1.9 %up.11 = (bf16[512,512]{1,0:T(8,128)(2,1)S(1)}, f32[8,128]{1,0:T(8,128)S(1)}) custom-call(s32[1]{0:T(128)} %bitcast.5.place_ref, bf16[2,512,384]{2,1,0:T(8,128)(2,1)S(1)} %collective-permute-done.13.refs_0_, bf16[2,512,384]{2,1,0:T(8,128)(2,1)S(1)} %collective-permute-done.15.refs_1_, bf16[6144,512]{1,0:T(8,128)(2,1)S(1)} %get-tuple-element.49.refs_1_.refs_2_, ...), custom_call_target="tpu_custom_call" | custom-call | flops 1610612736 | bytes 6815744 | tf_op jit(solution)/shard_map/up/pallas_call | solution.py:98
  77.5 1.0 down.11.rest_0_.rest_1_
  78.6 1.0 down.12.rest_1_.rest_2_
  79.6 0.5 collective-permute-start.20
  80.2 1.0 down.14
  81.3 2.7 %collective-permute-start.21 = (bf16[2,512,384]{2,1,0:T(8,128)(2,1)S(1)}, bf16[2,512,384]{2,1,0:T(8,128)(2,1)S(1)}, u32[]{:S(2)}, u32[]{:S(2)}) collective-permute-start(bf16[2,512,384]{2,1,0:T(8,128)(2,1)S(1)} %get-tuple-element.77), channel_id=1, source_target_pairs={{0,24},{1,7},{2,26},{3,1},{4,28},{5,3},{6,30},{7,5},{8,0},{9,15},{... | collective-permute-start | bytes 2359304 | tf_op jit(solution)/shard_map/ppermute | solution.py:27
  84.0 1.0 down.13
  85.0 0.7 collective-permute-start.17
  85.7 7.9 %collective-permute-done.19.rest_1_ = bf16[2,512,384]{2,1,0:T(8,128)(2,1)S(1)} collective-permute-done((bf16[2,512,384]{2,1,0:T(8,128)(2,1)S(1)}, bf16[2,512,384]{2,1,0:T(8,128)(2,1)S(1)}, u32[]{:S(2)}, u32[]{:S(2)}) %collective-permute-start.19) | collective-permute-done | bytes 786464 | tf_op jit(solution)/shard_map/ppermute | solution.py:27
  93.6 0.9 down.15.rest_1_.rest_2_
  94.6 1.0 down.16.rest_2_.rest_3_
  95.7 2.9 %collective-permute-start.25 = (bf16[3,512,384]{2,1,0:T(8,128)(2,1)S(1)}, bf16[3,512,384]{2,1,0:T(8,128)(2,1)S(1)}, u32[]{:S(2)}, u32[]{:S(2)}) collective-permute-start(bf16[3,512,384]{2,1,0:T(8,128)(2,1)S(1)} %down.16.rest_2_.rest_3_), channel_id=1, source_target_pairs={{0,24},{1,7},{2,26},{3,1},{4,28},{5,3},{6,30},{7,5},{8,0},{9,15},{... | collective-permute-start | bytes 3538952 | tf_op jit(solution)/shard_map/ppermute | solution.py:27
  98.6 0.4 down.18
  99.0 0.5 down.19
  99.5 1.0 down.17
  100.5 10.6 %collective-permute-done.22.refs_0_ = bf16[3,512,384]{2,1,0:T(8,128)(2,1)S(1)} collective-permute-done((bf16[3,512,384]{2,1,0:T(8,128)(2,1)S(1)}, bf16[3,512,384]{2,1,0:T(8,128)(2,1)S(1)}, u32[]{:S(2)}, u32[]{:S(2)}) %collective-permute-start.22) | collective-permute-done | bytes 1179680 | tf_op jit(solution)/shard_map/ppermute | solution.py:27
  111.2 2.7 %collective-permute-start.24 = (bf16[1,512,384]{2,1,0:T(8,128)(2,1)S(1)}, bf16[1,512,384]{2,1,0:T(8,128)(2,1)S(1)}, u32[]{:S(2)}, u32[]{:S(2)}) collective-permute-start(bf16[1,512,384]{2,1,0:T(8,128)(2,1)S(1)} %down.19), channel_id=1, source_target_pairs={{0,24},{1,7},{2,26},{3,1},{4,28},{5,3},{6,30},{7,5},{8,0},{9,15},{... | collective-permute-start | bytes 1179656 | tf_op jit(solution)/shard_map/ppermute | solution.py:27
  113.8 0.4 add.94
  114.3 0.3 collective-permute-start.27
  114.6 2.4 %collective-permute-start.28 = (bf16[512,384]{1,0:T(8,128)(2,1)S(1)}, bf16[512,384]{1,0:T(8,128)(2,1)S(1)}, u32[]{:S(2)}, u32[]{:S(2)}) collective-permute-start(bf16[512,384]{1,0:T(8,128)(2,1)S(1)} %get-tuple-element.84), channel_id=1, source_target_pairs={{0,6},{1,25},{2,0},{3,27},{4,2},{5,29},{6,4},{7,31},{8,14},{9,1},{... | collective-permute-start | bytes 1179656 | tf_op jit(solution)/shard_map/ppermute | solution.py:31
  117.0 2.3 %collective-permute-done.23 = bf16[1,512,384]{2,1,0:T(8,128)(2,1)S(1)} collective-permute-done((bf16[1,512,384]{2,1,0:T(8,128)(2,1)S(1)}, bf16[1,512,384]{2,1,0:T(8,128)(2,1)S(1)}, u32[]{:S(2)}, u32[]{:S(2)}) %collective-permute-start.23) | collective-permute-done | bytes 393248 | tf_op jit(solution)/shard_map/ppermute | solution.py:27
  119.3 4.3 %collective-permute-done.24 = bf16[1,512,384]{2,1,0:T(8,128)(2,1)S(1)} collective-permute-done((bf16[1,512,384]{2,1,0:T(8,128)(2,1)S(1)}, bf16[1,512,384]{2,1,0:T(8,128)(2,1)S(1)}, u32[]{:S(2)}, u32[]{:S(2)}) %collective-permute-start.24) | collective-permute-done | bytes 393248 | tf_op jit(solution)/shard_map/ppermute | solution.py:27
  123.5 6.1 %collective-permute-done.27 = bf16[512,384]{1,0:T(8,128)(2,1)S(1)} collective-permute-done((bf16[512,384]{1,0:T(8,128)(2,1)S(1)}, bf16[512,384]{1,0:T(8,128)(2,1)S(1)}, u32[]{:S(2)}, u32[]{:S(2)}) %collective-permute-start.27) | collective-permute-done | bytes 393248 | tf_op jit(solution)/shard_map/ppermute | solution.py:31
  129.7 0.3 fusion.2
  130.0 0.4 collective-permute-start.29
  130.4 1.1 collective-permute-start.31
  131.5 1.5 %collective-permute-start.30 = (bf16[128,384]{1,0:T(8,128)(2,1)S(1)}, bf16[128,384]{1,0:T(8,128)(2,1)S(1)}, u32[]{:S(2)}, u32[]{:S(2)}) collective-permute-start(bf16[128,384]{1,0:T(8,128)(2,1)S(1)} %get-tuple-element.89), channel_id=1, source_target_pairs={{0,96},{32,0},{64,32},{96,64},{1,97},{33,1},{65,33},{97,65},{2,98}... | collective-permute-start | bytes 294920 | tf_op jit(solution)/shard_map/ppermute | solution.py:39
  133.1 2.6 %collective-permute-done.29 = bf16[128,384]{1,0:T(8,128)(2,1)S(1)} collective-permute-done((bf16[128,384]{1,0:T(8,128)(2,1)S(1)}, bf16[128,384]{1,0:T(8,128)(2,1)S(1)}, u32[]{:S(2)}, u32[]{:S(2)}) %collective-permute-start.29) | collective-permute-done | bytes 98336 | tf_op jit(solution)/shard_map/ppermute | solution.py:39
  135.6 2.8 %collective-permute-done.31 = bf16[128,384]{1,0:T(8,128)(2,1)S(1)} collective-permute-done((bf16[128,384]{1,0:T(8,128)(2,1)S(1)}, bf16[128,384]{1,0:T(8,128)(2,1)S(1)}, u32[]{:S(2)}, u32[]{:S(2)}) %collective-permute-start.31) | collective-permute-done | bytes 98336 | tf_op jit(solution)/shard_map/ppermute | solution.py:39
  138.4 0.1 add_convert_fusion
  138.7 0.6 collective-permute-start.32
  139.3 0.9 collective-permute-done.32
  140.3 0.7 copy.9
  (40 shorter events, 1.1 us)
Async XLA Ops:
  1.0 3.0 %collective-permute-start = (bf16[128,192]{1,0:T(8,128)(2,1)S(1)}, bf16[128,192]{1,0:T(8,128)(2,1)S(1)}, u32[]{:S(2)}, u32[]{:S(2)}) collective-permute-start(bf16[128,192]{1,0:T(8,128)(2,1)S(1)} %get-tuple-element.93), channel_id=1, source_target_pairs={{0,1},{1,0},{2,3},{3,2},{4,5},{5,4},{6,7},{7,6},{8,9},{9,8},{10,11... | collective-permute-start | bytes 147464 | tf_op jit(solution)/shard_map/ppermute | solution.py:35
  4.1 9.2 %collective-permute-start.3 = (bf16[128,384]{1,0:T(8,128)(2,1)S(1)}, bf16[128,384]{1,0:T(8,128)(2,1)S(1)}, u32[]{:S(2)}, u32[]{:S(2)}) collective-permute-start(bf16[128,384]{1,0:T(8,128)(2,1)S(1)} %maximum_select_fusion.refs_2_.refs_0_), channel_id=1, source_target_pairs={{0,96},{32,0},{64,32},{96,64},{1,97},{33,1},{65,33},{97,65},{2,98}... | collective-permute-start | bytes 294920 | tf_op jit(solution)/shard_map/ppermute | solution.py:39
  7.0 7.6 %collective-permute-start.2 = (bf16[128,384]{1,0:T(8,128)(2,1)S(1)}, bf16[128,384]{1,0:T(8,128)(2,1)S(1)}, u32[]{:S(2)}, u32[]{:S(2)}) collective-permute-start(bf16[128,384]{1,0:T(8,128)(2,1)S(1)} %maximum_select_fusion.refs_2_.refs_0_), channel_id=1, source_target_pairs={{0,32},{32,64},{64,96},{96,0},{1,33},{33,65},{65,97},{97,1},{2,34}... | collective-permute-start | bytes 294920 | tf_op jit(solution)/shard_map/ppermute | solution.py:39
  7.0 7.6 %collective-permute-start.1 = (bf16[128,384]{1,0:T(8,128)(2,1)S(1)}, bf16[128,384]{1,0:T(8,128)(2,1)S(1)}, u32[]{:S(2)}, u32[]{:S(2)}) collective-permute-start(bf16[128,384]{1,0:T(8,128)(2,1)S(1)} %maximum_select_fusion.refs_2_.refs_0_), channel_id=1, source_target_pairs={{0,64},{32,96},{64,0},{96,32},{1,65},{33,97},{65,1},{97,33},{2,66}... | collective-permute-start | bytes 294920 | tf_op jit(solution)/shard_map/ppermute | solution.py:39
  14.7 12.8 %collective-permute-start.6 = (bf16[1,512,384]{2,1,0:T(8,128)(2,1)S(1)}, bf16[1,512,384]{2,1,0:T(8,128)(2,1)S(1)}, u32[]{:S(2)}, u32[]{:S(2)}) collective-permute-start(bf16[1,512,384]{2,1,0:T(8,128)(2,1)S(1)} %gather.3.refs_1_.refs_0_), channel_id=1, source_target_pairs={{0,6},{1,25},{2,0},{3,27},{4,2},{5,29},{6,4},{7,31},{8,14},{9,1},{... | collective-permute-start | bytes 1179656 | tf_op jit(solution)/shard_map/ppermute | solution.py:31
  18.5 12.3 %collective-permute-start.5 = (bf16[1,512,384]{2,1,0:T(8,128)(2,1)S(1)}, bf16[1,512,384]{2,1,0:T(8,128)(2,1)S(1)}, u32[]{:S(2)}, u32[]{:S(2)}) collective-permute-start(bf16[1,512,384]{2,1,0:T(8,128)(2,1)S(1)} %gather.3.refs_1_.refs_0_), channel_id=1, source_target_pairs={{0,2},{1,9},{2,4},{3,11},{4,6},{5,13},{6,0},{7,15},{8,10},{9,17},{... | collective-permute-start | bytes 1179656 | tf_op jit(solution)/shard_map/ppermute | solution.py:31
  18.5 12.3 %collective-permute-start.4 = (bf16[1,512,384]{2,1,0:T(8,128)(2,1)S(1)}, bf16[1,512,384]{2,1,0:T(8,128)(2,1)S(1)}, u32[]{:S(2)}, u32[]{:S(2)}) collective-permute-start(bf16[1,512,384]{2,1,0:T(8,128)(2,1)S(1)} %gather.3.refs_1_.refs_0_), channel_id=1, source_target_pairs={{0,4},{1,17},{2,6},{3,19},{4,0},{5,21},{6,2},{7,23},{8,12},{9,25},... | collective-permute-start | bytes 1179656 | tf_op jit(solution)/shard_map/ppermute | solution.py:31
  31.0 4.2 %collective-permute-start.8 = (bf16[4,512,384]{2,1,0:T(8,128)(2,1)S(1)}, bf16[4,512,384]{2,1,0:T(8,128)(2,1)S(1)}, u32[]{:S(2)}, u32[]{:S(2)}) collective-permute-start(bf16[4,512,384]{2,1,0:T(8,128)(2,1)S(1)} %gather.4.refs_0_), channel_id=1, source_target_pairs={{0,1},{1,0},{2,3},{3,2},{4,5},{5,4},{6,7},{7,6},{8,9},{9,8},{10,11... | collective-permute-start | bytes 4718600 | tf_op jit(solution)/shard_map/ppermute | solution.py:35
  31.8 19.6 %collective-permute-start.9 = (bf16[4,512,384]{2,1,0:T(8,128)(2,1)S(1)}, bf16[4,512,384]{2,1,0:T(8,128)(2,1)S(1)}, u32[]{:S(2)}, u32[]{:S(2)}) collective-permute-start(bf16[4,512,384]{2,1,0:T(8,128)(2,1)S(1)} %gather.4.refs_0_), channel_id=1, source_target_pairs={{0,24},{1,7},{2,26},{3,1},{4,28},{5,3},{6,30},{7,5},{8,0},{9,15},{... | collective-permute-start | bytes 4718600 | tf_op jit(solution)/shard_map/ppermute | solution.py:27
  33.3 20.8 %collective-permute-start.7 = (bf16[4,512,384]{2,1,0:T(8,128)(2,1)S(1)}, bf16[4,512,384]{2,1,0:T(8,128)(2,1)S(1)}, u32[]{:S(2)}, u32[]{:S(2)}) collective-permute-start(bf16[4,512,384]{2,1,0:T(8,128)(2,1)S(1)} %gather.4.refs_0_), channel_id=1, source_target_pairs={{0,8},{1,3},{2,10},{3,5},{4,12},{5,7},{6,14},{7,1},{8,16},{9,11},{... | collective-permute-start | bytes 4718600 | tf_op jit(solution)/shard_map/ppermute | solution.py:27
  54.2 8.6 %collective-permute-start.11 = (bf16[4,512,384]{2,1,0:T(8,128)(2,1)S(1)}, bf16[4,512,384]{2,1,0:T(8,128)(2,1)S(1)}, u32[]{:S(2)}, u32[]{:S(2)}) collective-permute-start(bf16[4,512,384]{2,1,0:T(8,128)(2,1)S(1)} %collective-permute-done.7.refs_0_), channel_id=1, source_target_pairs={{0,1},{1,0},{2,3},{3,2},{4,5},{5,4},{6,7},{7,6},{8,9},{9,8},{10,11... | collective-permute-start | bytes 4718600 | tf_op jit(solution)/shard_map/ppermute | solution.py:35
  57.8 5.3 %collective-permute-start.12 = (bf16[4,512,384]{2,1,0:T(8,128)(2,1)S(1)}, bf16[4,512,384]{2,1,0:T(8,128)(2,1)S(1)}, u32[]{:S(2)}, u32[]{:S(2)}) collective-permute-start(bf16[4,512,384]{2,1,0:T(8,128)(2,1)S(1)} %collective-permute-done.9.refs_1_), channel_id=1, source_target_pairs={{0,1},{1,0},{2,3},{3,2},{4,5},{5,4},{6,7},{7,6},{8,9},{9,8},{10,11... | collective-permute-start | bytes 4718600 | tf_op jit(solution)/shard_map/ppermute | solution.py:35
  57.9 11.1 %collective-permute-start.14 = (bf16[2,512,384]{2,1,0:T(8,128)(2,1)S(1)}, bf16[2,512,384]{2,1,0:T(8,128)(2,1)S(1)}, u32[]{:S(2)}, u32[]{:S(2)}) collective-permute-start(bf16[2,512,384]{2,1,0:T(8,128)(2,1)S(1)} %get-tuple-element.56.refs_7_), channel_id=1, source_target_pairs={{0,24},{1,7},{2,26},{3,1},{4,28},{5,3},{6,30},{7,5},{8,0},{9,15},{... | collective-permute-start | bytes 2359304 | tf_op jit(solution)/shard_map/ppermute | solution.py:27
  57.9 12.3 %collective-permute-start.10 = (bf16[2,512,384]{2,1,0:T(8,128)(2,1)S(1)}, bf16[2,512,384]{2,1,0:T(8,128)(2,1)S(1)}, u32[]{:S(2)}, u32[]{:S(2)}) collective-permute-start(bf16[2,512,384]{2,1,0:T(8,128)(2,1)S(1)} %get-tuple-element.55.refs_6_), channel_id=1, source_target_pairs={{0,8},{1,3},{2,10},{3,5},{4,12},{5,7},{6,14},{7,1},{8,16},{9,11},{... | collective-permute-start | bytes 2359304 | tf_op jit(solution)/shard_map/ppermute | solution.py:27
  70.2 5.3 %collective-permute-start.13 = (bf16[2,512,384]{2,1,0:T(8,128)(2,1)S(1)}, bf16[2,512,384]{2,1,0:T(8,128)(2,1)S(1)}, u32[]{:S(2)}, u32[]{:S(2)}) collective-permute-start(bf16[2,512,384]{2,1,0:T(8,128)(2,1)S(1)} %collective-permute-done.10.refs_0_), channel_id=1, source_target_pairs={{0,1},{1,0},{2,3},{3,2},{4,5},{5,4},{6,7},{7,6},{8,9},{9,8},{10,11... | collective-permute-start | bytes 2359304 | tf_op jit(solution)/shard_map/ppermute | solution.py:35
  71.5 4.1 %collective-permute-start.15 = (bf16[2,512,384]{2,1,0:T(8,128)(2,1)S(1)}, bf16[2,512,384]{2,1,0:T(8,128)(2,1)S(1)}, u32[]{:S(2)}, u32[]{:S(2)}) collective-permute-start(bf16[2,512,384]{2,1,0:T(8,128)(2,1)S(1)} %collective-permute-done.14.refs_1_), channel_id=1, source_target_pairs={{0,1},{1,0},{2,3},{3,2},{4,5},{5,4},{6,7},{7,6},{8,9},{9,8},{10,11... | collective-permute-start | bytes 2359304 | tf_op jit(solution)/shard_map/ppermute | solution.py:35
  75.0 5.2 %collective-permute-start.16 = (bf16[4,512,384]{2,1,0:T(8,128)(2,1)S(1)}, bf16[4,512,384]{2,1,0:T(8,128)(2,1)S(1)}, u32[]{:S(2)}, u32[]{:S(2)}) collective-permute-start(bf16[4,512,384]{2,1,0:T(8,128)(2,1)S(1)} %down.10.refs_6_), channel_id=1, source_target_pairs={{0,1},{1,0},{2,3},{3,2},{4,5},{5,4},{6,7},{7,6},{8,9},{9,8},{10,11... | collective-permute-start | bytes 4718600 | tf_op jit(solution)/shard_map/ppermute | solution.py:35
  78.5 7.2 %collective-permute-start.18 = (bf16[4,512,384]{2,1,0:T(8,128)(2,1)S(1)}, bf16[4,512,384]{2,1,0:T(8,128)(2,1)S(1)}, u32[]{:S(2)}, u32[]{:S(2)}) collective-permute-start(bf16[4,512,384]{2,1,0:T(8,128)(2,1)S(1)} %down.11.rest_0_.rest_1_), channel_id=1, source_target_pairs={{0,1},{1,0},{2,3},{3,2},{4,5},{5,4},{6,7},{7,6},{8,9},{9,8},{10,11... | collective-permute-start | bytes 4718600 | tf_op jit(solution)/shard_map/ppermute | solution.py:35
  79.6 15.0 %collective-permute-start.20 = (bf16[4,512,384]{2,1,0:T(8,128)(2,1)S(1)}, bf16[4,512,384]{2,1,0:T(8,128)(2,1)S(1)}, u32[]{:S(2)}, u32[]{:S(2)}) collective-permute-start(bf16[4,512,384]{2,1,0:T(8,128)(2,1)S(1)} %down.12.rest_1_.rest_2_), channel_id=1, source_target_pairs={{0,1},{1,0},{2,3},{3,2},{4,5},{5,4},{6,7},{7,6},{8,9},{9,8},{10,11... | collective-permute-start | bytes 4718600 | tf_op jit(solution)/shard_map/ppermute | solution.py:35
  81.2 12.4 %collective-permute-start.19 = (bf16[2,512,384]{2,1,0:T(8,128)(2,1)S(1)}, bf16[2,512,384]{2,1,0:T(8,128)(2,1)S(1)}, u32[]{:S(2)}, u32[]{:S(2)}) collective-permute-start(bf16[2,512,384]{2,1,0:T(8,128)(2,1)S(1)} %get-tuple-element.75), channel_id=1, source_target_pairs={{0,8},{1,3},{2,10},{3,5},{4,12},{5,7},{6,14},{7,1},{8,16},{9,11},{... | collective-permute-start | bytes 2359304 | tf_op jit(solution)/shard_map/ppermute | solution.py:27
  81.3 13.3 %collective-permute-start.21 = (bf16[2,512,384]{2,1,0:T(8,128)(2,1)S(1)}, bf16[2,512,384]{2,1,0:T(8,128)(2,1)S(1)}, u32[]{:S(2)}, u32[]{:S(2)}) collective-permute-start(bf16[2,512,384]{2,1,0:T(8,128)(2,1)S(1)} %get-tuple-element.77), channel_id=1, source_target_pairs={{0,24},{1,7},{2,26},{3,1},{4,28},{5,3},{6,30},{7,5},{8,0},{9,15},{... | collective-permute-start | bytes 2359304 | tf_op jit(solution)/shard_map/ppermute | solution.py:27
  85.0 14.5 %collective-permute-start.17 = (bf16[4,512,384]{2,1,0:T(8,128)(2,1)S(1)}, bf16[4,512,384]{2,1,0:T(8,128)(2,1)S(1)}, u32[]{:S(2)}, u32[]{:S(2)}) collective-permute-start(bf16[4,512,384]{2,1,0:T(8,128)(2,1)S(1)} %down.13), channel_id=1, source_target_pairs={{0,1},{1,0},{2,3},{3,2},{4,5},{5,4},{6,7},{7,6},{8,9},{9,8},{10,11... | collective-permute-start | bytes 4718600 | tf_op jit(solution)/shard_map/ppermute | solution.py:35
  94.5 16.6 %collective-permute-start.22 = (bf16[3,512,384]{2,1,0:T(8,128)(2,1)S(1)}, bf16[3,512,384]{2,1,0:T(8,128)(2,1)S(1)}, u32[]{:S(2)}, u32[]{:S(2)}) collective-permute-start(bf16[3,512,384]{2,1,0:T(8,128)(2,1)S(1)} %down.15.rest_1_.rest_2_), channel_id=1, source_target_pairs={{0,8},{1,3},{2,10},{3,5},{4,12},{5,7},{6,14},{7,1},{8,16},{9,11},{... | collective-permute-start | bytes 3538952 | tf_op jit(solution)/shard_map/ppermute | solution.py:27
  95.7 18.2 %collective-permute-start.25 = (bf16[3,512,384]{2,1,0:T(8,128)(2,1)S(1)}, bf16[3,512,384]{2,1,0:T(8,128)(2,1)S(1)}, u32[]{:S(2)}, u32[]{:S(2)}) collective-permute-start(bf16[3,512,384]{2,1,0:T(8,128)(2,1)S(1)} %down.16.rest_2_.rest_3_), channel_id=1, source_target_pairs={{0,24},{1,7},{2,26},{3,1},{4,28},{5,3},{6,30},{7,5},{8,0},{9,15},{... | collective-permute-start | bytes 3538952 | tf_op jit(solution)/shard_map/ppermute | solution.py:27
  111.2 8.1 %collective-permute-start.23 = (bf16[1,512,384]{2,1,0:T(8,128)(2,1)S(1)}, bf16[1,512,384]{2,1,0:T(8,128)(2,1)S(1)}, u32[]{:S(2)}, u32[]{:S(2)}) collective-permute-start(bf16[1,512,384]{2,1,0:T(8,128)(2,1)S(1)} %down.18), channel_id=1, source_target_pairs={{0,8},{1,3},{2,10},{3,5},{4,12},{5,7},{6,14},{7,1},{8,16},{9,11},{... | collective-permute-start | bytes 1179656 | tf_op jit(solution)/shard_map/ppermute | solution.py:27
  111.2 12.4 %collective-permute-start.24 = (bf16[1,512,384]{2,1,0:T(8,128)(2,1)S(1)}, bf16[1,512,384]{2,1,0:T(8,128)(2,1)S(1)}, u32[]{:S(2)}, u32[]{:S(2)}) collective-permute-start(bf16[1,512,384]{2,1,0:T(8,128)(2,1)S(1)} %down.19), channel_id=1, source_target_pairs={{0,24},{1,7},{2,26},{3,1},{4,28},{5,3},{6,30},{7,5},{8,0},{9,15},{... | collective-permute-start | bytes 1179656 | tf_op jit(solution)/shard_map/ppermute | solution.py:27
  114.2 9.4 %collective-permute-start.26 = (bf16[512,384]{1,0:T(8,128)(2,1)S(1)}, bf16[512,384]{1,0:T(8,128)(2,1)S(1)}, u32[]{:S(2)}, u32[]{:S(2)}) collective-permute-start(bf16[512,384]{1,0:T(8,128)(2,1)S(1)} %get-tuple-element.82), channel_id=1, source_target_pairs={{0,4},{1,17},{2,6},{3,19},{4,0},{5,21},{6,2},{7,23},{8,12},{9,25},... | collective-permute-start | bytes 1179656 | tf_op jit(solution)/shard_map/ppermute | solution.py:31
  114.3 15.4 %collective-permute-start.27 = (bf16[512,384]{1,0:T(8,128)(2,1)S(1)}, bf16[512,384]{1,0:T(8,128)(2,1)S(1)}, u32[]{:S(2)}, u32[]{:S(2)}) collective-permute-start(bf16[512,384]{1,0:T(8,128)(2,1)S(1)} %get-tuple-element.83), channel_id=1, source_target_pairs={{0,2},{1,9},{2,4},{3,11},{4,6},{5,13},{6,0},{7,15},{8,10},{9,17},{... | collective-permute-start | bytes 1179656 | tf_op jit(solution)/shard_map/ppermute | solution.py:31
  114.6 15.1 %collective-permute-start.28 = (bf16[512,384]{1,0:T(8,128)(2,1)S(1)}, bf16[512,384]{1,0:T(8,128)(2,1)S(1)}, u32[]{:S(2)}, u32[]{:S(2)}) collective-permute-start(bf16[512,384]{1,0:T(8,128)(2,1)S(1)} %get-tuple-element.84), channel_id=1, source_target_pairs={{0,6},{1,25},{2,0},{3,27},{4,2},{5,29},{6,4},{7,31},{8,14},{9,1},{... | collective-permute-start | bytes 1179656 | tf_op jit(solution)/shard_map/ppermute | solution.py:31
  130.0 5.6 %collective-permute-start.29 = (bf16[128,384]{1,0:T(8,128)(2,1)S(1)}, bf16[128,384]{1,0:T(8,128)(2,1)S(1)}, u32[]{:S(2)}, u32[]{:S(2)}) collective-permute-start(bf16[128,384]{1,0:T(8,128)(2,1)S(1)} %get-tuple-element.87), channel_id=1, source_target_pairs={{0,64},{32,96},{64,0},{96,32},{1,65},{33,97},{65,1},{97,33},{2,66}... | collective-permute-start | bytes 294920 | tf_op jit(solution)/shard_map/ppermute | solution.py:39
  130.4 8.0 %collective-permute-start.31 = (bf16[128,384]{1,0:T(8,128)(2,1)S(1)}, bf16[128,384]{1,0:T(8,128)(2,1)S(1)}, u32[]{:S(2)}, u32[]{:S(2)}) collective-permute-start(bf16[128,384]{1,0:T(8,128)(2,1)S(1)} %get-tuple-element.88), channel_id=1, source_target_pairs={{0,32},{32,64},{64,96},{96,0},{1,33},{33,65},{65,97},{97,1},{2,34}... | collective-permute-start | bytes 294920 | tf_op jit(solution)/shard_map/ppermute | solution.py:39
  131.5 6.9 %collective-permute-start.30 = (bf16[128,384]{1,0:T(8,128)(2,1)S(1)}, bf16[128,384]{1,0:T(8,128)(2,1)S(1)}, u32[]{:S(2)}, u32[]{:S(2)}) collective-permute-start(bf16[128,384]{1,0:T(8,128)(2,1)S(1)} %get-tuple-element.89), channel_id=1, source_target_pairs={{0,96},{32,0},{64,32},{96,64},{1,97},{33,1},{65,33},{97,65},{2,98}... | collective-permute-start | bytes 294920 | tf_op jit(solution)/shard_map/ppermute | solution.py:39
  138.7 1.5 %collective-permute-start.32 = (bf16[128,192]{1,0:T(8,128)(2,1)S(1)}, bf16[128,192]{1,0:T(8,128)(2,1)S(1)}, u32[]{:S(2)}, u32[]{:S(2)}) collective-permute-start(bf16[128,192]{1,0:T(8,128)(2,1)S(1)} %broadcast_select_fusion.1), channel_id=1, source_target_pairs={{0,1},{1,0},{2,3},{3,2},{4,5},{5,4},{6,7},{7,6},{8,9},{9,8},{10,11... | collective-permute-start | bytes 147464 | tf_op jit(solution)/shard_map/ppermute | solution.py:35
